TPU v7x, 128 devices: a whole 4x4x4 slice. The times are simulated.
128 devices in a mesh: side: 2 (over core), grp: 64 (over y, z, x).
Axes of the slice: x: 4, y: 4, z: 4, core: 2. Of those that a mesh axis runs over, the one named last changes fastest.
Arguments:
- query_heads: bfloat16 [1024, 8192], P('grp'), may hold values from -160 to 160
- key_cache: bfloat16 [1024, 128, 512], P('grp'), may hold values from -4 to 4
- value_cache: bfloat16 [1024, 128, 512], P('grp'), may hold values from -6 to 6
- cache_lengths: int32 [1024], P('grp'), may hold values from 2 to 128, as said below
- out_weight: bfloat16 [8192, 4096], P(None, 'grp'), may hold values from -0.0625 to 0.0625
- residual: bfloat16 [1024, 4096], P('grp'), may hold values from -4 to 4
- norm_gain: float32 [4096], replicated, may hold values from 0.5 to 1.5
- expert_ids: int32 [1024, 8], P('grp'), may hold values from 0 to 63, all different within a row; in each aligned block of 16 rows (0 to 15, 16 to 31, ...) at most 4 rows name the same one
- route_weights: float32 [1024, 8], P('grp'), may hold values from 0.05 to 0.25
- gate_up: bfloat16 [64, 4096, 1536], P('grp'), may hold values from -0.09375 to 0.09375
- down_weight: bfloat16 [64, 768, 4096], P('grp'), may hold values from -0.21875 to 0.21875
Outputs:
- layer_out: bfloat16 [1024, 4096], P('grp', 'side')
Inputs may be any that keep to these rules, and one draw needn't show every extreme that they name: `cache_lengths`: at least one session has 128 live positions. `expert_ids`: each row names 8 different experts; among the 16 sessions of one index of grp (aligned blocks of rows) no expert is named by more than 4 rows, a bound that some block reaches.
All inputs are finite; a program needn't handle non-finite values.
Results may differ from a plain program's by a relative error of at most 0.0055.
Values may be sent and summed in bfloat16 or wider, within the bound.
A program may use at most 128 MiB of HBM per device.

v0:
```python
import jax
import jax.numpy as jnp
from jax import lax
from jax.sharding import PartitionSpec as P

HQ = 64
KVH = 4
HD = 128
HID = 768
TOPK = 8
CTX = 128


def from_behind(value, axis, steps):
    count = lax.axis_size(axis)
    leading, last = (max(0, -steps), min(count, count - steps))
    return lax.ppermute(value, axis, [(source, source + steps) for source in range(leading, last)])


def partner(block, axis, apart):
    count = lax.axis_size(axis)
    route = []
    for low in range(count):
        high = low | 1 << apart
        if high != low and high < count:
            route += [(low, high), (high, low)]
    return lax.ppermute(block, axis, route)


def slots_of(expert_block, groups):
    flat_ids = expert_block.reshape(-1)
    onehot = (flat_ids[:, None] == jnp.arange(groups, dtype=jnp.int32)[None, :]).astype(jnp.int32)
    running = jnp.cumsum(onehot, axis=0)
    return jnp.sum(onehot * running, axis=1) - 1


def attend(query_heads, key_cache, value_cache, cache_lengths):
    session_count = query_heads.shape[0]
    group_size = HQ // KVH
    queries = query_heads.reshape(session_count, KVH, group_size, HD)
    key_heads = key_cache.reshape(session_count, CTX, KVH, HD)
    value_heads = value_cache.reshape(session_count, CTX, KVH, HD)
    scores = jnp.einsum(
        "skgd,stkd->skgt", queries, key_heads, preferred_element_type=jnp.float32
    ) * HD ** (-0.5)
    visible = jnp.arange(CTX, dtype=jnp.int32)[None, :] < cache_lengths[:, None]
    scores = jnp.where(visible[:, None, None, :], scores, -1e30)
    row_max = jnp.max(scores, axis=-1, keepdims=True)
    lifted = jnp.exp(scores - row_max)
    softmax_weights = (lifted / jnp.sum(lifted, axis=-1, keepdims=True)).astype(jnp.bfloat16)
    attended = jnp.einsum(
        "skgt,stkd->skgd", softmax_weights, value_heads, preferred_element_type=jnp.float32
    )
    return attended.astype(jnp.bfloat16).reshape(session_count, HQ * HD)


def expert_rows(token_rows, expert_gate_up, expert_down):
    both_halves = jnp.dot(token_rows, expert_gate_up, preferred_element_type=jnp.float32)
    activated = (jax.nn.silu(both_halves[:, :HID]) * both_halves[:, HID:]).astype(jnp.bfloat16)
    return jnp.dot(activated, expert_down, preferred_element_type=jnp.float32).astype(jnp.bfloat16)


def body(
    query_heads,
    key_cache,
    value_cache,
    cache_lengths,
    out_weight,
    residual,
    norm_gain,
    expert_ids,
    route_weights,
    gate_up,
    down_weight,
):
    side_index = lax.axis_index("side")
    on_attention = side_index == 0
    groups = lax.axis_size("grp")
    session_count = query_heads.shape[0]
    model_width = residual.shape[1]
    capacity = max(2, 2 * session_count * TOPK // groups)
    total_slots = groups * capacity
    attn_out = lax.cond(
        on_attention,
        attend,
        lambda *operands: jnp.zeros((session_count, HQ * HD), jnp.bfloat16),
        query_heads,
        key_cache,
        value_cache,
        cache_lengths,
    )
    columns = jnp.dot(
        lax.all_gather(attn_out, "grp", axis=0, tiled=True),
        out_weight,
        preferred_element_type=jnp.float32,
    )
    attn_proj = lax.all_to_all(columns, "grp", split_axis=0, concat_axis=1, tiled=True)
    hidden = residual.astype(jnp.float32) + attn_proj
    scaling = lax.rsqrt(jnp.mean(hidden * hidden, axis=-1, keepdims=True) + 1e-06)
    normed = (hidden * scaling * norm_gain).astype(jnp.bfloat16)
    slot_index = slots_of(expert_ids, groups)
    position = expert_ids.reshape(-1) * capacity + slot_index
    placing = jnp.arange(total_slots, dtype=jnp.int32)[:, None] == position[None, :]
    dispatch = jnp.sum(
        placing.reshape(total_slots, session_count, TOPK).astype(jnp.bfloat16), axis=2
    )
    outgoing_rows = jnp.dot(dispatch, normed, preferred_element_type=jnp.float32).astype(
        jnp.bfloat16
    )
    outgoing_rows = outgoing_rows.reshape(groups, capacity, model_width)
    expert_gate_up = gate_up[0]
    expert_down = down_weight[0]

    def compute(token_slots):
        flat_rows = token_slots.reshape(-1, model_width)
        return expert_rows(flat_rows, expert_gate_up, expert_down).reshape(token_slots.shape)

    crossed = from_behind(outgoing_rows, "side", 1)
    results = lax.cond(
        on_attention,
        lambda operands: jnp.zeros_like(operands),
        compute,
        lax.all_to_all(crossed, "grp", split_axis=0, concat_axis=0, tiled=True),
    )
    returned = lax.all_to_all(results, "grp", split_axis=0, concat_axis=0, tiled=True)
    weighting = (position[:, None] == jnp.arange(total_slots, dtype=jnp.int32)[None, :]).astype(
        jnp.float32
    )
    weighting = weighting * route_weights.reshape(-1)[:, None]
    weighting = jnp.sum(weighting.reshape(session_count, TOPK, total_slots), axis=1)
    mixture = jnp.dot(
        weighting,
        returned.reshape(total_slots, model_width).astype(jnp.float32),
        precision=lax.Precision.HIGHEST,
    )
    half_width = model_width // 2
    outgoing = jnp.where(on_attention, hidden[:, half_width:], mixture[:, :half_width])
    incoming = partner(outgoing, "side", 0)
    combined = jnp.where(
        on_attention, hidden[:, :half_width] + incoming, incoming + mixture[:, half_width:]
    )
    return combined.astype(jnp.bfloat16)


def solution(mesh):
    return jax.shard_map(
        body,
        mesh=mesh,
        in_specs=(
            P("grp", None),
            P("grp", None, None),
            P("grp", None, None),
            P("grp"),
            P(None, "grp"),
            P("grp", None),
            P(),
            P("grp", None),
            P("grp", None),
            P("grp", None, None),
            P("grp", None, None),
        ),
        out_specs=P("grp", "side"),
        check_vma=False,
    )
```

profile of v0, /device:TPU:0, one launch (start us, length us, event | category | flops | bytes accessed | tf_op | source)
XLA Modules:
  0.0 251.1 jit_solution(2321294567143406813)
XLA Ops:
  6.5 0.0 copy-start
  6.5 0.0 all-gather.2.cloned.1.call-start
  6.5 0.0 copy-start.5
  6.5 8.6 %conditional.2 = (bf16[16,8192]{1,0:T(8,128)(2,1)S(1)}) conditional(s32[]{:T(128)} %convert_element_type.39, () %tuple.17, (s32[16]{0:T(128)}, bf16[16,8192]{1,0:T(8,128)(2,1)}, bf16[16,128,512]{2,1,0:T(8,128)(2,1)}, bf16[16,128,512]{2,1,0:T(8,128)(2,1)}) %tuple.18), branch_computations={%region_0.0_spmd, %region_1.4_spmd} | conditional | flops 68160768 | bytes 7352392 | solution.py:83
  6.5 1.1 copy.41
  7.6 0.7 iota_compare_fusion
  8.4 2.8 %fusion.12 = f32[16,4,16,128]{3,2,1,0:T(8,128)S(1)} fusion(bf16[16,4,16,128]{3,2,1,0:T(8,128)(2,1)S(1)} %bitcast.48, pred[16,128]{1,0:T(8,128)(4,1)S(1)} %iota_compare_fusion, bf16[16,128,512]{2,1,0:T(8,128)(2,1)} %get-tuple-element.40), kind=kOutput, calls=%fused_computation.10 | convolution fusion | flops 33816576 | bytes 2885632 | tf_op jit(solution)/shard_map/cond/branch_1_fun/skgd,stkd->skgt/dot_general | solution.py:43
  11.1 0.4 fusion.38
  11.5 3.4 %fusion.15 = bf16[16,4,16,128]{3,2,1,0:T(8,128)(2,1)S(1)} fusion(f32[16,4,16]{2,1,0:T(4,128)S(1)} %fusion.38, f32[16,4,16,128]{3,2,1,0:T(8,128)S(1)} %fusion.12, bf16[16,128,512]{2,1,0:T(8,128)(2,1)} %get-tuple-element.41), kind=kOutput, calls=%fused_computation.11 | convolution fusion | flops 34079872 | bytes 2887680 | tf_op jit(solution)/shard_map/cond/branch_1_fun/skgt,stkd->skgd/dot_general | solution.py:51
  15.0 0.2 copy.58
  15.2 0.0 copy-start.2
  15.2 0.7 copy-done.2
  15.9 0.0 all-gather.2.cloned.1.call-update
  15.9 0.0 copy-done.5
  15.9 0.1 copy.35
  16.0 0.1 eq.47
  16.1 0.1 fusion.37
  16.2 0.2 reduce_window_sum.11
  16.3 0.2 select_reduce_fusion.1
  16.5 0.1 sub.15
  16.6 105.9 %all-gather.2.cloned.1.call-done = bf16[1024,8192]{1,0:T(8,128)(2,1)} async-done(((bf16[16,8192]{1,0:T(8,128)(2,1)}), bf16[1024,8192]{1,0:T(8,128)(2,1)}) %all-gather.2.cloned.1.call-update) | async-done | bytes 16777232 | tf_op jit(solution)/shard_map/all_gather | solution.py:93
  122.5 0.0 copy-done
  122.5 8.1 %fusion.39 = f32[1024,64]{1,0:T(8,128)S(1)} fusion(bf16[1024,8192]{1,0:T(8,128)(2,1)} %all-gather.2.cloned.1.call-done, bf16[8192,64]{0,1:T(8,128)(2,1)S(1)} %copy-done), kind=kOutput, calls=%fused_computation.49 | convolution fusion | flops 1073741824 | bytes 18087936 | tf_op jit(solution)/shard_map/dot_general | solution.py:92
  130.6 0.0 copy-start.3
  130.6 1.0 reshape.103
  131.6 0.0 copy-start.4
  131.6 8.7 %all-to-all-start = ((f32[64,1,1024]{2,1,0:T(1,128)}), f32[64,1,1024]{2,1,0:T(1,128)S(1)}, u32[]{:S(2)}, u32[]{:S(2)}) async-start(f32[64,1,1024]{2,1,0:T(1,128)} %reshape.103), calls=%async_computation | async-start | bytes 524288 | tf_op jit(solution)/shard_map/all_to_all | solution.py:97
  140.4 0.1 fusion.36
  140.5 10.5 %all-to-all-done = f32[64,1,1024]{2,1,0:T(1,128)S(1)} async-done(((f32[64,1,1024]{2,1,0:T(1,128)}), f32[64,1,1024]{2,1,0:T(1,128)S(1)}, u32[]{:S(2)}, u32[]{:S(2)}) %all-to-all-start) | async-done | bytes 262176 | tf_op jit(solution)/shard_map/all_to_all | solution.py:97
  151.0 0.6 broadcast.92
  151.6 1.3 reduce.1
  152.9 0.1 reshape.104
  153.0 0.2 copy.34
  153.2 0.2 all_to_all.23
  153.4 0.0 copy-done.3
  153.4 0.2 multiply_reduce_fusion
  153.6 0.0 copy-done.4
  153.6 0.8 convolution_convert_fusion
  154.3 2.2 reshape.101
  156.6 2.6 %collective-permute-start = (bf16[64,4,4096]{2,1,0:T(4,128)(2,1)}, bf16[64,4,4096]{2,1,0:T(4,128)(2,1)}, u32[]{:S(2)}, u32[]{:S(2)}) collective-permute-start(bf16[64,4,4096]{2,1,0:T(4,128)(2,1)} %reshape.101), channel_id=1, source_target_pairs={{0,64},{1,65},{2,66},{3,67},{4,68},{5,69},{6,70},{7,71},{8,72},{9,... | collective-permute-start | bytes 6291464 | tf_op jit(solution)/shard_map/ppermute | solution.py:17
  159.1 2.8 %collective-permute-done = bf16[64,4,4096]{2,1,0:T(4,128)(2,1)} collective-permute-done((bf16[64,4,4096]{2,1,0:T(4,128)(2,1)}, bf16[64,4,4096]{2,1,0:T(4,128)(2,1)}, u32[]{:S(2)}, u32[]{:S(2)}) %collective-permute-start) | collective-permute-done | bytes 2097184 | tf_op jit(solution)/shard_map/ppermute | solution.py:17
  162.0 4.9 %all-to-all-start.1 = ((bf16[64,4,4096]{2,1,0:T(4,128)(2,1)}), bf16[64,4,4096]{2,1,0:T(4,128)(2,1)S(1)}, u32[]{:S(2)}, u32[]{:S(2)}) async-start(bf16[64,4,4096]{2,1,0:T(4,128)(2,1)} %collective-permute-done), calls=%async_computation.1 | async-start | bytes 4194304 | tf_op jit(solution)/shard_map/all_to_all | solution.py:123
  166.8 31.5 %all-to-all-done.1 = bf16[64,4,4096]{2,1,0:T(4,128)(2,1)S(1)} async-done(((bf16[64,4,4096]{2,1,0:T(4,128)(2,1)}), bf16[64,4,4096]{2,1,0:T(4,128)(2,1)S(1)}, u32[]{:S(2)}, u32[]{:S(2)}) %all-to-all-start.1) | async-done | bytes 2097184 | tf_op jit(solution)/shard_map/all_to_all | solution.py:123
  198.3 1.0 conditional.3
  198.3 1.0 broadcast.75
  199.3 0.0 copy-start.1
  199.3 1.3 copy-done.1
  200.7 0.0 copy-start.6
  200.7 4.8 %all-to-all-start.2 = ((bf16[64,4,4096]{2,1,0:T(4,128)(2,1)}), bf16[64,4,4096]{2,1,0:T(4,128)(2,1)S(1)}, u32[]{:S(2)}, u32[]{:S(2)}) async-start(bf16[64,4,4096]{2,1,0:T(4,128)(2,1)} %copy-done.1), calls=%async_computation.2 | async-start | bytes 4194304 | tf_op jit(solution)/shard_map/all_to_all | solution.py:125
  205.5 0.0 copy-done.6
  205.5 0.1 copy.37
  205.6 0.1 select_reduce_fusion
  205.7 21.1 %all-to-all-done.2 = bf16[64,4,4096]{2,1,0:T(4,128)(2,1)S(1)} async-done(((bf16[64,4,4096]{2,1,0:T(4,128)(2,1)}), bf16[64,4,4096]{2,1,0:T(4,128)(2,1)S(1)}, u32[]{:S(2)}, u32[]{:S(2)}) %all-to-all-start.2) | async-done | bytes 2097184 | tf_op jit(solution)/shard_map/all_to_all | solution.py:125
  226.8 2.1 reshape.102
  228.8 2.5 %fusion.40 = f32[16,4096]{1,0:T(8,128)S(1)} fusion(f32[16,256]{1,0:T(8,128)S(1)} %select_reduce_fusion, bf16[256,4096]{1,0:T(8,128)(2,1)} %reshape.102), kind=kOutput, calls=%fused_computation.50 | convolution fusion | flops 201326592 | bytes 2375680 | tf_op jit(solution)/shard_map/dot_general | solution.py:131
  231.4 11.3 %collective-permute-start.1 = (f32[16,2048]{1,0:T(8,128)S(1)}, f32[16,2048]{1,0:T(8,128)S(1)}, u32[]{:S(2)}, u32[]{:S(2)}) collective-permute-start(f32[16,2048]{1,0:T(8,128)S(1)} %slice_select_fusion), channel_id=1, source_target_pairs={{0,64},{64,0},{1,65},{65,1},{2,66},{66,2},{3,67},{67,3},{4,68},{68... | collective-permute-start | bytes 393224 | tf_op jit(solution)/shard_map/ppermute | solution.py:27
  242.6 1.0 collective-permute-done.1
  243.6 0.7 fusion.32
  (4 shorter events, 0.0 us)
Async XLA Ops:
  6.5 116.0 %copy-start = (bf16[8192,64]{0,1:T(8,128)(2,1)S(1)}, bf16[8192,64]{0,1:T(8,128)(2,1)}, u32[]{:S(2)}) copy-start(bf16[8192,64]{0,1:T(8,128)(2,1)} %param.19) | copy-start | bytes 3145732
  6.5 116.0 %all-gather.2.cloned.1.call-start = ((), (), s32[]{:S(2)}) async-start(), calls=%async_computation.3 | async-start | bytes 17039360 | tf_op jit(solution)/shard_map/all_gather | solution.py:93
  6.5 9.4 %copy-start.5 = (s32[16,8]{0,1:T(8,128)S(1)}, s32[16,8]{0,1:T(8,128)}, u32[]{:S(2)}) copy-start(s32[16,8]{0,1:T(8,128)} %param.22) | copy-start | bytes 1540
  15.2 0.7 copy-start.2
  130.6 22.8 %copy-start.3 = (bf16[16,4096]{1,0:T(8,128)(2,1)S(1)}, bf16[16,4096]{1,0:T(8,128)(2,1)}, u32[]{:S(2)}) copy-start(bf16[16,4096]{1,0:T(8,128)(2,1)} %param.20) | copy-start | bytes 393220
  131.6 21.9 %copy-start.4 = (f32[4096]{0:T(1024)S(1)}, f32[4096]{0:T(1024)}, u32[]{:S(2)}) copy-start(f32[4096]{0:T(1024)} %param.21) | copy-start | bytes 49156
  131.6 19.3 %all-to-all-start = ((f32[64,1,1024]{2,1,0:T(1,128)}), f32[64,1,1024]{2,1,0:T(1,128)S(1)}, u32[]{:S(2)}, u32[]{:S(2)}) async-start(f32[64,1,1024]{2,1,0:T(1,128)} %reshape.103), calls=%async_computation | async-start | bytes 524288 | tf_op jit(solution)/shard_map/all_to_all | solution.py:97
  156.6 5.4 %collective-permute-start = (bf16[64,4,4096]{2,1,0:T(4,128)(2,1)}, bf16[64,4,4096]{2,1,0:T(4,128)(2,1)}, u32[]{:S(2)}, u32[]{:S(2)}) collective-permute-start(bf16[64,4,4096]{2,1,0:T(4,128)(2,1)} %reshape.101), channel_id=1, source_target_pairs={{0,64},{1,65},{2,66},{3,67},{4,68},{5,69},{6,70},{7,71},{8,72},{9,... | collective-permute-start | bytes 6291464 | tf_op jit(solution)/shard_map/ppermute | solution.py:17
  162.0 36.3 %all-to-all-start.1 = ((bf16[64,4,4096]{2,1,0:T(4,128)(2,1)}), bf16[64,4,4096]{2,1,0:T(4,128)(2,1)S(1)}, u32[]{:S(2)}, u32[]{:S(2)}) async-start(bf16[64,4,4096]{2,1,0:T(4,128)(2,1)} %collective-permute-done), calls=%async_computation.1 | async-start | bytes 4194304 | tf_op jit(solution)/shard_map/all_to_all | solution.py:123
  199.3 1.4 copy-start.1
  200.7 4.8 %copy-start.6 = (f32[16,8]{0,1:T(8,128)S(1)}, f32[16,8]{0,1:T(8,128)}, u32[]{:S(2)}) copy-start(f32[16,8]{0,1:T(8,128)} %param.23) | copy-start | bytes 1540
  200.7 26.1 %all-to-all-start.2 = ((bf16[64,4,4096]{2,1,0:T(4,128)(2,1)}), bf16[64,4,4096]{2,1,0:T(4,128)(2,1)S(1)}, u32[]{:S(2)}, u32[]{:S(2)}) async-start(bf16[64,4,4096]{2,1,0:T(4,128)(2,1)} %copy-done.1), calls=%async_computation.2 | async-start | bytes 4194304 | tf_op jit(solution)/shard_map/all_to_all | solution.py:125
  231.4 12.2 %collective-permute-start.1 = (f32[16,2048]{1,0:T(8,128)S(1)}, f32[16,2048]{1,0:T(8,128)S(1)}, u32[]{:S(2)}, u32[]{:S(2)}) collective-permute-start(f32[16,2048]{1,0:T(8,128)S(1)} %slice_select_fusion), channel_id=1, source_target_pairs={{0,64},{64,0},{1,65},{65,1},{2,66},{66,2},{3,67},{67,3},{4,68},{68... | collective-permute-start | bytes 393224 | tf_op jit(solution)/shard_map/ppermute | solution.py:27
Sparse Core Ops, SparseCore 0:
  16.0 106.4 all-gather.1
where the time goes:
time: 253 us; the launch traced here: 251 us
  waiting for transfers between devices  173 us (68%)
  starting transfers between devices  32.3 us (13%)
  matrix products  17.6 us (7%)
  between operations  13.6 us (5%)
  local copies, waits for them, and re-layouts  11 us (4%)
  other arithmetic  3.96 us (2%)
    all_gather x1, waiting for transfers between devices, body(): lax.all_gather(attn_out, 'grp', axis=0, tiled=True)  106 us
    all_to_all x1, waiting for transfers between devices, body(): lax.all_to_all(crossed, 'grp', split_axis=0, concat_axis=0, tiled=True)  31.5 us
    all_to_all x1, waiting for transfers between devices, body(): lax.all_to_all(results, 'grp', split_axis=0, concat_axis=0, tiled=True)  21.1 us
    ppermute x1, starting transfers between devices, partner(): return lax.ppermute(block, axis, route)  11.3 us
    all_to_all x1, waiting for transfers between devices, body(): lax.all_to_all(columns, 'grp', split_axis=0, concat_axis=1, tiled=True)  10.5 us
    all_to_all x1, starting transfers between devices, body(): lax.all_to_all(columns, 'grp', split_axis=0, concat_axis=1, tiled=True)  8.73 us
    dot_general x1, matrix products, body(): jnp.dot(lax.all_gather(attn_out, 'grp', axis=0, tiled=True), out_weight,...  8.09 us
  transfers between devices with their start and end apart: 6, of which 6 were waited for; matrix products, arithmetic and copies ran while one was open for 0% of the time, Pallas kernels for 0%

commit v1 on v0

--- a/solution.py
+++ b/solution.py
@@ -1,6 +1,10 @@
+import functools
+
 import jax
 import jax.numpy as jnp
 from jax import lax
+from jax.experimental import pallas as pl
+from jax.experimental.pallas import tpu as pltpu
 from jax.sharding import PartitionSpec as P
 
 HQ = 64
@@ -9,6 +13,237 @@
 HID = 768
 TOPK = 8
 CTX = 128
+D = 4096
+S = 16
+MESH = pl.DeviceIdType.MESH
+BF = jnp.bfloat16
+F32 = jnp.float32
+NT = (((1,), (1,)), ((), ()))
+
+
+def place():
+    side = lax.axis_index("side")
+    g = lax.axis_index("grp")
+    sa = 16 - 12 * side
+    sb = 4 + 12 * side
+    ca = lax.rem(g // sa, 4)
+    cb = lax.rem(g // sb, 4)
+    cx = lax.rem(g, 4)
+    return side, g, sa, sb, ca, cb, cx
+
+
+def moved(g, c, stride, by):
+    return g + (lax.rem(c + by + 4, 4) - c) * stride
+
+
+class Ring:
+    def __init__(self, side, plus, minus, sends, recvs, own, slot, half):
+        self.side, self.plus, self.minus = side, plus, minus
+        self.sends, self.recvs, self.own, self.slot, self.half = sends, recvs, own, slot, half
+
+    def copy(self, src, dst, i, to):
+        return pltpu.make_async_remote_copy(
+            src_ref=src, dst_ref=dst, send_sem=self.sends.at[i], recv_sem=self.recvs.at[i],
+            device_id=(self.side, to), device_id_type=MESH)
+
+    def start(self):
+        self.c0 = self.copy(self.own, self.slot(0, 1), 0, self.plus)
+        self.c1 = self.copy(self.own, self.slot(0, 3), 1, self.minus)
+        self.c0.start()
+        self.c1.start()
+
+    def forward(self):
+        self.c0.wait_recv()
+        self.c2 = self.copy(self.half(self.slot(1, 1), 0), self.half(self.slot(1, 2), 0), 2, self.plus)
+        self.c2.start()
+        self.c1.wait_recv()
+        self.c3 = self.copy(self.half(self.slot(3, 3), 1), self.half(self.slot(3, 2), 1), 3, self.minus)
+        self.c3.start()
+
+    def finish(self):
+        self.c2.wait_recv()
+        self.c3.wait_recv()
+
+    def drain(self):
+        for c in (self.c0, self.c1, self.c2, self.c3):
+            c.wait_send()
+
+
+def attend(q_buf, k_buf, v_buf, lens_ref, kv, out):
+    lane = lax.broadcasted_iota(jnp.int32, (S, CTX), 1)
+    row = lax.broadcasted_iota(jnp.int32, (S, CTX), 0)
+    live = jnp.zeros((S, CTX), jnp.int32)
+    for s in range(S):
+        live = jnp.where(row == s, lens_ref[s], live)
+    group = HQ // KVH
+    live = jnp.concatenate([live] * group, axis=0)
+    lane = jnp.concatenate([lane] * group, axis=0)
+    row = jnp.concatenate([row] * group, axis=0)
+    queries = jnp.concatenate(
+        [q_buf[:, (kv * group + j) * HD:(kv * group + j + 1) * HD] for j in range(group)], axis=0)
+    scores = jnp.zeros((S * group, CTX), F32)
+    for s in range(S):
+        part = lax.dot_general(queries, k_buf[s, :, kv * HD:(kv + 1) * HD], NT, preferred_element_type=F32)
+        scores = jnp.where(row == s, part, scores)
+    scores = jnp.where(lane < live, scores * HD ** (-0.5), -1e30)
+    lifted = jnp.exp(scores - jnp.max(scores, axis=1, keepdims=True))
+    weights = (lifted / jnp.sum(lifted, axis=1, keepdims=True))
+    spread = jnp.concatenate([jnp.where(row == s, weights, 0.0).astype(BF) for s in range(S)], axis=1)
+    values = v_buf[:, :, kv * HD:(kv + 1) * HD].reshape(S * CTX, HD)
+    result = jnp.dot(spread, values, preferred_element_type=F32).astype(BF)
+    for j in range(group):
+        out[:, j * HD:(j + 1) * HD] = result[j * S:(j + 1) * S, :]
+
+
+def kernel_a(q_ref, k_ref, v_ref, lens_ref, wt_ref, res_ref, gain_ref, hid_ref, nrm_ref,
+             q_buf, k_buf, v_buf, w_buf, g0, g1, o_st, r_buf,
+             loc, ws, wr, s0p, r0p, s0q, r0q, s1p, r1p, s1q, r1q, os, orv):
+    side, g, sa, sb, ca, cb, cx = place()
+    other = 1 - side
+    ap, am = moved(g, ca, sa, 1), moved(g, ca, sa, -1)
+    bp, bm = moved(g, cb, sb, 1), moved(g, cb, sb, -1)
+    xp, xm = moved(g, cx, 1, 1), moved(g, cx, 1, -1)
+    cy, cz = g // 16, lax.rem(g // 4, 4)
+
+    barrier = pltpu.get_barrier_semaphore()
+
+    def hello(to_side, to):
+        pl.semaphore_signal(barrier, inc=1, device_id=(to_side, to), device_id_type=MESH)
+
+    hello(side, ap)
+    hello(side, am)
+    for i in range(4):
+        for j in range(4):
+            if i or j:
+                hello(side, moved(moved(g, cb, sb, i), cx, 1, j))
+            hello(other, moved(moved(g, ca, sa, i), cx, 1, j))
+
+    c_q = pltpu.make_async_copy(q_ref.at[:, pl.ds(pl.multiple_of(side * 4096, 128), 4096)], q_buf, loc.at[0])
+    c_k = pltpu.make_async_copy(k_ref.at[:, :, pl.ds(pl.multiple_of(side * 256, 128), 256)], k_buf, loc.at[1])
+    c_v = pltpu.make_async_copy(v_ref.at[:, :, pl.ds(pl.multiple_of(side * 256, 128), 256)], v_buf, loc.at[2])
+    w_own = wt_ref.at[:, pl.ds(pl.multiple_of(side * 4096, 128), 4096)]
+    c_w = pltpu.make_async_copy(w_own, w_buf.at[ca], loc.at[3])
+    c_q.start()
+    c_k.start()
+    c_v.start()
+    c_w.start()
+    pl.semaphore_wait(barrier, 33)
+
+    def w_slot(source, at):
+        return w_buf.at[lax.rem(ca - source + 4, 4)]
+
+    ring_w = Ring(side, ap, am, ws, wr, w_own, w_slot, lambda ref, h: ref.at[h * 32:(h + 1) * 32])
+    ring_w.start()
+    c_q.wait()
+    c_k.wait()
+    c_v.wait()
+
+    def first(route, plus, minus, sends, recvs):
+        return Ring(side, plus, minus, sends, recvs, route.at[0, 0],
+                    lambda source, at: route.at[0, at], lambda ref, h: ref.at[:, h * 1024:(h + 1) * 1024])
+
+    def second(route, plus, minus, sends, recvs):
+        return Ring(side, plus, minus, sends, recvs, route.at[0],
+                    lambda source, at: route.at[at], lambda ref, h: ref.at[h * 2:(h + 1) * 2])
+
+    ra, rb = first(g0, bp, bm, s0p, r0p), first(g1, xp, xm, s1p, r1p)
+    rc, rd = second(g0, xp, xm, s0q, r0q), second(g1, bp, bm, s1q, r1q)
+    attend(q_buf, k_buf, v_buf, lens_ref, 0, g0.at[0, 0])
+    ra.start()
+    attend(q_buf, k_buf, v_buf, lens_ref, 1, g1.at[0, 0])
+    rb.start()
+    ra.forward()
+    rb.forward()
+    ra.finish()
+    rc.start()
+    rb.finish()
+    rd.start()
+    ring_w.forward()
+    rc.forward()
+    rd.forward()
+    c_w.wait()
+    ring_w.finish()
+    rc.finish()
+    p0 = lax.dot_general(g0[...].reshape(256, 2048), w_buf[:, :, 0:2048].reshape(256, 2048), NT,
+                         preferred_element_type=F32)
+    rd.finish()
+    p1 = lax.dot_general(g1[...].reshape(256, 2048), w_buf[:, :, 2048:4096].reshape(256, 2048), NT,
+                         preferred_element_type=F32)
+    mine = cb * 4 + cx
+    sent = []
+    for bi in range(4):
+        for xi in range(4):
+            n = bi * 4 + xi
+            u, w = (xi * 4 + bi) * S, (bi * 4 + xi) * S
+            block = (p0[u:u + S, :] + p1[w:w + S, :]).astype(BF)
+            o_st[n] = block
+            if n == 0:
+                r_buf[side, mine] = block
+    for bi in range(4):
+        for xi in range(4):
+            n = bi * 4 + xi
+            to = moved(moved(g, cb, sb, -bi), cx, 1, -xi)
+            for e in range(2):
+                if n == 0 and e == 0:
+                    continue
+                copy = pltpu.make_async_remote_copy(
+                    src_ref=o_st.at[n], dst_ref=r_buf.at[side, mine],
+                    send_sem=os.at[n, e], recv_sem=orv.at[side, mine],
+                    device_id=(side if e == 0 else other, to), device_id_type=MESH)
+                copy.start()
+                sent.append(copy)
+    for i in range(4):
+        for j in range(4):
+            if i or j:
+                n = lax.rem(cb + i, 4) * 4 + lax.rem(cx + j, 4)
+                pltpu.make_async_remote_copy(
+                    src_ref=o_st.at[0], dst_ref=r_buf.at[side, n], send_sem=os.at[0, 0], recv_sem=orv.at[side, n],
+                    device_id=(side, bp), device_id_type=MESH).wait_recv()
+            n = lax.rem(ca + i, 4) * 4 + lax.rem(cx + j, 4)
+            pltpu.make_async_remote_copy(
+                src_ref=o_st.at[0], dst_ref=r_buf.at[other, n], send_sem=os.at[0, 0], recv_sem=orv.at[other, n],
+                device_id=(side, bp), device_id_type=MESH).wait_recv()
+    squares = jnp.zeros((S, 128), F32)
+    for y in range(4):
+        for z in range(4):
+            for m in range(2):
+                pieces = []
+                for x in (2 * m, 2 * m + 1):
+                    pieces.append(r_buf[0, z * 4 + x, :, y * 64:(y + 1) * 64].astype(F32)
+                                  + r_buf[1, y * 4 + x, :, z * 64:(z + 1) * 64].astype(F32))
+                at = (y * 8 + z * 2 + m) * 128
+                tile = res_ref[:, at:at + 128].astype(F32) + jnp.concatenate(pieces, axis=1)
+                hid_ref[:, at:at + 128] = tile
+                squares = squares + tile * tile
+    scaling = lax.rsqrt(jnp.sum(squares, axis=1, keepdims=True) * (1.0 / D) + 1e-06)
+    for at in range(0, D, 512):
+        nrm_ref[:, at:at + 512] = (hid_ref[:, at:at + 512] * scaling * gain_ref[:, at:at + 512]).astype(BF)
+    for ring in (ring_w, ra, rb, rc, rd):
+        ring.drain()
+    for copy in sent:
+        copy.wait_send()
+
+
+def attention_half(q, k, v, lens, wt, res, gain):
+    vm = pl.BlockSpec(memory_space=pltpu.VMEM)
+    hb = pl.BlockSpec(memory_space=pl.ANY)
+    sm = pl.BlockSpec(memory_space=pltpu.SMEM)
+    dma = pltpu.SemaphoreType.DMA
+    return pl.pallas_call(
+        kernel_a,
+        out_shape=(jax.ShapeDtypeStruct((S, D), F32), jax.ShapeDtypeStruct((S, D), BF)),
+        in_specs=[hb, hb, hb, sm, hb, vm, vm],
+        out_specs=(vm, vm),
+        scratch_shapes=[
+            pltpu.VMEM((S, 4096), BF), pltpu.VMEM((S, CTX, 256), BF), pltpu.VMEM((S, CTX, 256), BF),
+            pltpu.VMEM((4, 64, 4096), BF), pltpu.VMEM((4, 4, S, 2048), BF), pltpu.VMEM((4, 4, S, 2048), BF),
+            pltpu.VMEM((16, S, 256), BF), pltpu.VMEM((2, 16, S, 256), BF),
+            dma((4,)), dma((4,)), dma((4,)), dma((4,)), dma((4,)), dma((4,)), dma((4,)),
+            dma((4,)), dma((4,)), dma((4,)), dma((4,)), dma((16, 2)), dma((2, 16)),
+        ],
+        compiler_params=pltpu.CompilerParams(collective_id=0, has_side_effects=True, vmem_limit_bytes=40 << 20),
+        name="attention_half",
+    )(q, k, v, lens, wt, res, gain)
 
 
 def from_behind(value, axis, steps):
@@ -32,26 +267,6 @@
     onehot = (flat_ids[:, None] == jnp.arange(groups, dtype=jnp.int32)[None, :]).astype(jnp.int32)
     running = jnp.cumsum(onehot, axis=0)
     return jnp.sum(onehot * running, axis=1) - 1
-
-
-def attend(query_heads, key_cache, value_cache, cache_lengths):
-    session_count = query_heads.shape[0]
-    group_size = HQ // KVH
-    queries = query_heads.reshape(session_count, KVH, group_size, HD)
-    key_heads = key_cache.reshape(session_count, CTX, KVH, HD)
-    value_heads = value_cache.reshape(session_count, CTX, KVH, HD)
-    scores = jnp.einsum(
-        "skgd,stkd->skgt", queries, key_heads, preferred_element_type=jnp.float32
-    ) * HD ** (-0.5)
-    visible = jnp.arange(CTX, dtype=jnp.int32)[None, :] < cache_lengths[:, None]
-    scores = jnp.where(visible[:, None, None, :], scores, -1e30)
-    row_max = jnp.max(scores, axis=-1, keepdims=True)
-    lifted = jnp.exp(scores - row_max)
-    softmax_weights = (lifted / jnp.sum(lifted, axis=-1, keepdims=True)).astype(jnp.bfloat16)
-    attended = jnp.einsum(
-        "skgt,stkd->skgd", softmax_weights, value_heads, preferred_element_type=jnp.float32
-    )
-    return attended.astype(jnp.bfloat16).reshape(session_count, HQ * HD)
 
 
 def expert_rows(token_rows, expert_gate_up, expert_down):
@@ -80,24 +295,9 @@
     model_width = residual.shape[1]
     capacity = max(2, 2 * session_count * TOPK // groups)
     total_slots = groups * capacity
-    attn_out = lax.cond(
-        on_attention,
-        attend,
-        lambda *operands: jnp.zeros((session_count, HQ * HD), jnp.bfloat16),
-        query_heads,
-        key_cache,
-        value_cache,
-        cache_lengths,
-    )
-    columns = jnp.dot(
-        lax.all_gather(attn_out, "grp", axis=0, tiled=True),
-        out_weight,
-        preferred_element_type=jnp.float32,
-    )
-    attn_proj = lax.all_to_all(columns, "grp", split_axis=0, concat_axis=1, tiled=True)
-    hidden = residual.astype(jnp.float32) + attn_proj
-    scaling = lax.rsqrt(jnp.mean(hidden * hidden, axis=-1, keepdims=True) + 1e-06)
-    normed = (hidden * scaling * norm_gain).astype(jnp.bfloat16)
+    hidden, normed = attention_half(
+        query_heads, key_cache, value_cache, cache_lengths, out_weight.T, residual, norm_gain.reshape(1, -1)
+    )
     slot_index = slots_of(expert_ids, groups)
     position = expert_ids.reshape(-1) * capacity + slot_index
     placing = jnp.arange(total_slots, dtype=jnp.int32)[:, None] == position[None, :]

time: 253 us -> 141 us (0.56)
  waiting for transfers between devices: 173 us -> 56.1 us
  Pallas kernels: 0 us -> 37.5 us
  matrix products: 17.6 us -> 3.24 us
  between operations: 13.6 us -> 0.13 us
  starting transfers between devices: 32.3 us -> 25.3 us
  local copies, waits for them, and re-layouts: 11 us -> 15.3 us
  other arithmetic: 3.96 us -> 1.38 us
    all_gather x1 -> x0, waiting for transfers between devices: 106 us -> none  [body(): lax.all_gather(attn_out, 'grp', axis=0, tiled=True)]
    pallas_call x0 -> x1, Pallas kernels: none -> 37.5 us  [attention_half(): pl.pallas_call(kernel_a, out_shape=(jax.ShapeDtypeStruct((S, D), F32), ja...]
    dot_general x3 -> x0, matrix products: 14.3 us -> none  [the longest x1 8.09 us: body(): jnp.dot(lax.all_gather(attn_out, 'grp', axis=0, tiled=True), out_weight,...]
    all_to_all x1 -> x0, waiting for transfers between devices: 10.5 us -> none  [body(): lax.all_to_all(columns, 'grp', split_axis=0, concat_axis=1, tiled=True)]
    all_to_all x1 -> x0, starting transfers between devices: 8.73 us -> none  [body(): lax.all_to_all(columns, 'grp', split_axis=0, concat_axis=1, tiled=True)]
    unnamed x18 -> x20, local copies, waits for them, and re-layouts: 3.36 us -> 9.8 us
  transfers between devices with their start and end apart: 6 -> 4, of which waited for: 6 -> 4; matrix products, arithmetic and copies ran while one was open for 0% -> 0% of each run, Pallas kernels for 0% -> 0%
where the time goes in v1:
time: 141 us; the launch traced here: 139 us
  waiting for transfers between devices  56.1 us (40%)
  Pallas kernels  37.5 us (27%)
  starting transfers between devices  25.3 us (18%)
  local copies, waits for them, and re-layouts  15.3 us (11%)
  matrix products  3.24 us (2%)
    pallas_call x1, Pallas kernels, attention_half(): pl.pallas_call(kernel_a, out_shape=(jax.ShapeDtypeStruct((S, D), F32), ja...  37.5 us
    all_to_all x1, waiting for transfers between devices, body(): lax.all_to_all(crossed, 'grp', split_axis=0, concat_axis=0, tiled=True)  31.3 us
    all_to_all x1, waiting for transfers between devices, body(): lax.all_to_all(results, 'grp', split_axis=0, concat_axis=0, tiled=True)  21.1 us
    ppermute x1, starting transfers between devices, partner(): return lax.ppermute(block, axis, route)  11.3 us
    unnamed x20, local copies, waits for them, and re-layouts  9.8 us
    all_to_all x1, starting transfers between devices, body(): lax.all_to_all(crossed, 'grp', split_axis=0, concat_axis=0, tiled=True)  5.85 us
    all_to_all x1, starting transfers between devices, body(): lax.all_to_all(results, 'grp', split_axis=0, concat_axis=0, tiled=True)  4.82 us
    ppermute x1, starting transfers between devices, from_behind(): lax.ppermute(value, axis, [(source, source + steps) for source in range(l...  3.32 us
  transfers between devices with their start and end apart: 4, of which 4 were waited for; matrix products, arithmetic and copies ran while one was open for 0% of the time, Pallas kernels for 0%

profile of v1, /device:TPU:0, one launch (start us, length us, event | category | flops | bytes accessed | tf_op | source)
XLA Modules:
  0.0 138.9 jit_solution(4760822068838227272)
XLA Ops:
  0.0 0.8 copy.20
  0.8 0.1 eq.47
  0.8 0.1 fusion.15
  0.9 0.2 reduce_window_sum.11
  1.1 0.2 select_reduce_fusion.1
  1.3 0.1 sub.7
  1.4 0.1 fusion.14
  1.5 0.0 copy-start
  1.5 1.6 %copy-done = bf16[16,128,512]{2,1,0:T(8,128)(2,1)S(1)} copy-done((bf16[16,128,512]{2,1,0:T(8,128)(2,1)S(1)}, bf16[16,128,512]{2,1,0:T(8,128)(2,1)}, u32[]{:S(2)}) %copy-start) | copy-done | bytes 2097176
  3.1 0.0 copy-start.1
  3.1 1.6 %copy-done.1 = bf16[16,128,512]{2,1,0:T(8,128)(2,1)S(1)} copy-done((bf16[16,128,512]{2,1,0:T(8,128)(2,1)S(1)}, bf16[16,128,512]{2,1,0:T(8,128)(2,1)}, u32[]{:S(2)}) %copy-start.1) | copy-done | bytes 2097176
  4.7 0.0 copy-start.2
  4.7 1.2 copy-done.2
  5.9 0.0 copy-start.3
  5.9 0.9 copy-done.3
  6.9 0.0 copy-start.4
  6.9 0.9 copy-done.4
  7.8 0.0 copy-start.5
  7.8 0.7 copy-done.5
  8.5 0.0 copy-start.6
  8.5 0.7 copy-done.6
  9.2 37.5 %attention_half.1 = (f32[16,4096]{1,0:T(8,128)S(1)}, bf16[16,4096]{1,0:T(8,128)(2,1)S(1)}) custom-call(bf16[16,8192]{1,0:T(8,128)(2,1)S(1)} %copy-done.3, bf16[16,128,512]{2,1,0:T(8,128)(2,1)S(1)} %copy-done, bf16[16,128,512]{2,1,0:T(8,128)(2,1)S(1)} %copy-done.1, s32[16]{0:T(128)S(1)} %copy-done.6, bf16[64,8192]{1,0:T(8,128)(2,1)S(1)} %bitcast.15, ...), custom_call_target="tpu_custom_call" | custom-call | tf_op jit(solution)/shard_map/attention_half/pallas_call | solution.py:232
  46.7 0.7 convolution_convert_fusion
  47.4 2.2 %reshape.62 = bf16[64,4,4096]{2,1,0:T(4,128)(2,1)} reshape(bf16[256,4096]{1,0:T(8,128)(2,1)S(1)} %convolution_convert_fusion) | data formatting | bytes 4194304 | tf_op jit(solution)/shard_map/reshape | solution.py:310
  49.6 3.3 %collective-permute-start = (bf16[64,4,4096]{2,1,0:T(4,128)(2,1)}, bf16[64,4,4096]{2,1,0:T(4,128)(2,1)}, u32[]{:S(2)}, u32[]{:S(2)}) collective-permute-start(bf16[64,4,4096]{2,1,0:T(4,128)(2,1)} %reshape.62), channel_id=1, source_target_pairs={{0,64},{1,65},{2,66},{3,67},{4,68},{5,69},{6,70},{7,71},{8,72},{9,... | collective-permute-start | bytes 6291464 | tf_op jit(solution)/shard_map/ppermute | solution.py:252
  53.0 2.8 %collective-permute-done = bf16[64,4,4096]{2,1,0:T(4,128)(2,1)} collective-permute-done((bf16[64,4,4096]{2,1,0:T(4,128)(2,1)}, bf16[64,4,4096]{2,1,0:T(4,128)(2,1)}, u32[]{:S(2)}, u32[]{:S(2)}) %collective-permute-start) | collective-permute-done | bytes 2097184 | tf_op jit(solution)/shard_map/ppermute | solution.py:252
  55.8 5.8 %all-to-all-start = ((bf16[64,4,4096]{2,1,0:T(4,128)(2,1)}), bf16[64,4,4096]{2,1,0:T(4,128)(2,1)S(1)}, u32[]{:S(2)}, u32[]{:S(2)}) async-start(bf16[64,4,4096]{2,1,0:T(4,128)(2,1)} %collective-permute-done), calls=%async_computation | async-start | bytes 4194304 | tf_op jit(solution)/shard_map/all_to_all | solution.py:323
  61.6 31.3 %all-to-all-done = bf16[64,4,4096]{2,1,0:T(4,128)(2,1)S(1)} async-done(((bf16[64,4,4096]{2,1,0:T(4,128)(2,1)}), bf16[64,4,4096]{2,1,0:T(4,128)(2,1)S(1)}, u32[]{:S(2)}, u32[]{:S(2)}) %all-to-all-start) | async-done | bytes 2097184 | tf_op jit(solution)/shard_map/all_to_all | solution.py:323
  92.9 1.0 conditional.1
  92.9 1.0 broadcast.42
  93.9 0.0 copy-start.7
  93.9 1.3 copy-done.7
  95.3 0.0 copy-start.8
  95.3 4.8 %all-to-all-start.1 = ((bf16[64,4,4096]{2,1,0:T(4,128)(2,1)}), bf16[64,4,4096]{2,1,0:T(4,128)(2,1)S(1)}, u32[]{:S(2)}, u32[]{:S(2)}) async-start(bf16[64,4,4096]{2,1,0:T(4,128)(2,1)} %copy-done.7), calls=%async_computation.1 | async-start | bytes 4194304 | tf_op jit(solution)/shard_map/all_to_all | solution.py:325
  100.1 0.0 copy-done.8
  100.1 0.1 copy.22
  100.2 0.1 select_reduce_fusion
  100.3 21.1 %all-to-all-done.1 = bf16[64,4,4096]{2,1,0:T(4,128)(2,1)S(1)} async-done(((bf16[64,4,4096]{2,1,0:T(4,128)(2,1)}), bf16[64,4,4096]{2,1,0:T(4,128)(2,1)S(1)}, u32[]{:S(2)}, u32[]{:S(2)}) %all-to-all-start.1) | async-done | bytes 2097184 | tf_op jit(solution)/shard_map/all_to_all | solution.py:325
  121.4 2.1 %reshape.63 = bf16[256,4096]{1,0:T(8,128)(2,1)} reshape(bf16[64,4,4096]{2,1,0:T(4,128)(2,1)S(1)} %all-to-all-done.1) | data formatting | bytes 4194304 | tf_op jit(solution)/shard_map/reshape | solution.py:333
  123.4 2.5 %fusion.16 = f32[16,4096]{1,0:T(8,128)S(1)} fusion(f32[16,256]{1,0:T(8,128)S(1)} %select_reduce_fusion, bf16[256,4096]{1,0:T(8,128)(2,1)} %reshape.63), kind=kOutput, calls=%fused_computation.24 | convolution fusion | flops 201326592 | bytes 2375680 | tf_op jit(solution)/shard_map/dot_general | solution.py:331
  126.0 11.3 %collective-permute-start.1 = (f32[16,2048]{1,0:T(8,128)S(1)}, f32[16,2048]{1,0:T(8,128)S(1)}, u32[]{:S(2)}, u32[]{:S(2)}) collective-permute-start(f32[16,2048]{1,0:T(8,128)S(1)} %slice_select_fusion), channel_id=1, source_target_pairs={{0,64},{64,0},{1,65},{65,1},{2,66},{66,2},{3,67},{67,3},{4,68},{68... | collective-permute-start | bytes 393224 | tf_op jit(solution)/shard_map/ppermute | solution.py:262
  137.3 1.0 collective-permute-done.1
  138.3 0.7 fusion.12
  (3 shorter events, 0.0 us)
Async XLA Ops:
  1.5 1.6 %copy-start = (bf16[16,128,512]{2,1,0:T(8,128)(2,1)S(1)}, bf16[16,128,512]{2,1,0:T(8,128)(2,1)}, u32[]{:S(2)}) copy-start(bf16[16,128,512]{2,1,0:T(8,128)(2,1)} %k_ref.1) | copy-start | bytes 6291460
  3.1 1.6 %copy-start.1 = (bf16[16,128,512]{2,1,0:T(8,128)(2,1)S(1)}, bf16[16,128,512]{2,1,0:T(8,128)(2,1)}, u32[]{:S(2)}) copy-start(bf16[16,128,512]{2,1,0:T(8,128)(2,1)} %v_ref.1) | copy-start | bytes 6291460
  4.7 1.2 copy-start.2
  5.9 0.9 copy-start.3
  6.9 0.9 copy-start.4
  7.8 0.7 copy-start.5
  8.5 0.7 copy-start.6
  49.6 6.1 %collective-permute-start = (bf16[64,4,4096]{2,1,0:T(4,128)(2,1)}, bf16[64,4,4096]{2,1,0:T(4,128)(2,1)}, u32[]{:S(2)}, u32[]{:S(2)}) collective-permute-start(bf16[64,4,4096]{2,1,0:T(4,128)(2,1)} %reshape.62), channel_id=1, source_target_pairs={{0,64},{1,65},{2,66},{3,67},{4,68},{5,69},{6,70},{7,71},{8,72},{9,... | collective-permute-start | bytes 6291464 | tf_op jit(solution)/shard_map/ppermute | solution.py:252
  55.8 37.2 %all-to-all-start = ((bf16[64,4,4096]{2,1,0:T(4,128)(2,1)}), bf16[64,4,4096]{2,1,0:T(4,128)(2,1)S(1)}, u32[]{:S(2)}, u32[]{:S(2)}) async-start(bf16[64,4,4096]{2,1,0:T(4,128)(2,1)} %collective-permute-done), calls=%async_computation | async-start | bytes 4194304 | tf_op jit(solution)/shard_map/all_to_all | solution.py:323
  93.9 1.4 copy-start.7
  95.3 4.8 %copy-start.8 = (f32[16,8]{0,1:T(8,128)S(1)}, f32[16,8]{0,1:T(8,128)}, u32[]{:S(2)}) copy-start(f32[16,8]{0,1:T(8,128)} %param.21) | copy-start | bytes 1540
  95.3 26.1 %all-to-all-start.1 = ((bf16[64,4,4096]{2,1,0:T(4,128)(2,1)}), bf16[64,4,4096]{2,1,0:T(4,128)(2,1)S(1)}, u32[]{:S(2)}, u32[]{:S(2)}) async-start(bf16[64,4,4096]{2,1,0:T(4,128)(2,1)} %copy-done.7), calls=%async_computation.1 | async-start | bytes 4194304 | tf_op jit(solution)/shard_map/all_to_all | solution.py:325
  126.0 12.3 %collective-permute-start.1 = (f32[16,2048]{1,0:T(8,128)S(1)}, f32[16,2048]{1,0:T(8,128)S(1)}, u32[]{:S(2)}, u32[]{:S(2)}) collective-permute-start(f32[16,2048]{1,0:T(8,128)S(1)} %slice_select_fusion), channel_id=1, source_target_pairs={{0,64},{64,0},{1,65},{65,1},{2,66},{66,2},{3,67},{67,3},{4,68},{68... | collective-permute-start | bytes 393224 | tf_op jit(solution)/shard_map/ppermute | solution.py:262

commit v2 on v1

v2 whole, which is shorter than its diff:
```python
import jax
import jax.numpy as jnp
from jax import lax
from jax.experimental import pallas as pl
from jax.experimental.pallas import tpu as pltpu
from jax.sharding import PartitionSpec as P

HQ = 64
KVH = 4
HD = 128
HID = 768
TOPK = 8
CTX = 128
D = 4096
S = 16
MESH = pl.DeviceIdType.MESH
BF = jnp.bfloat16
F32 = jnp.float32
NT = (((1,), (1,)), ((), ()))


def place():
    side = lax.axis_index("side")
    g = lax.axis_index("grp")
    sa = 16 - 12 * side
    sb = 4 + 12 * side
    ca = lax.rem(g // sa, 4)
    cb = lax.rem(g // sb, 4)
    cx = lax.rem(g, 4)
    return side, g, sa, sb, ca, cb, cx


def moved(g, c, stride, by):
    return g + (lax.rem(c + by + 4, 4) - c) * stride


def attend(q_buf, k_buf, v_buf, lens_ref, kv, out):
    lane = lax.broadcasted_iota(jnp.int32, (S, CTX), 1)
    row = lax.broadcasted_iota(jnp.int32, (S, CTX), 0)
    live = jnp.zeros((S, CTX), jnp.int32)
    for s in range(S):
        live = jnp.where(row == s, lens_ref[s], live)
    group = HQ // KVH
    live = jnp.concatenate([live] * group, axis=0)
    lane = jnp.concatenate([lane] * group, axis=0)
    row = jnp.concatenate([row] * group, axis=0)
    queries = jnp.concatenate(
        [q_buf[:, (kv * group + j) * HD:(kv * group + j + 1) * HD] for j in range(group)], axis=0)
    scores = jnp.zeros((S * group, CTX), F32)
    for s in range(S):
        part = lax.dot_general(queries, k_buf[s, :, kv * HD:(kv + 1) * HD], NT, preferred_element_type=F32)
        scores = jnp.where(row == s, part, scores)
    scores = jnp.where(lane < live, scores * HD ** (-0.5), -1e30)
    lifted = jnp.exp(scores - jnp.max(scores, axis=1, keepdims=True))
    weights = (lifted / jnp.sum(lifted, axis=1, keepdims=True))
    spread = jnp.concatenate([jnp.where(row == s, weights, 0.0).astype(BF) for s in range(S)], axis=1)
    values = v_buf[:, :, kv * HD:(kv + 1) * HD].reshape(S * CTX, HD)
    result = jnp.dot(spread, values, preferred_element_type=F32).astype(BF)
    for j in range(group):
        out[:, j * HD:(j + 1) * HD] = result[j * S:(j + 1) * S, :]


class Links:
    def __init__(self, sends, recvs):
        self.sends, self.recvs, self.used, self.open = sends, recvs, 0, []

    def make(self, src, dst, to_side, to):
        i = self.used
        self.used += 1
        copy = pltpu.make_async_remote_copy(
            src_ref=src, dst_ref=dst, send_sem=self.sends.at[i], recv_sem=self.recvs.at[i],
            device_id=(to_side, to), device_id_type=MESH)
        self.open.append(copy)
        return copy

    def push(self, src, dst, to_side, to):
        copy = self.make(src, dst, to_side, to)
        copy.start()
        return copy

    def drain(self):
        for copy in self.open:
            copy.wait_send()


class Gather:
    def __init__(self, links, side, plus, minus, own, slot, half):
        self.links, self.side, self.plus, self.minus = links, side, plus, minus
        self.own, self.slot, self.half = own, slot, half

    def start(self):
        self.c0 = self.links.push(self.own, self.slot(0, 1), self.side, self.plus)
        self.c1 = self.links.push(self.own, self.slot(0, 3), self.side, self.minus)

    def forward(self):
        half, slot = self.half, self.slot
        self.c0.wait_recv()
        self.c2 = self.links.push(half(slot(1, 1), 0), half(slot(1, 2), 0), self.side, self.plus)
        self.c1.wait_recv()
        self.c3 = self.links.push(half(slot(3, 3), 1), half(slot(3, 2), 1), self.side, self.minus)

    def finish(self):
        self.c2.wait_recv()
        self.c3.wait_recv()


class Scatter:
    def __init__(self, links, side, plus, minus, block, stage, into, half):
        self.links, self.side, self.plus, self.minus = links, side, plus, minus
        self.block, self.stage, self.into, self.half = block, stage, into, half

    def start(self):
        stage, into, half = self.stage, self.into, self.half
        for h in range(2):
            half(stage.at[0], h)[...] = self.block(2, h).astype(BF)
        self.c0 = self.links.push(half(stage.at[0], 0), half(into.at[0], 0), self.side, self.plus)
        self.c1 = self.links.push(half(stage.at[0], 1), half(into.at[0], 1), self.side, self.minus)
        half(stage.at[1], 1)[...] = self.block(3, 1).astype(BF)
        half(stage.at[2], 0)[...] = self.block(1, 0).astype(BF)

    def forward(self):
        stage, into, half = self.stage, self.into, self.half
        self.c0.wait_recv()
        half(stage.at[1], 0)[...] = (self.block(3, 0) + half(into.at[0], 0)[...].astype(F32)).astype(BF)
        self.c2 = self.links.push(stage.at[1], into.at[1], self.side, self.plus)
        self.c1.wait_recv()
        half(stage.at[2], 1)[...] = (self.block(1, 1) + half(into.at[0], 1)[...].astype(F32)).astype(BF)
        self.c3 = self.links.push(stage.at[2], into.at[2], self.side, self.minus)

    def finish(self):
        self.c2.wait_recv()
        self.c3.wait_recv()

    def result(self, h):
        return (self.block(0, h) + self.half(self.into.at[1], h)[...].astype(F32)
                + self.half(self.into.at[2], h)[...].astype(F32))


def routing(info, order, experts):
    lane = lax.broadcasted_iota(jnp.int32, (16, 128), 1)
    tiles = []
    for t in range(2):
        tile = jnp.zeros((16, 128), F32)
        for i in range(8):
            b, x = order(t * 8 + i)
            block = info[x, b]
            moved_block = pltpu.roll(block, 16 * i, 1) if i else block
            tile = jnp.where(lane // 16 == i, moved_block, tile)
        tiles.append(tile)
    table = jnp.concatenate(tiles, axis=1)
    ids, route = table[0:8, :], table[8:16, :]
    first = lax.broadcasted_iota(jnp.int32, (256, 256), 0)
    later = lax.broadcasted_iota(jnp.int32, (256, 256), 1)
    before = jnp.where((first // 16 == later // 16) & (first < later), 1.0, 0.0).astype(BF)
    token = lax.broadcasted_iota(jnp.int32, (8, 256), 1) // 16
    named, weight = [], []
    for e in experts:
        hit = ids == e.astype(F32)
        named.append(jnp.sum(jnp.where(hit, 1.0, 0.0), axis=0, keepdims=True))
        weight.append(jnp.sum(jnp.where(hit, route, 0.0), axis=0, keepdims=True))
    named8 = jnp.concatenate(named + [jnp.zeros((4, 256), F32)], axis=0)
    rank = jnp.dot(named8.astype(BF), before, preferred_element_type=F32)
    b, x = order(token)
    spot = jnp.where(named8 > 0.5, (b * 4 + x).astype(F32) * 4.0 + rank, -1.0)
    rows = lax.broadcasted_iota(jnp.int32, (64, 256), 0).astype(F32)
    picks, weighted = [], []
    for i in range(4):
        hit = rows == spot[i:i + 1, :]
        picks.append(jnp.where(hit, 1.0, 0.0))
        weighted.append(jnp.where(hit, weight[i], 0.0))
    return jnp.concatenate(picks, axis=0).astype(BF), jnp.concatenate(weighted, axis=0)


def order0(n):
    return n % 4, n // 4


def order1(n):
    return n // 4, n % 4


def kernel(q_ref, k_ref, v_ref, lens_ref, wt_ref, res_ref, gain_ref, ids_ref, route_ref, up_ref, down_ref, out_ref,
           q_buf, k_buf, v_buf, w_buf, g0, g1, o_st, r_buf, hid, info, n0, n1, x_st, x_own, x_far, x_via,
           wg, wu, wd, a_own, a_far, y_st, z_buf, z_via, m0, m1, st0, in0, st1, in1, st2, in2, st3, in3, f0, f1,
           loc, sends, recvs, os, orv):
    side, g, sa, sb, ca, cb, cx = place()
    other = 1 - side
    ap, am = moved(g, ca, sa, 1), moved(g, ca, sa, -1)
    bp, bm = moved(g, cb, sb, 1), moved(g, cb, sb, -1)
    xp, xm = moved(g, cx, 1, 1), moved(g, cx, 1, -1)
    links = Links(sends, recvs)
    barrier = pltpu.get_barrier_semaphore()

    def hello(to_side, to):
        pl.semaphore_signal(barrier, inc=1, device_id=(to_side, to), device_id_type=MESH)

    hello(side, ap)
    hello(side, am)
    for i in range(4):
        for j in range(4):
            if i or j:
                hello(side, moved(moved(g, cb, sb, i), cx, 1, j))
            hello(other, moved(moved(g, ca, sa, i), cx, 1, j))

    def fetch(src, dst, i):
        copy = pltpu.make_async_copy(src, dst, loc.at[i])
        copy.start()
        return copy

    def at_side(base, size):
        return pl.ds(pl.multiple_of(base * size, 128), size)

    c_q = fetch(q_ref.at[:, at_side(side, 4096)], q_buf, 0)
    c_k = fetch(k_ref.at[:, :, at_side(side, 256)], k_buf, 1)
    c_v = fetch(v_ref.at[:, :, at_side(side, 256)], v_buf, 2)
    w_own = wt_ref.at[:, at_side(side, 4096)]
    c_w = fetch(w_own, w_buf.at[ca], 3)
    c_ffn = []
    for h in range(2):
        depth = at_side(side if h == 0 else other, 2048)
        c_ffn.append(fetch(up_ref.at[depth, at_side(side, 384)], wg.at[h], 4 + h))
        c_ffn.append(fetch(up_ref.at[depth, at_side(side + 2, 384)], wu.at[h], 6 + h))
        c_ffn.append(fetch(down_ref.at[at_side(side if h == 0 else other, 384), at_side(side, 2048)], wd.at[h], 8 + h))
    info[0, 0] = jnp.zeros((16, 128), F32)
    info[0, 0, 0:8, 0:16] = ids_ref[...].astype(F32)
    info[0, 0, 8:16, 0:16] = route_ref[...]
    pl.semaphore_wait(barrier, 33)

    def gather(plus, minus, own, slot, half):
        return Gather(links, side, plus, minus, own, slot, half)

    def first(buf, plus, minus, half):
        return gather(plus, minus, buf.at[0, 0], lambda source, at: buf.at[0, at], half)

    def second(buf, plus, minus):
        return gather(plus, minus, buf.at[0], lambda source, at: buf.at[at], lambda ref, h: ref.at[h * 2:(h + 1) * 2])

    def cut(size):
        return lambda ref, h: ref.at[:, h * size:(h + 1) * size]

    ring_w = gather(ap, am, w_own, lambda source, at: w_buf.at[lax.rem(ca - source + 4, 4)],
                    lambda ref, h: ref.at[h * 32:(h + 1) * 32])
    ring_w.start()
    tell = first(info, bp, bm, lambda ref, h: ref.at[h * 8:(h + 1) * 8])
    tell_on = second(info, xp, xm)
    tell.start()
    c_q.wait()
    c_k.wait()
    c_v.wait()
    ra, rb = first(g0, bp, bm, cut(1024)), first(g1, xp, xm, cut(1024))
    rc, rd = second(g0, xp, xm), second(g1, bp, bm)
    attend(q_buf, k_buf, v_buf, lens_ref, 0, g0.at[0, 0])
    ra.start()
    tell.forward()
    attend(q_buf, k_buf, v_buf, lens_ref, 1, g1.at[0, 0])
    rb.start()
    tell.finish()
    tell_on.start()
    ra.forward()
    rb.forward()
    ra.finish()
    rc.start()
    rb.finish()
    rd.start()
    tell_on.forward()
    ring_w.forward()
    rc.forward()
    rd.forward()
    tell_on.finish()
    experts = [moved(g, ca, sa, i) for i in range(4)]
    pick0, weigh0 = routing(info, order0, experts)
    pick1, weigh1 = routing(info, order1, experts)
    c_w.wait()
    ring_w.finish()
    rc.finish()
    p0 = lax.dot_general(g0[...].reshape(256, 2048), w_buf[:, :, 0:2048].reshape(256, 2048), NT,
                         preferred_element_type=F32)
    rd.finish()
    p1 = lax.dot_general(g1[...].reshape(256, 2048), w_buf[:, :, 2048:4096].reshape(256, 2048), NT,
                         preferred_element_type=F32)
    mine = cb * 4 + cx
    for n in range(16):
        bi, xi = n // 4, n % 4
        u = (xi * 4 + bi) * S
        block = (p0[u:u + S, :] + p1[n * S:(n + 1) * S, :]).astype(BF)
        o_st[n] = block
        if n == 0:
            r_buf[side, mine] = block
    sent = []
    for n in range(16):
        to = moved(moved(g, cb, sb, -(n // 4)), cx, 1, -(n % 4))
        for e in range(2):
            if n == 0 and e == 0:
                continue
            copy = pltpu.make_async_remote_copy(
                src_ref=o_st.at[n], dst_ref=r_buf.at[side, mine], send_sem=os.at[n, e], recv_sem=orv.at[side, mine],
                device_id=(side if e == 0 else other, to), device_id_type=MESH)
            copy.start()
            sent.append(copy)

    def arrived(source_side, n):
        pltpu.make_async_remote_copy(
            src_ref=o_st.at[0], dst_ref=r_buf.at[source_side, n], send_sem=os.at[0, 0], recv_sem=orv.at[source_side, n],
            device_id=(side, bp), device_id_type=MESH).wait_recv()

    for i in range(4):
        for j in range(4):
            if i or j:
                arrived(side, lax.rem(cb + i, 4) * 4 + lax.rem(cx + j, 4))
            arrived(other, lax.rem(ca + i, 4) * 4 + lax.rem(cx + j, 4))
    squares = jnp.zeros((S, 128), F32)
    for y in range(4):
        for z in range(4):
            for m in range(2):
                pieces = []
                for x in (2 * m, 2 * m + 1):
                    pieces.append(r_buf[0, z * 4 + x, :, y * 64:(y + 1) * 64].astype(F32)
                                  + r_buf[1, y * 4 + x, :, z * 64:(z + 1) * 64].astype(F32))
                at = (y * 8 + z * 2 + m) * 128
                tile = res_ref[:, at:at + 128].astype(F32) + jnp.concatenate(pieces, axis=1)
                hid[:, at:at + 128] = tile
                squares = squares + tile * tile
    scaling = lax.rsqrt(jnp.sum(squares, axis=1, keepdims=True) * (1.0 / D) + 1e-06)

    def columns(r):
        return pl.ds(pl.multiple_of(side * 2048 + r * 1024, 128), 1024)

    na, nb = first(n0, bp, bm, cut(512)), first(n1, xp, xm, cut(512))
    nc, nd = second(n0, xp, xm), second(n1, bp, bm)
    n0[0, 0] = (hid[:, columns(0)] * scaling * gain_ref[:, columns(0)]).astype(BF)
    na.start()
    n1[0, 0] = (hid[:, columns(1)] * scaling * gain_ref[:, columns(1)]).astype(BF)
    nb.start()
    na.forward()
    nb.forward()
    na.finish()
    nc.start()
    nb.finish()
    nd.start()
    nc.forward()
    nd.forward()

    def part(r):
        return slice(r * 1024, (r + 1) * 1024)

    nc.finish()
    rows = jnp.dot(pick0, n0[...].reshape(256, 1024), preferred_element_type=F32).astype(BF).reshape(4, 4, S, 1024)
    x_own[0, :, :, part(0)] = rows[0]
    x_st[:, :, :, part(0)] = rows[1:]
    via0 = links.push(x_st.at[1, :, :, part(0)], x_via.at[0], side, ap)
    to0 = [links.push(x_st.at[0, :, :, part(0)], x_own.at[1, :, :, part(0)], side, ap),
           links.push(x_st.at[2, :, :, part(0)], x_own.at[3, :, :, part(0)], side, am)]
    nd.finish()
    rows = jnp.dot(pick1, n1[...].reshape(256, 1024), preferred_element_type=F32).astype(BF).reshape(4, 4, S, 1024)
    x_own[0, :, :, part(1)] = rows[0]
    x_st[:, :, :, part(1)] = rows[1:]
    via1 = links.push(x_st.at[1, :, :, part(1)], x_via.at[1], side, am)
    to1 = [links.push(x_st.at[0, :, :, part(1)], x_own.at[1, :, :, part(1)], side, ap),
           links.push(x_st.at[2, :, :, part(1)], x_own.at[3, :, :, part(1)], side, am)]
    swaps = [links.push(x_own.at[0], x_far.at[:, 0], other, g)]
    via0.wait_recv()
    on0 = links.push(x_via.at[0], x_own.at[2, :, :, part(0)], side, ap)
    via1.wait_recv()
    on1 = links.push(x_via.at[1], x_own.at[2, :, :, part(1)], side, am)
    to0[0].wait_recv()
    to1[0].wait_recv()
    swaps.append(links.push(x_own.at[1], x_far.at[:, 1], other, g))
    to0[1].wait_recv()
    to1[1].wait_recv()
    swaps.append(links.push(x_own.at[3], x_far.at[:, 3], other, g))
    on0.wait_recv()
    on1.wait_recv()
    swaps.append(links.push(x_own.at[2], x_far.at[:, 2], other, g))
    for copy in c_ffn:
        copy.wait()
    near = x_own[...].reshape(256, 2048)
    gate = jnp.dot(near, wg[0], preferred_element_type=F32)
    up = jnp.dot(near, wu[0], preferred_element_type=F32)
    for copy in swaps:
        copy.wait_recv()
    far = x_far[...].reshape(256, 2048)
    gate = gate + jnp.dot(far, wg[1], preferred_element_type=F32)
    up = up + jnp.dot(far, wu[1], preferred_element_type=F32)
    a_own[...] = (gate / (1.0 + jnp.exp(-gate)) * up).astype(BF).reshape(4, 4, S, 384)
    swaps = [links.push(a_own.at[i], a_far.at[:, i], other, g) for i in range(4)]
    results = jnp.dot(a_own[...].reshape(256, 384), wd[0], preferred_element_type=F32)
    for copy in swaps:
        copy.wait_recv()
    results = results + jnp.dot(a_far[...].reshape(256, 384), wd[1], preferred_element_type=F32)
    results = results.astype(BF).reshape(4, 64, 2048)
    z_buf[0] = results[0]
    y_st[...] = results[1:]
    via0 = links.push(y_st.at[1, :, part(0)], z_via.at[0], side, ap)
    via1 = links.push(y_st.at[1, :, part(1)], z_via.at[1], side, am)
    back = [links.push(y_st.at[0], z_buf.at[1], side, am), links.push(y_st.at[2], z_buf.at[3], side, ap)]
    via0.wait_recv()
    on0 = links.push(z_via.at[0], z_buf.at[2, :, part(0)], side, ap)
    via1.wait_recv()
    on1 = links.push(z_via.at[1], z_buf.at[2, :, part(1)], side, am)
    for copy in back + [on0, on1]:
        copy.wait_recv()

    def mix(weigh, r):
        high = weigh.astype(BF)
        low = (weigh - high.astype(F32)).astype(BF)
        both = jnp.concatenate([high, low], axis=1)
        both = lax.dot_general(both, z_buf[:, :, part(r)].reshape(256, 1024), (((0,), (0,)), ((), ())),
                               preferred_element_type=F32)
        return (both[0:256, :] + both[256:512, :]).reshape(4, 4, S, 1024)

    m0[...] = mix(weigh0, 0)
    m1[...] = mix(weigh1, 1)

    def scatter_first(m, plus, minus, stage, into):
        return Scatter(links, side, plus, minus, lambda i, h: m[i, h * 2:(h + 1) * 2], stage, into,
                       lambda ref, h: ref.at[h * 2:(h + 1) * 2])

    def scatter_last(f, plus, minus, stage, into):
        return Scatter(links, side, plus, minus, lambda i, h: f[i, :, h * 512:(h + 1) * 512], stage, into, cut(512))

    sc, sd = scatter_first(m0, xp, xm, st0, in0), scatter_first(m1, bp, bm, st1, in1)
    sa0, sb0 = scatter_last(f0, bp, bm, st2, in2), scatter_last(f1, xp, xm, st3, in3)
    sc.start()
    sd.start()
    sc.forward()
    sd.forward()
    for last, before, f in ((sa0, sc, f0), (sb0, sd, f1)):
        before.finish()
        for h in range(2):
            f[h * 2:(h + 1) * 2] = before.result(h)
        last.start()
    sa0.forward()
    sb0.forward()
    for r, last in ((0, sa0), (1, sb0)):
        last.finish()
        for h in range(2):
            at = pl.ds(pl.multiple_of(side * 2048 + r * 1024 + h * 512, 128), 512)
            out_ref[:, r * 1024 + h * 512:r * 1024 + (h + 1) * 512] = (hid[:, at] + last.result(h)).astype(BF)
    links.drain()
    for copy in sent:
        copy.wait_send()


def body(q, k, v, lens, out_weight, residual, norm_gain, expert_ids, route_weights, gate_up, down_weight):
    vm = pl.BlockSpec(memory_space=pltpu.VMEM)
    hb = pl.BlockSpec(memory_space=pltpu.HBM)
    sm = pl.BlockSpec(memory_space=pltpu.SMEM)
    dma = pltpu.SemaphoreType.DMA

    def vb(*shape):
        return pltpu.VMEM(shape, BF)

    def vf(*shape):
        return pltpu.VMEM(shape, F32)

    return pl.pallas_call(
        kernel,
        out_shape=jax.ShapeDtypeStruct((S, D // 2), BF),
        in_specs=[hb, hb, hb, sm, hb, vm, vm, vm, vm, hb, hb],
        out_specs=vm,
        scratch_shapes=[
            vb(S, 4096), vb(S, CTX, 256), vb(S, CTX, 256), vb(4, 64, 4096), vb(4, 4, S, 2048), vb(4, 4, S, 2048),
            vb(16, S, 256), vb(2, 16, S, 256), vf(S, D), vf(4, 4, 16, 128), vb(4, 4, S, 1024), vb(4, 4, S, 1024),
            vb(3, 4, S, 2048), vb(4, 4, S, 2048), vb(4, 4, S, 2048), vb(2, 4, S, 1024),
            vb(2, 2048, 384), vb(2, 2048, 384), vb(2, 384, 2048), vb(4, 4, S, 384), vb(4, 4, S, 384),
            vb(3, 64, 2048), vb(4, 64, 2048), vb(2, 64, 1024), vf(4, 4, S, 1024), vf(4, 4, S, 1024),
            vb(3, 4, S, 1024), vb(3, 4, S, 1024), vb(3, 4, S, 1024), vb(3, 4, S, 1024),
            vb(3, S, 1024), vb(3, S, 1024), vb(3, S, 1024), vb(3, S, 1024), vf(4, S, 1024), vf(4, S, 1024),
            dma((10,)), dma((96,)), dma((96,)), dma((16, 2)), dma((2, 16)),
        ],
        compiler_params=pltpu.CompilerParams(collective_id=0, has_side_effects=True, vmem_limit_bytes=60 << 20),
        name="decode_layer",
    )(q, k, v, lens, out_weight.T, residual, norm_gain.reshape(1, -1), expert_ids.T, route_weights.T,
      gate_up[0], down_weight[0])


def solution(mesh):
    return jax.shard_map(
        body,
        mesh=mesh,
        in_specs=(
            P("grp", None), P("grp", None, None), P("grp", None, None), P("grp"), P(None, "grp"), P("grp", None), P(),
            P("grp", None), P("grp", None), P("grp", None, None), P("grp", None, None),
        ),
        out_specs=P("grp", "side"),
        check_vma=False,
    )
```

time: 141 us -> 99.4 us (0.70); the launches traced: 139 us -> 99.2 us
  Pallas kernels: 37.5 us -> 97.7 us
  waiting for transfers between devices: 56.1 us -> 0 us
  starting transfers between devices: 25.3 us -> 0 us
  local copies, waits for them, and re-layouts: 15.3 us -> 1.47 us
  matrix products: 3.24 us -> 0 us
    pallas_call x1, Pallas kernels: 37.5 us -> 97.7 us  [body(): pl.pallas_call(kernel, out_shape=jax.ShapeDtypeStruct((S, D // 2), BF), i...]
    all_to_all x2 -> x0, waiting for transfers between devices: 52.3 us -> none  [the longest x1 31.3 us: body(): lax.all_to_all(crossed, 'grp', split_axis=0, concat_axis=0, tiled=True)]
    ppermute x2 -> x0, starting transfers between devices: 14.6 us -> none  [the longest x1 11.3 us: partner(): return lax.ppermute(block, axis, route)]
    all_to_all x2 -> x0, starting transfers between devices: 10.7 us -> none  [the longest x1 5.85 us: body(): lax.all_to_all(crossed, 'grp', split_axis=0, concat_axis=0, tiled=True)]
    unnamed x20 -> x1, local copies, waits for them, and re-layouts: 9.8 us -> 1.47 us
    reshape x2 -> x0, local copies, waits for them, and re-layouts: 4.29 us -> none  [the longest x1 2.23 us: body(): outgoing_rows = outgoing_rows.reshape(groups, capacity, model_width)]
    ppermute x2 -> x0, waiting for transfers between devices: 3.79 us -> none  [the longest x1 2.8 us: from_behind(): lax.ppermute(value, axis, [(source, source + steps) for source in range(l...]
    dot_general x2 -> x0, matrix products: 3.24 us -> none  [the longest x1 2.51 us: body(): jnp.dot(weighting, returned.reshape(total_slots, model_width).astype(jnp....]
  transfers between devices with their start and end apart: 4 -> 0, of which waited for: 4 -> 0; matrix products, arithmetic and copies ran while one was open for 0% -> 0% of each run, Pallas kernels for 0% -> 0%
where the time goes in v2:
time: 99.4 us; the launch traced here: 99.2 us
  Pallas kernels  97.7 us (98%)
  local copies, waits for them, and re-layouts  1.47 us (1%)
    pallas_call x1, Pallas kernels, body(): pl.pallas_call(kernel, out_shape=jax.ShapeDtypeStruct((S, D // 2), BF), i...  97.7 us

profile of v2, /device:TPU:0, one launch (start us, length us, event | category | flops | bytes accessed | tf_op | source)
XLA Modules:
  0.0 99.2 jit_solution(8871097588394270873)
XLA Ops:
  0.0 97.7 %decode_layer.1 = bf16[16,2048]{1,0:T(8,128)(2,1)} custom-call(bf16[16,8192]{1,0:T(8,128)(2,1)} %q_ref.1, bf16[16,128,512]{2,1,0:T(8,128)(2,1)} %k_ref.1, bf16[16,128,512]{2,1,0:T(8,128)(2,1)} %v_ref.1, s32[16]{0:T(128)} %lens_ref.1, bf16[64,8192]{1,0:T(8,128)(2,1)} %bitcast.8, bf16[16,4096]{1,0:T(8,128)(2,1)} %res_ref.1, f32[1,4096]{1,0:T(1,128)} %bitcast.9, ...), custom_call_target="tpu_custom_call" | custom-call | tf_op jit(solution)/shard_map/decode_layer/pallas_call | solution.py:456
  97.7 1.5 %copy.13 = bf16[16,2048]{1,0:T(8,128)(2,1)} copy(bf16[16,2048]{1,0:T(8,128)(2,1)} %decode_layer.1) | data formatting | bytes 131072

commit v3 on v2

v3 whole, which is shorter than its diff:
```python
import jax
import jax.numpy as jnp
from jax import lax
from jax.experimental import pallas as pl
from jax.experimental.pallas import tpu as pltpu
from jax.sharding import PartitionSpec as P

HQ = 64
KVH = 4
HD = 128
HID = 768
TOPK = 8
CTX = 128
D = 4096
S = 16
MESH = pl.DeviceIdType.MESH
BF = jnp.bfloat16
F32 = jnp.float32
NT = (((1,), (1,)), ((), ()))


def place():
    side = lax.axis_index("side")
    g = lax.axis_index("grp")
    sa = 16 - 12 * side
    sb = 4 + 12 * side
    ca = lax.rem(g // sa, 4)
    cb = lax.rem(g // sb, 4)
    cx = lax.rem(g, 4)
    return side, g, sa, sb, ca, cb, cx


def moved(g, c, stride, by):
    return g + (lax.rem(c + by + 4, 4) - c) * stride


def attend(q_buf, k_buf, v_buf, lens_ref, kv, out):
    lane = lax.broadcasted_iota(jnp.int32, (S, CTX), 1)
    row = lax.broadcasted_iota(jnp.int32, (S, CTX), 0)
    live = jnp.zeros((S, CTX), jnp.int32)
    for s in range(S):
        live = jnp.where(row == s, lens_ref[s], live)
    group = HQ // KVH
    live = jnp.concatenate([live] * group, axis=0)
    lane = jnp.concatenate([lane] * group, axis=0)
    row = jnp.concatenate([row] * group, axis=0)
    queries = jnp.concatenate(
        [q_buf[:, (kv * group + j) * HD:(kv * group + j + 1) * HD] for j in range(group)], axis=0)
    scores = jnp.zeros((S * group, CTX), F32)
    for s in range(S):
        part = lax.dot_general(queries, k_buf[s, :, kv * HD:(kv + 1) * HD], NT, preferred_element_type=F32)
        scores = jnp.where(row == s, part, scores)
    scores = jnp.where(lane < live, scores * HD ** (-0.5), -1e30)
    lifted = jnp.exp(scores - jnp.max(scores, axis=1, keepdims=True))
    weights = (lifted / jnp.sum(lifted, axis=1, keepdims=True))
    spread = jnp.concatenate([jnp.where(row == s, weights, 0.0).astype(BF) for s in range(S)], axis=1)
    values = v_buf[:, :, kv * HD:(kv + 1) * HD].reshape(S * CTX, HD)
    result = jnp.dot(spread, values, preferred_element_type=F32).astype(BF)
    for j in range(group):
        out[:, j * HD:(j + 1) * HD] = result[j * S:(j + 1) * S, :]


class Links:
    def __init__(self, sends, recvs):
        self.sends, self.recvs, self.used, self.open = sends, recvs, 0, []

    def make(self, src, dst, to_side, to):
        i = self.used
        self.used += 1
        copy = pltpu.make_async_remote_copy(
            src_ref=src, dst_ref=dst, send_sem=self.sends.at[i], recv_sem=self.recvs.at[i],
            device_id=(to_side, to), device_id_type=MESH)
        self.open.append(copy)
        return copy

    def push(self, src, dst, to_side, to):
        copy = self.make(src, dst, to_side, to)
        copy.start()
        return copy

    def drain(self):
        for copy in self.open:
            copy.wait_send()


class Columns:
    def __init__(self, links, side, plus, minus, own, slot):
        self.links, self.side, self.plus, self.minus, self.own, self.slot = links, side, plus, minus, own, slot

    def start(self):
        low, high = slice(0, 32), slice(32, 64)
        push, own, slot = self.links.push, self.own, self.slot(0)
        self.c0 = push(own.at[low], slot.at[low], self.side, self.plus)
        self.c1 = push(own.at[high], slot.at[high], self.side, self.minus)
        self.rest = [push(own.at[high], slot.at[high], self.side, self.plus),
                     push(own.at[low], slot.at[low], self.side, self.minus)]

    def forward(self):
        self.c0.wait_recv()
        at = self.slot(1).at[0:32]
        self.rest.append(self.links.push(at, at, self.side, self.plus))
        self.c1.wait_recv()
        at = self.slot(3).at[32:64]
        self.rest.append(self.links.push(at, at, self.side, self.minus))

    def finish(self):
        for copy in self.rest:
            copy.wait_recv()


class Gather:
    def __init__(self, links, side, p, q, buf, half=None):
        self.links, self.side, self.p, self.q, self.buf, self.half = links, side, p, q, buf, half
        self.got = {}

    def send(self, i, j, to, di, dj, view=None):
        src, dst = self.buf.at[i, j], self.buf.at[(i + di) % 4, (j + dj) % 4]
        if view is not None:
            src, dst = self.half(src, view), self.half(dst, view)
        self.got[(i + di) % 4, (j + dj) % 4, view] = self.links.push(src, dst, self.side, to)

    def wait(self, i, j, view=None):
        self.got.pop((i, j, view)).wait_recv()

    def along_q(self, j):
        self.send(0, j, self.q[0], 1, 0)
        self.send(0, j, self.q[1], 3, 0)

    def start(self):
        self.send(0, 0, self.p[0], 0, 1)
        self.send(0, 0, self.p[1], 0, 3)
        if self.half is None:
            self.send(0, 0, self.p[2], 0, 2)
        self.along_q(0)

    def step1(self):
        self.wait(0, 1)
        if self.half is not None:
            self.send(0, 1, self.p[0], 0, 1, 0)
        self.along_q(1)
        self.wait(0, 3)
        if self.half is not None:
            self.send(0, 3, self.p[1], 0, 3, 1)
        self.along_q(3)
        self.wait(1, 0)
        self.send(1, 0, self.q[0], 1, 0)

    def step2(self):
        if self.half is None:
            self.wait(0, 2)
        else:
            self.wait(0, 2, 0)
            self.wait(0, 2, 1)
        self.along_q(2)
        self.wait(1, 1)
        self.send(1, 1, self.q[0], 1, 0)
        self.wait(3, 3)
        self.send(3, 3, self.q[1], 3, 0)

    def step3(self):
        self.wait(3, 2)
        self.send(3, 2, self.q[1], 3, 0)

    def finish(self):
        for key in list(self.got):
            self.wait(*key)


class Scatter:
    def __init__(self, links, side, p, q, m, far, over, near, last):
        self.links, self.side, self.p, self.q, self.m = links, side, p, q, m
        self.far, self.over, self.near, self.last = far, over, near, last

    def start(self):
        links, m, far, over = self.links, self.m, self.far, self.over
        self.c_far, self.c_over = {}, {}
        for j in (0, 3, 1, 2):
            far[0, j] = m[2, j].astype(BF)
            to = self.q[0] if j < 2 else self.q[1]
            self.c_far[j] = links.push(far.at[0, j], far.at[1, j], self.side, to)
        for j in (2, 1, 3, 0):
            way = 0 if j >= 2 else 1
            over[0, way, j] = m[3 if way == 0 else 1, j].astype(BF)
            self.c_over[way, j] = links.push(over.at[0, way, j], over.at[1, way, j], self.side, self.q[way])

    def forward(self):
        links, m, far, over = self.links, self.m, self.far, self.over
        for j in (0, 3, 1, 2):
            way = 0 if j < 2 else 1
            self.c_far[j].wait_recv()
            over[0, way, j] = (m[3 if way == 0 else 1, j] + far[1, j].astype(F32)).astype(BF)
            self.c_over[way, j] = links.push(over.at[0, way, j], over.at[1, way, j], self.side, self.q[way])

    def turn(self, js):
        links, near, over = self.links, self.near, self.over
        for j in js:
            self.c_over[0, j].wait_recv()
            self.c_over[1, j].wait_recv()
            block = self.m[0, j] + over[1, 0, j].astype(F32) + over[1, 1, j].astype(F32)
            if j == 0:
                self.own = block
            else:
                near[0, j] = block.astype(BF)
                self.last[j] = links.push(near.at[0, j], near.at[1, j], self.side, self.p[(None, 1, 2, 0)[j]])

    def result(self):
        block = self.own
        for j in (1, 3, 2):
            self.last[j].wait_recv()
            block = block + self.near[1, j].astype(F32)
        return block


def routing(info, order, experts):
    lane = lax.broadcasted_iota(jnp.int32, (16, 128), 1)
    tiles = []
    for t in range(2):
        tile = jnp.zeros((16, 128), F32)
        for i in range(8):
            b, x = order(t * 8 + i)
            block = info[x, b]
            moved_block = pltpu.roll(block, 16 * i, 1) if i else block
            tile = jnp.where(lane // 16 == i, moved_block, tile)
        tiles.append(tile)
    table = jnp.concatenate(tiles, axis=1)
    ids, route = table[0:8, :], table[8:16, :]
    first = lax.broadcasted_iota(jnp.int32, (256, 256), 0)
    later = lax.broadcasted_iota(jnp.int32, (256, 256), 1)
    before = jnp.where((first // 16 == later // 16) & (first < later), 1.0, 0.0).astype(BF)
    token = lax.broadcasted_iota(jnp.int32, (8, 256), 1) // 16
    named, weight = [], []
    for e in experts:
        hit = ids == e.astype(F32)
        named.append(jnp.sum(jnp.where(hit, 1.0, 0.0), axis=0, keepdims=True))
        weight.append(jnp.sum(jnp.where(hit, route, 0.0), axis=0, keepdims=True))
    named8 = jnp.concatenate(named + [jnp.zeros((4, 256), F32)], axis=0)
    rank = jnp.dot(named8.astype(BF), before, preferred_element_type=F32)
    b, x = order(token)
    spot = jnp.where(named8 > 0.5, (b * 4 + x).astype(F32) * 4.0 + rank, -1.0)
    rows = lax.broadcasted_iota(jnp.int32, (64, 256), 0).astype(F32)
    picks, weighted = [], []
    for i in range(4):
        hit = rows == spot[i:i + 1, :]
        picks.append(jnp.where(hit, 1.0, 0.0))
        weighted.append(jnp.where(hit, weight[i], 0.0))
    return jnp.concatenate(picks, axis=0).astype(BF), jnp.concatenate(weighted, axis=0)


def order0(n):
    return n % 4, n // 4


def order1(n):
    return n // 4, n % 4


def kernel(q_ref, k_ref, v_ref, lens_ref, wt_ref, res_ref, gain_ref, ids_ref, route_ref, up_ref, down_ref, out_ref,
           q_buf, k_buf, v_buf, w_buf, g0, g1, o_st, r_buf, hid, info, n0, n1, x_st, x_own, x_far, x_via,
           w_gu, wd, h_own, h_far, a_own, a_far, y_st, z_buf, z_via, m0, m1,
           far0, over0, near0, far1, over1, near1, loc, sends, recvs, os, orv):
    side, g, sa, sb, ca, cb, cx = place()
    other = 1 - side
    ap, am = moved(g, ca, sa, 1), moved(g, ca, sa, -1)
    b_way = [moved(g, cb, sb, i) for i in (1, -1, 2)]
    x_way = [moved(g, cx, 1, i) for i in (1, -1, 2)]
    links = Links(sends, recvs)
    barrier = pltpu.get_barrier_semaphore()

    def hello(to_side, to):
        pl.semaphore_signal(barrier, inc=1, device_id=(to_side, to), device_id_type=MESH)

    hello(side, ap)
    hello(side, am)
    for i in range(4):
        for j in range(4):
            if i or j:
                hello(side, moved(moved(g, cb, sb, i), cx, 1, j))
            hello(other, moved(moved(g, ca, sa, i), cx, 1, j))

    def fetch(src, dst, i):
        copy = pltpu.make_async_copy(src, dst, loc.at[i])
        copy.start()
        return copy

    def at_side(base, size):
        return pl.ds(pl.multiple_of(base * size, 128), size)

    c_q = fetch(q_ref.at[:, at_side(side, 4096)], q_buf, 0)
    c_k = fetch(k_ref.at[:, :, at_side(side, 256)], k_buf, 1)
    c_v = fetch(v_ref.at[:, :, at_side(side, 256)], v_buf, 2)
    w_own = wt_ref.at[:, at_side(side, 4096)]
    c_w = fetch(w_own, w_buf.at[ca], 3)
    info[0, 0] = jnp.zeros((16, 128), F32)
    info[0, 0, 0:8, 0:16] = ids_ref[...].astype(F32)
    info[0, 0, 8:16, 0:16] = route_ref[...]
    c_q.wait()
    c_k.wait()
    c_v.wait()
    attend(q_buf, k_buf, v_buf, lens_ref, 0, g0.at[0, 0])
    attend(q_buf, k_buf, v_buf, lens_ref, 1, g1.at[0, 0])
    pl.semaphore_wait(barrier, 33)
    ring_w = Columns(links, side, ap, am, w_own, lambda source: w_buf.at[lax.rem(ca - source + 4, 4)])
    tell = Gather(links, side, b_way, x_way, info)
    cut = lambda ref, h: ref.at[:, h * 1024:(h + 1) * 1024]
    ra = Gather(links, side, b_way, x_way, g0, cut)
    rb = Gather(links, side, x_way, b_way, g1, cut)
    ra.start()
    rb.start()
    tell.start()
    ring_w.start()
    c_ffn = []
    for h in range(2):
        depth = at_side(side if h == 0 else other, 2048)
        c_ffn.append(fetch(up_ref.at[depth, at_side(side, 384)], w_gu.at[h, :, 0:384], 4 + h))
        c_ffn.append(fetch(up_ref.at[depth, at_side(side + 2, 384)], w_gu.at[h, :, 384:768], 6 + h))
        c_ffn.append(fetch(down_ref.at[at_side(side if h == 0 else other, 384), at_side(side, 2048)], wd.at[h], 8 + h))
    ra.step1()
    rb.step1()
    tell.step1()
    ra.step2()
    rb.step2()
    tell.step2()
    ring_w.forward()
    ra.step3()
    rb.step3()
    tell.step3()
    tell.finish()
    experts = [moved(g, ca, sa, i) for i in range(4)]
    pick0, weigh0 = routing(info, order0, experts)
    pick1, weigh1 = routing(info, order1, experts)
    ra.finish()
    rb.finish()
    c_w.wait()
    ring_w.finish()
    p0 = lax.dot_general(g0[...].reshape(256, 2048), w_buf[:, :, 0:2048].reshape(256, 2048), NT,
                         preferred_element_type=F32)
    p1 = lax.dot_general(g1[...].reshape(256, 2048), w_buf[:, :, 2048:4096].reshape(256, 2048), NT,
                         preferred_element_type=F32)
    mine = cb * 4 + cx
    sent = []
    for n in sorted(range(16), key=lambda n: -((0, 1, 2, 1)[n // 4] + (0, 1, 2, 1)[n % 4])):
        bi, xi = n // 4, n % 4
        u = (xi * 4 + bi) * S
        block = (p0[u:u + S, :] + p1[n * S:(n + 1) * S, :]).astype(BF)
        o_st[n] = block
        if n == 0:
            r_buf[side, mine] = block
        to = moved(moved(g, cb, sb, -bi), cx, 1, -xi)
        for e in range(2):
            if n == 0 and e == 0:
                continue
            copy = pltpu.make_async_remote_copy(
                src_ref=o_st.at[n], dst_ref=r_buf.at[side, mine], send_sem=os.at[n, e], recv_sem=orv.at[side, mine],
                device_id=(side if e == 0 else other, to), device_id_type=MESH)
            copy.start()
            sent.append(copy)

    def arrived(source_side, n):
        pltpu.make_async_remote_copy(
            src_ref=o_st.at[0], dst_ref=r_buf.at[source_side, n], send_sem=os.at[0, 0], recv_sem=orv.at[source_side, n],
            device_id=(side, ap), device_id_type=MESH).wait_recv()

    for i in range(4):
        for j in range(4):
            if i or j:
                arrived(side, lax.rem(cb + i, 4) * 4 + lax.rem(cx + j, 4))
            arrived(other, lax.rem(ca + i, 4) * 4 + lax.rem(cx + j, 4))
    squares = jnp.zeros((S, 128), F32)
    for y in range(4):
        for z in range(4):
            for m in range(2):
                pieces = []
                for x in (2 * m, 2 * m + 1):
                    pieces.append(r_buf[0, z * 4 + x, :, y * 64:(y + 1) * 64].astype(F32)
                                  + r_buf[1, y * 4 + x, :, z * 64:(z + 1) * 64].astype(F32))
                at = (y * 8 + z * 2 + m) * 128
                tile = res_ref[:, at:at + 128].astype(F32) + jnp.concatenate(pieces, axis=1)
                hid[:, at:at + 128] = tile
                squares = squares + tile * tile
    scaling = lax.rsqrt(jnp.sum(squares, axis=1, keepdims=True) * (1.0 / D) + 1e-06)

    def columns(r):
        return pl.ds(pl.multiple_of(side * 2048 + r * 1024, 128), 1024)

    na = Gather(links, side, b_way, x_way, n0)
    nb = Gather(links, side, x_way, b_way, n1)
    n0[0, 0] = (hid[:, columns(0)] * scaling * gain_ref[:, columns(0)]).astype(BF)
    na.start()
    n1[0, 0] = (hid[:, columns(1)] * scaling * gain_ref[:, columns(1)]).astype(BF)
    nb.start()
    na.step1()
    nb.step1()
    na.step2()
    nb.step2()
    na.step3()
    nb.step3()

    def part(r):
        return slice(r * 1024, (r + 1) * 1024)

    def via_out(r, c):
        at = slice(2 * c, 2 * c + 2)
        return links.push(x_st.at[1, at, :, part(r)], x_via.at[r, at], side, (ap, am)[r])

    def via_on(r, c):
        at = slice(2 * c, 2 * c + 2)
        return links.push(x_via.at[r, at], x_own.at[2, at, :, part(r)], side, (ap, am)[r])

    vias, direct = [], {1: [], 3: []}
    for r, ring, n_buf, pick in ((0, na, n0, pick0), (1, nb, n1, pick1)):
        ring.finish()
        rows = jnp.dot(pick, n_buf[...].reshape(256, 1024), preferred_element_type=F32).astype(BF)
        rows = rows.reshape(4, 4, S, 1024)
        x_st[:, :, :, part(r)] = rows[1:]
        x_own[0, :, :, part(r)] = rows[0]
        vias += [(r, c, via_out(r, c)) for c in range(2)]
        direct[1].append(links.push(x_st.at[0, :, :, part(r)], x_own.at[1, :, :, part(r)], side, ap))
        direct[3].append(links.push(x_st.at[2, :, :, part(r)], x_own.at[3, :, :, part(r)], side, am))

    def swap(i):
        return links.push(x_own.at[i], x_far.at[i], other, g)

    def front(src, dst, h, i):
        rows = src[i].reshape(64, 2048)
        dst[i] = jnp.dot(rows, w_gu[h], preferred_element_type=F32).reshape(4, S, 768)

    swaps = {0: swap(0)}
    for copy in c_ffn:
        copy.wait()
    front(x_own, h_own, 0, 0)
    ons = []
    for r, c, copy in vias:
        copy.wait_recv()
        ons.append(via_on(r, c))
    for i in (1, 3):
        for copy in direct[i]:
            copy.wait_recv()
        swaps[i] = swap(i)
    front(x_own, h_own, 0, 1)
    front(x_own, h_own, 0, 3)
    for i in (0, 1, 3):
        swaps[i].wait_recv()
        front(x_far, h_far, 1, i)
    for copy in ons:
        copy.wait_recv()
    swaps[2] = swap(2)
    front(x_own, h_own, 0, 2)
    swaps[2].wait_recv()
    front(x_far, h_far, 1, 2)
    swaps = []
    for i in range(4):
        both = h_own[i] + h_far[:, i]
        gate, up = both[:, :, 0:384], both[:, :, 384:768]
        a_own[i] = (gate / (1.0 + jnp.exp(-gate)) * up).astype(BF)
        swaps.append(links.push(a_own.at[i], a_far.at[:, i], other, g))
    near2 = jnp.dot(a_own[2].reshape(64, 384), wd[0], preferred_element_type=F32)
    for copy in swaps:
        copy.wait_recv()
    y_st[1] = (near2 + jnp.dot(a_far[2].reshape(64, 384), wd[1], preferred_element_type=F32)).astype(BF)
    vias = []
    for r in range(2):
        for c in range(2):
            at = slice(32 * c, 32 * c + 32)
            vias.append((r, at, links.push(y_st.at[1, at, part(r)], z_via.at[r, at], side, (ap, am)[r])))
    back = []
    for i in (1, 3, 0):
        rows = (jnp.dot(a_own[i].reshape(64, 384), wd[0], preferred_element_type=F32)
                + jnp.dot(a_far[i].reshape(64, 384), wd[1], preferred_element_type=F32)).astype(BF)
        if i == 0:
            z_buf[0] = rows
        else:
            y_st[i - 1] = rows
            back.append(links.push(y_st.at[i - 1], z_buf.at[i], side, am if i == 1 else ap))
    for r, at, copy in vias:
        copy.wait_recv()
        back.append(links.push(z_via.at[r, at], z_buf.at[2, at, part(r)], side, (ap, am)[r]))
    for copy in back:
        copy.wait_recv()

    def mix(weigh, r):
        high = weigh.astype(BF)
        low = (weigh - high.astype(F32)).astype(BF)
        both = jnp.concatenate([high, low], axis=1)
        both = lax.dot_general(both, z_buf[:, :, part(r)].reshape(256, 1024), (((0,), (0,)), ((), ())),
                               preferred_element_type=F32)
        return (both[0:256, :] + both[256:512, :]).reshape(4, 4, S, 1024)

    sc = Scatter(links, side, b_way, x_way, m0, far0, over0, near0, {})
    sd = Scatter(links, side, x_way, b_way, m1, far1, over1, near1, {})
    m0[...] = mix(weigh0, 0)
    sc.start()
    m1[...] = mix(weigh1, 1)
    sd.start()
    sc.forward()
    sd.forward()
    sc.turn((2, 1, 3, 0))
    sd.turn((2, 1, 3, 0))
    for r, ring in ((0, sc), (1, sd)):
        out_ref[:, part(r)] = hid[:, columns(r)] + ring.result()
    links.drain()
    for copy in sent:
        copy.wait_send()


def body(q, k, v, lens, out_weight, residual, norm_gain, expert_ids, route_weights, gate_up, down_weight):
    vm = pl.BlockSpec(memory_space=pltpu.VMEM)
    hb = pl.BlockSpec(memory_space=pltpu.HBM)
    sm = pl.BlockSpec(memory_space=pltpu.SMEM)
    dma = pltpu.SemaphoreType.DMA

    def vb(*shape):
        return pltpu.VMEM(shape, BF)

    def vf(*shape):
        return pltpu.VMEM(shape, F32)

    return pl.pallas_call(
        kernel,
        out_shape=jax.ShapeDtypeStruct((S, D // 2), F32),
        in_specs=[hb, hb, hb, sm, hb, vm, vm, vm, vm, hb, hb],
        out_specs=vm,
        scratch_shapes=[
            vb(S, 4096), vb(S, CTX, 256), vb(S, CTX, 256), vb(4, 64, 4096), vb(4, 4, S, 2048), vb(4, 4, S, 2048),
            vb(16, S, 256), vb(2, 16, S, 256), vf(S, D), vf(4, 4, 16, 128), vb(4, 4, S, 1024), vb(4, 4, S, 1024),
            vb(3, 4, S, 2048), vb(4, 4, S, 2048), vb(4, 4, S, 2048), vb(2, 4, S, 1024),
            vb(2, 2048, 768), vb(2, 384, 2048), vf(4, 4, S, 768), vf(4, 4, S, 768), vb(4, 4, S, 384), vb(4, 4, S, 384),
            vb(3, 64, 2048), vb(4, 64, 2048), vb(2, 64, 1024), vf(4, 4, S, 1024), vf(4, 4, S, 1024),
            vb(2, 4, S, 1024), vb(2, 2, 4, S, 1024), vb(2, 4, S, 1024),
            vb(2, 4, S, 1024), vb(2, 2, 4, S, 1024), vb(2, 4, S, 1024),
            dma((10,)), dma((160,)), dma((160,)), dma((16, 2)), dma((2, 16)),
        ],
        compiler_params=pltpu.CompilerParams(collective_id=0, has_side_effects=True, vmem_limit_bytes=60 << 20),
        name="decode_layer",
    )(q, k, v, lens, out_weight.T, residual, norm_gain.reshape(1, -1), expert_ids.T, route_weights.T,
      gate_up[0], down_weight[0]).astype(BF)


def solution(mesh):
    return jax.shard_map(
        body,
        mesh=mesh,
        in_specs=(
            P("grp", None), P("grp", None, None), P("grp", None, None), P("grp"), P(None, "grp"), P("grp", None), P(),
            P("grp", None), P("grp", None), P("grp", None, None), P("grp", None, None),
        ),
        out_specs=P("grp", "side"),
        check_vma=False,
    )
```

time: 99.4 us -> 88.2 us (0.89)
  Pallas kernels: 97.7 us -> 86.3 us
  other arithmetic: 0 us -> 1.54 us
  local copies, waits for them, and re-layouts: 1.47 us -> 0 us
    pallas_call x1, Pallas kernels: 97.7 us -> 86.3 us  [body(): pl.pallas_call(kernel, out_shape=jax.ShapeDtypeStruct((S, D // 2), F32),...]
    convert_element_type x0 -> x1, other arithmetic: none -> 1.54 us  [body(): return pl.pallas_call(kernel, out_shape=jax.ShapeDtypeStruct((S, D // 2),...]
    unnamed x1 -> x0, local copies, waits for them, and re-layouts: 1.47 us -> none
where the time goes in v3:
time: 88.2 us; the launch traced here: 87.9 us
  Pallas kernels  86.3 us (98%)
  other arithmetic  1.54 us (2%)
    pallas_call x1, Pallas kernels, body(): pl.pallas_call(kernel, out_shape=jax.ShapeDtypeStruct((S, D // 2), F32),...  86.3 us

profile of v3, /device:TPU:0, one launch (start us, length us, event | category | flops | bytes accessed | tf_op | source)
XLA Modules:
  0.0 87.9 jit_solution(6308071267736994757)
XLA Ops:
  0.0 86.3 %decode_layer.1 = f32[16,2048]{1,0:T(8,128)} custom-call(bf16[16,8192]{1,0:T(8,128)(2,1)} %q_ref.1, bf16[16,128,512]{2,1,0:T(8,128)(2,1)} %k_ref.1, bf16[16,128,512]{2,1,0:T(8,128)(2,1)} %v_ref.1, s32[16]{0:T(128)} %lens_ref.1, bf16[64,8192]{1,0:T(8,128)(2,1)} %bitcast.8, bf16[16,4096]{1,0:T(8,128)(2,1)} %res_ref.1, f32[1,4096]{1,0:T(1,128)} %bitcast.9, ...), custom_call_target="tpu_custom_call" | custom-call | tf_op jit(solution)/shard_map/decode_layer/pallas_call | solution.py:517
  86.4 1.5 %convert_element_type.3 = bf16[16,2048]{1,0:T(8,128)(2,1)} convert(f32[16,2048]{1,0:T(8,128)} %decode_layer.1) | non-fusion elementwise | flops 32768 | bytes 196608 | tf_op jit(solution)/shard_map/convert_element_type | solution.py:535

commit v4 on v3

v4 whole, which is shorter than its diff:
```python
import jax
import jax.numpy as jnp
from jax import lax
from jax.experimental import pallas as pl
from jax.experimental.pallas import tpu as pltpu
from jax.sharding import PartitionSpec as P

HQ = 64
KVH = 4
HD = 128
HID = 768
TOPK = 8
CTX = 128
D = 4096
S = 16
MESH = pl.DeviceIdType.MESH
BF = jnp.bfloat16
F32 = jnp.float32
NT = (((1,), (1,)), ((), ()))


def place():
    side = lax.axis_index("side")
    g = lax.axis_index("grp")
    sa = 16 - 12 * side
    sb = 4 + 12 * side
    ca = lax.rem(g // sa, 4)
    cb = lax.rem(g // sb, 4)
    cx = lax.rem(g, 4)
    return side, g, sa, sb, ca, cb, cx


def moved(g, c, stride, by):
    return g + (lax.rem(c + by + 4, 4) - c) * stride


def attend(q_buf, k_buf, v_buf, lens_ref, kv):
    lane = lax.broadcasted_iota(jnp.int32, (S, CTX), 1)
    row = lax.broadcasted_iota(jnp.int32, (S, CTX), 0)
    live = jnp.zeros((S, CTX), jnp.int32)
    for s in range(S):
        live = jnp.where(row == s, lens_ref[s], live)
    group = HQ // KVH
    live = jnp.concatenate([live] * group, axis=0)
    lane = jnp.concatenate([lane] * group, axis=0)
    row = jnp.concatenate([row] * group, axis=0)
    queries = jnp.concatenate(
        [q_buf[:, (kv * group + j) * HD:(kv * group + j + 1) * HD] for j in range(group)], axis=0)
    scores = jnp.zeros((S * group, CTX), F32)
    for s in range(S):
        part = lax.dot_general(queries, k_buf[s, :, kv * HD:(kv + 1) * HD], NT, preferred_element_type=F32)
        scores = jnp.where(row == s, part, scores)
    scores = jnp.where(lane < live, scores * HD ** (-0.5), -1e30)
    lifted = jnp.exp(scores - jnp.max(scores, axis=1, keepdims=True))
    weights = (lifted / jnp.sum(lifted, axis=1, keepdims=True))
    spread = jnp.concatenate([jnp.where(row == s, weights, 0.0).astype(BF) for s in range(S)], axis=1)
    values = v_buf[:, :, kv * HD:(kv + 1) * HD].reshape(S * CTX, HD)
    return jnp.dot(spread, values, preferred_element_type=F32).astype(BF)


class Links:
    def __init__(self, sends, recvs):
        self.sends, self.recvs, self.used, self.open = sends, recvs, 0, []

    def make(self, src, dst, to_side, to):
        i = self.used
        self.used += 1
        copy = pltpu.make_async_remote_copy(
            src_ref=src, dst_ref=dst, send_sem=self.sends.at[i], recv_sem=self.recvs.at[i],
            device_id=(to_side, to), device_id_type=MESH)
        self.open.append(copy)
        return copy

    def push(self, src, dst, to_side, to):
        copy = self.make(src, dst, to_side, to)
        copy.start()
        return copy

    def drain(self):
        for copy in self.open:
            copy.wait_send()


class Columns:
    def __init__(self, links, side, plus, minus, own, slot):
        self.links, self.side, self.plus, self.minus, self.own, self.slot = links, side, plus, minus, own, slot

    def start(self):
        low, high = slice(0, 32), slice(32, 64)
        push, own, slot = self.links.push, self.own, self.slot(0)
        self.c0 = push(own.at[low], slot.at[low], self.side, self.plus)
        self.c1 = push(own.at[high], slot.at[high], self.side, self.minus)
        self.rest = [push(own.at[high], slot.at[high], self.side, self.plus),
                     push(own.at[low], slot.at[low], self.side, self.minus)]

    def forward(self):
        self.c0.wait_recv()
        at = self.slot(1).at[0:32]
        self.rest.append(self.links.push(at, at, self.side, self.plus))
        self.c1.wait_recv()
        at = self.slot(3).at[32:64]
        self.rest.append(self.links.push(at, at, self.side, self.minus))

    def finish(self):
        for copy in self.rest:
            copy.wait_recv()


class Gather:
    def __init__(self, links, side, p, q, buf, half=None):
        self.links, self.side, self.p, self.q, self.buf, self.half = links, side, p, q, buf, half
        self.got = {}

    def send(self, i, j, to, di, dj, view=None):
        src, dst = self.buf.at[i, j], self.buf.at[(i + di) % 4, (j + dj) % 4]
        if view is not None:
            src, dst = self.half(src, view), self.half(dst, view)
        self.got[(i + di) % 4, (j + dj) % 4, view] = self.links.push(src, dst, self.side, to)

    def wait(self, i, j, view=None):
        self.got.pop((i, j, view)).wait_recv()

    def along_q(self, j):
        self.send(0, j, self.q[0], 1, 0)
        self.send(0, j, self.q[1], 3, 0)

    def start(self):
        self.send(0, 0, self.p[0], 0, 1)
        self.send(0, 0, self.p[1], 0, 3)
        if self.half is None:
            self.send(0, 0, self.p[2], 0, 2)
        self.along_q(0)

    def step1(self):
        self.wait(0, 1)
        if self.half is not None:
            self.send(0, 1, self.p[0], 0, 1, 0)
        self.along_q(1)
        self.wait(0, 3)
        if self.half is not None:
            self.send(0, 3, self.p[1], 0, 3, 1)
        self.along_q(3)
        self.wait(1, 0)
        self.send(1, 0, self.q[0], 1, 0)

    def step2(self):
        if self.half is None:
            self.wait(0, 2)
        else:
            self.wait(0, 2, 0)
            self.wait(0, 2, 1)
        self.along_q(2)

    def step3(self):
        self.wait(1, 1)
        self.send(1, 1, self.q[0], 1, 0)
        self.wait(3, 3)
        self.send(3, 3, self.q[1], 3, 0)
        self.wait(3, 2)
        self.send(3, 2, self.q[1], 3, 0)

    def finish(self):
        for key in list(self.got):
            self.wait(*key)


class Scatter:
    def __init__(self, links, side, p, q, m, far, over, near):
        self.links, self.side, self.p, self.q, self.m = links, side, p, q, m
        self.far, self.over, self.near = far, over, near
        self.c_far, self.c_over, self.c_near = {}, {}, {}

    def start_far(self):
        for j in (2, 1, 3, 0):
            self.far[0, j] = self.m[2, j].astype(BF)
            self.c_far[j] = self.links.push(self.far.at[0, j], self.far.at[1, j], self.side, self.q[0 if j < 2 else 1])

    def send_over(self, way, j, extra):
        block = self.m[3 if way == 0 else 1, j]
        if extra:
            self.c_far[j].wait_recv()
            block = block + self.far[1, j].astype(F32)
        self.over[0, way, j] = block.astype(BF)
        self.c_over[way, j] = self.links.push(
            self.over.at[0, way, j], self.over.at[1, way, j], self.side, self.q[way])

    def start_over(self):
        for j in (2, 1, 3, 0):
            self.send_over(0 if j >= 2 else 1, j, False)

    def forward(self):
        for j in (2, 1, 3, 0):
            self.send_over(0 if j < 2 else 1, j, True)

    def turn(self):
        for j in (2, 1, 3, 0):
            self.c_over[0, j].wait_recv()
            self.c_over[1, j].wait_recv()
            block = self.m[0, j] + self.over[1, 0, j].astype(F32) + self.over[1, 1, j].astype(F32)
            if j == 0:
                self.own = block
            else:
                self.near[0, j] = block.astype(BF)
                self.c_near[j] = self.links.push(
                    self.near.at[0, j], self.near.at[1, j], self.side, self.p[(None, 1, 2, 0)[j]])

    def result(self):
        block = self.own
        for j in (1, 3, 2):
            self.c_near[j].wait_recv()
            block = block + self.near[1, j].astype(F32)
        return block


def routing(info, experts):
    lane = lax.broadcasted_iota(jnp.int32, (16, 128), 1)
    tiles = []
    for t in range(2):
        tile = jnp.zeros((16, 128), F32)
        for i in range(8):
            b, x = divmod(t * 8 + i, 4)
            block = info[x, b]
            moved_block = pltpu.roll(block, 16 * i, 1) if i else block
            tile = jnp.where(lane // 16 == i, moved_block, tile)
        tiles.append(tile)
    table = jnp.concatenate(tiles, axis=1)
    ids, route = table[0:8, :], table[8:16, :]
    first = lax.broadcasted_iota(jnp.int32, (256, 256), 0)
    later = lax.broadcasted_iota(jnp.int32, (256, 256), 1)
    before = jnp.where((first // 16 == later // 16) & (first < later), 1.0, 0.0).astype(BF)
    token = lax.broadcasted_iota(jnp.int32, (8, 256), 1) // 16
    named, weight = [], []
    for e in experts:
        hit = ids == e.astype(F32)
        named.append(jnp.sum(jnp.where(hit, 1.0, 0.0), axis=0, keepdims=True))
        weight.append(jnp.sum(jnp.where(hit, route, 0.0), axis=0, keepdims=True))
    named8 = jnp.concatenate(named + [jnp.zeros((4, 256), F32)], axis=0)
    rank = jnp.dot(named8.astype(BF), before, preferred_element_type=F32)
    spot = jnp.where(named8 > 0.5, (token % 4).astype(F32) * 4.0 + rank, -1.0)
    rows = lax.broadcasted_iota(jnp.int32, (16, 256), 0).astype(F32)
    picks, weighted = [], []
    for i in range(4):
        hit = rows == spot[i:i + 1, :]
        picks.append(jnp.where(hit, 1.0, 0.0))
        weighted.append(jnp.where(hit, weight[i], 0.0))
    picks, weighted = jnp.concatenate(picks, axis=0), jnp.concatenate(weighted, axis=0)
    pick, weigh = [], []
    for b in range(4):
        at = slice(64 * b, 64 * b + 64)
        pick.append(picks[:, at].astype(BF))
        high = weighted[:, at].astype(BF)
        weigh.append(jnp.concatenate([high, (weighted[:, at] - high.astype(F32)).astype(BF)], axis=1))
    return pick, weigh


SLOT = (0, 1, 3, 2)
HEADS0 = 20


def kernel(q_ref, k_ref, v_ref, lens_ref, wt_ref, res_ref, gain_ref, ids_ref, route_ref, up_ref, down_ref, out_ref,
           q_buf, k_buf, v_buf, w_buf, g0, g1, o_st, r_buf, hid, info, n_buf, x_st, x_own, x_far, x_via,
           w_gu, wd, h_own, h_far, a_own, a_far, d_near, y_st, z_buf, z_via, m_buf, far, over, near,
           res_buf, gain_buf, ids_buf, route_buf, lens_buf, loc, sends, recvs, os, orv):
    side, g, sa, sb, ca, cb, cx = place()
    other = 1 - side
    ap, am = moved(g, ca, sa, 1), moved(g, ca, sa, -1)
    b_way = [moved(g, cb, sb, i) for i in (1, -1, 2)]
    x_way = [moved(g, cx, 1, i) for i in (1, -1, 2)]
    links = Links(sends, recvs)
    barrier = pltpu.get_barrier_semaphore()

    def hello(to_side, to):
        pl.semaphore_signal(barrier, inc=1, device_id=(to_side, to), device_id_type=MESH)

    hello(side, ap)
    hello(side, am)
    for i in range(4):
        for j in range(4):
            if i or j:
                hello(side, moved(moved(g, cb, sb, i), cx, 1, j))
            hello(other, moved(moved(g, ca, sa, i), cx, 1, j))

    def fetch(src, dst, i):
        copy = pltpu.make_async_copy(src, dst, loc.at[i])
        copy.start()
        return copy

    def at_side(base, size):
        return pl.ds(pl.multiple_of(base * size, 128), size)

    c_lens = fetch(lens_ref, lens_buf, 14)
    c_q = fetch(q_ref.at[:, at_side(side, 4096)], q_buf, 0)
    c_k = fetch(k_ref.at[:, :, at_side(side, 256)], k_buf, 1)
    c_v = fetch(v_ref.at[:, :, at_side(side, 256)], v_buf, 2)
    w_own = wt_ref.at[:, at_side(side, 4096)]
    c_w = fetch(w_own, w_buf.at[ca], 3)
    c_ids = fetch(ids_ref, ids_buf, 10)
    c_route = fetch(route_ref, route_buf, 11)
    info[0, 0] = jnp.zeros((16, 128), F32)
    c_lens.wait()
    c_q.wait()
    c_k.wait()
    c_v.wait()
    group = HQ // KVH
    for kv in range(2):
        result = attend(q_buf, k_buf, v_buf, lens_buf, kv)
        for j in range(group):
            n = kv * group + j
            out, n = (g0, n) if n < HEADS0 else (g1, n - HEADS0)
            out[0, 0, :, n * HD:(n + 1) * HD] = result[j * S:(j + 1) * S, :]
    c_ids.wait()
    c_route.wait()
    info[0, 0, 0:8, 0:16] = ids_buf[...].astype(F32)
    info[0, 0, 8:16, 0:16] = route_buf[...]
    pl.semaphore_wait(barrier, 33)
    ring_w = Columns(links, side, ap, am, w_own, lambda source: w_buf.at[lax.rem(ca - source + 4, 4)])
    tell = Gather(links, side, b_way, x_way, info)

    def cut(size):
        return lambda ref, h: ref.at[:, h * size:(h + 1) * size]

    split = HEADS0 * HD
    ra = Gather(links, side, b_way, x_way, g0, cut(split // 2))
    rb = Gather(links, side, x_way, b_way, g1, cut((4096 - split) // 2))
    ra.start()
    rb.start()
    tell.start()
    ring_w.start()
    c_res = fetch(res_ref, res_buf, 12)
    c_gain = fetch(gain_ref, gain_buf, 13)
    c_ffn = []
    for h in range(2):
        depth = at_side(side if h == 0 else other, 2048)
        c_ffn.append(fetch(up_ref.at[depth, at_side(side, 384)], w_gu.at[h, :, 0:384], 4 + h))
        c_ffn.append(fetch(up_ref.at[depth, at_side(side + 2, 384)], w_gu.at[h, :, 384:768], 6 + h))
        c_ffn.append(fetch(down_ref.at[at_side(side if h == 0 else other, 384), at_side(side, 2048)], wd.at[h], 8 + h))
    ra.step1()
    rb.step1()
    tell.step1()
    ra.step2()
    rb.step2()
    tell.step2()
    ring_w.forward()
    ra.step3()
    rb.step3()
    tell.step3()
    tell.finish()
    experts = [moved(g, ca, sa, i) for i in range(4)]
    pick, weigh = routing(info, experts)
    ra.finish()
    rb.finish()
    c_w.wait()
    ring_w.finish()
    p0 = lax.dot_general(g0[...].reshape(256, split), w_buf[:, :, 0:split].reshape(256, split), NT,
                         preferred_element_type=F32)
    p1 = lax.dot_general(g1[...].reshape(256, 4096 - split), w_buf[:, :, split:4096].reshape(256, 4096 - split), NT,
                         preferred_element_type=F32)
    mine = cb * 4 + cx
    sent = []
    for n in sorted(range(16), key=lambda n: -((0, 1, 2, 1)[n // 4] + (0, 1, 2, 1)[n % 4])):
        bi, xi = n // 4, n % 4
        u = (xi * 4 + bi) * S
        block = (p0[u:u + S, :] + p1[n * S:(n + 1) * S, :]).astype(BF)
        o_st[n] = block
        if n == 0:
            r_buf[side, mine] = block
        to = moved(moved(g, cb, sb, -bi), cx, 1, -xi)
        for e in range(2):
            if n == 0 and e == 0:
                continue
            copy = pltpu.make_async_remote_copy(
                src_ref=o_st.at[n], dst_ref=r_buf.at[side, mine], send_sem=os.at[n, e], recv_sem=orv.at[side, mine],
                device_id=(side if e == 0 else other, to), device_id_type=MESH)
            copy.start()
            sent.append(copy)

    def arrived(source_side, n):
        pltpu.make_async_remote_copy(
            src_ref=o_st.at[0], dst_ref=r_buf.at[source_side, n], send_sem=os.at[0, 0], recv_sem=orv.at[source_side, n],
            device_id=(side, ap), device_id_type=MESH).wait_recv()

    for i in range(4):
        for j in range(4):
            if i or j:
                arrived(side, lax.rem(cb + i, 4) * 4 + lax.rem(cx + j, 4))
            arrived(other, lax.rem(ca + i, 4) * 4 + lax.rem(cx + j, 4))
    c_res.wait()
    c_gain.wait()
    squares = jnp.zeros((S, 128), F32)
    for y in range(4):
        for z in range(4):
            for m in range(2):
                pieces = []
                for x in (2 * m, 2 * m + 1):
                    pieces.append(r_buf[0, z * 4 + x, :, y * 64:(y + 1) * 64].astype(F32)
                                  + r_buf[1, y * 4 + x, :, z * 64:(z + 1) * 64].astype(F32))
                at = (y * 8 + z * 2 + m) * 128
                tile = res_buf[:, at:at + 128].astype(F32) + jnp.concatenate(pieces, axis=1)
                hid[:, at:at + 128] = tile
                squares = squares + tile * tile
    scaling = lax.rsqrt(jnp.sum(squares, axis=1, keepdims=True) * (1.0 / D) + 1e-06)

    half_at = pl.ds(pl.multiple_of(side * 2048, 128), 2048)
    na = Gather(links, side, x_way, b_way, n_buf, cut(1024))
    n_buf[0, 0] = (hid[:, half_at] * scaling * gain_buf[:, half_at]).astype(BF)
    na.start()

    def part(r):
        return slice(r * 1024, (r + 1) * 1024)

    a_way = (ap, am)
    c_via, c_on, c_one, c_swap = {}, {}, {}, {}

    def dispatch(b):
        rows = jnp.dot(pick[b], n_buf[b].reshape(64, 2048), preferred_element_type=F32).astype(BF)
        rows = rows.reshape(4, S, 2048)
        at = SLOT[b]
        x_st[at] = rows[1:]
        x_own[at, 0] = rows[0]
        for r in range(2):
            c_via[b, r] = links.push(x_st.at[at, 1, :, part(r)], x_via.at[r, at], side, a_way[r])
        c_one[b] = [links.push(x_st.at[at, 0], x_own.at[at, SLOT[1]], side, ap),
                    links.push(x_st.at[at, 2], x_own.at[at, SLOT[3]], side, am)]

    def pass_on(b):
        at = SLOT[b]
        for r in range(2):
            c_via[b, r].wait_recv()
            c_on[b, r] = links.push(x_via.at[r, at], x_own.at[at, SLOT[2], :, part(r)], side, a_way[r])

    def swap_three(b):
        at = SLOT[b]
        for copy in c_one[b]:
            copy.wait_recv()
        c_swap[b, 0] = links.push(x_own.at[at, 0:3], x_far.at[at, 0:3], other, g)

    def swap_last(b):
        at = SLOT[b]
        for r in range(2):
            c_on[b, r].wait_recv()
        c_swap[b, 1] = links.push(x_own.at[at, 3], x_far.at[at, 3], other, g)

    def front(src, dst, h, low, high):
        rows = src[low:high].reshape((high - low) * 64, 2048)
        dst[low:high] = jnp.dot(rows, w_gu[h], preferred_element_type=F32).reshape(high - low, 4, S, 768)

    na.step1()
    na.step2()
    dispatch(0)
    na.step3()
    na.wait(1, 2)
    na.wait(1, 3)
    dispatch(1)
    na.wait(3, 0)
    na.wait(3, 1)
    dispatch(3)
    pass_on(0)
    na.finish()
    dispatch(2)
    pass_on(1)
    pass_on(3)
    for b in (0, 1, 3):
        swap_three(b)
    pass_on(2)
    for b in (0, 1, 3):
        swap_last(b)
    for copy in c_ffn:
        copy.wait()
    front(x_own, h_own, 0, 0, 3)
    swap_three(2)
    for b in (0, 1, 3):
        c_swap[b, 0].wait_recv()
        c_swap[b, 1].wait_recv()
    front(x_far, h_far, 1, 0, 3)
    swap_last(2)
    front(x_own, h_own, 0, 3, 4)
    c_swap[2, 0].wait_recv()
    c_swap[2, 1].wait_recv()
    front(x_far, h_far, 1, 3, 4)
    swaps = []
    for i in range(4):
        both = h_own[i] + h_far[:, i]
        gate, up = both[:, :, 0:384], both[:, :, 384:768]
        a_own[i] = (gate / (1.0 + jnp.exp(-gate)) * up).astype(BF)
        swaps.append(links.push(a_own.at[i], a_far.at[:, i], other, g))
    d_near[...] = jnp.dot(a_own[...].reshape(256, 384), wd[0], preferred_element_type=F32).reshape(4, 64, 2048)
    for copy in swaps:
        copy.wait_recv()
    c_via, c_on, c_back = {}, {}, {}
    for b in (2, 1, 3, 0):
        at = SLOT[b]
        rows = d_near[at] + jnp.dot(a_far[at].reshape(64, 384), wd[1], preferred_element_type=F32)
        rows = rows.astype(BF).reshape(4, S, 2048)
        for a in (2, 1, 3):
            y_st[b, a - 1] = rows[SLOT[a]]
        z_buf[b, 0] = rows[0]
        for r in range(2):
            c_via[b, r] = links.push(y_st.at[b, 1, :, part(r)], z_via.at[r, b], side, a_way[r])
        c_back[b] = [links.push(y_st.at[b, 0], z_buf.at[b, 1], side, am),
                     links.push(y_st.at[b, 2], z_buf.at[b, 3], side, ap)]

    def back_on(b):
        for r in range(2):
            c_via[b, r].wait_recv()
            c_back[b].append(links.push(z_via.at[r, b], z_buf.at[b, 2, :, part(r)], side, a_way[r]))

    def mix(b):
        for copy in c_back[b]:
            copy.wait_recv()
        both = lax.dot_general(weigh[b], z_buf[b].reshape(64, 2048), (((0,), (0,)), ((), ())),
                               preferred_element_type=F32)
        m_buf[b] = (both[0:64, :] + both[64:128, :]).reshape(4, S, 2048)

    ring = Scatter(links, side, x_way, b_way, m_buf, far, over, near)
    back_on(2)
    back_on(1)
    back_on(3)
    mix(2)
    ring.start_far()
    back_on(0)
    mix(1)
    mix(3)
    ring.start_over()
    ring.forward()
    mix(0)
    ring.turn()
    out_ref[...] = hid[:, half_at] + ring.result()
    links.drain()
    for copy in sent:
        copy.wait_send()


def body(q, k, v, lens, out_weight, residual, norm_gain, expert_ids, route_weights, gate_up, down_weight):
    vm = pl.BlockSpec(memory_space=pltpu.VMEM)
    hb = pl.BlockSpec(memory_space=pltpu.HBM)
    dma = pltpu.SemaphoreType.DMA

    def vb(*shape):
        return pltpu.VMEM(shape, BF)

    def vf(*shape):
        return pltpu.VMEM(shape, F32)

    return pl.pallas_call(
        kernel,
        out_shape=jax.ShapeDtypeStruct((S, D // 2), F32),
        in_specs=[hb] * 11,
        out_specs=vm,
        scratch_shapes=[
            vb(S, 4096), vb(S, CTX, 256), vb(S, CTX, 256), vb(4, 64, 4096),
            vb(4, 4, S, HEADS0 * HD), vb(4, 4, S, 4096 - HEADS0 * HD),
            vb(16, S, 256), vb(2, 16, S, 256), vf(S, D), vf(4, 4, 16, 128), vb(4, 4, S, 2048),
            vb(4, 3, S, 2048), vb(4, 4, S, 2048), vb(4, 4, S, 2048), vb(2, 4, S, 1024),
            vb(2, 2048, 768), vb(2, 384, 2048), vf(4, 4, S, 768), vf(4, 4, S, 768), vb(4, 4, S, 384), vb(4, 4, S, 384),
            vf(4, 64, 2048), vb(4, 3, S, 2048), vb(4, 4, S, 2048), vb(2, 4, S, 1024), vf(4, 4, S, 2048),
            vb(2, 4, S, 2048), vb(2, 2, 4, S, 2048), vb(2, 4, S, 2048),
            vb(S, D), vf(1, D), pltpu.VMEM((8, S), jnp.int32), vf(8, S), pltpu.SMEM((S,), jnp.int32),
            dma((15,)), dma((160,)), dma((160,)), dma((16, 2)), dma((2, 16)),
        ],
        compiler_params=pltpu.CompilerParams(collective_id=0, has_side_effects=True, vmem_limit_bytes=46 << 20),
        name="decode_layer",
    )(*[pltpu.with_memory_space_constraint(value, pltpu.HBM) for value in (
        q, k, v, lens, out_weight.T, residual, norm_gain.reshape(1, -1), expert_ids.T, route_weights.T,
        gate_up[0], down_weight[0])]).astype(BF)


def solution(mesh):
    return jax.shard_map(
        body,
        mesh=mesh,
        in_specs=(
            P("grp", None), P("grp", None, None), P("grp", None, None), P("grp"), P(None, "grp"), P("grp", None), P(),
            P("grp", None), P("grp", None), P("grp", None, None), P("grp", None, None),
        ),
        out_specs=P("grp", "side"),
        check_vma=False,
    )
```

time: 88.2 us -> 84.5 us (0.958)
  Pallas kernels: 86.3 us -> 83.7 us
  other arithmetic: 1.54 us -> 0.64 us
    pallas_call x1, Pallas kernels: 86.3 us -> 83.7 us  [body(): pl.pallas_call(kernel, out_shape=jax.ShapeDtypeStruct((S, D // 2), F32),...]
    convert_element_type x1, other arithmetic: 1.54 us -> 0.64 us  [body(): return pl.pallas_call(kernel, out_shape=jax.ShapeDtypeStruct((S, D // 2),...]
where the time goes in v4:
time: 84.5 us; the launch traced here: 84.4 us
  Pallas kernels  83.7 us (99%)
    pallas_call x1, Pallas kernels, body(): pl.pallas_call(kernel, out_shape=jax.ShapeDtypeStruct((S, D // 2), F32),...  83.7 us

profile of v4, /device:TPU:0, one launch (start us, length us, event | category | flops | bytes accessed | tf_op | source)
XLA Modules:
  0.0 84.4 jit_solution(711863011055623432)
XLA Ops:
  0.0 83.7 %decode_layer.1 = f32[16,2048]{1,0:T(8,128)S(1)} custom-call(bf16[16,8192]{1,0:T(8,128)(2,1)} %q_ref.1, bf16[16,128,512]{2,1,0:T(8,128)(2,1)} %k_ref.1, bf16[16,128,512]{2,1,0:T(8,128)(2,1)} %v_ref.1, s32[16]{0:T(128)} %lens_ref.1, bf16[64,8192]{1,0:T(8,128)(2,1)} %bitcast.8, bf16[16,4096]{1,0:T(8,128)(2,1)} %res_ref.1, f32[1,4096]{1,0:T(1,128)} %bitcast.9, ...), custom_call_target="tpu_custom_call" | custom-call | tf_op jit(solution)/shard_map/decode_layer/pallas_call | solution.py:544
  83.7 0.6 convert_element_type.3

commit v5 on v4

--- a/solution.py
+++ b/solution.py
@@ -107,48 +107,40 @@
 
 
 class Gather:
-    def __init__(self, links, side, p, q, buf, half=None):
-        self.links, self.side, self.p, self.q, self.buf, self.half = links, side, p, q, buf, half
+    def __init__(self, links, side, p, q, buf, direct):
+        self.links, self.side, self.p, self.q, self.buf, self.direct = links, side, p, q, buf, direct
         self.got = {}
 
-    def send(self, i, j, to, di, dj, view=None):
-        src, dst = self.buf.at[i, j], self.buf.at[(i + di) % 4, (j + dj) % 4]
-        if view is not None:
-            src, dst = self.half(src, view), self.half(dst, view)
-        self.got[(i + di) % 4, (j + dj) % 4, view] = self.links.push(src, dst, self.side, to)
-
-    def wait(self, i, j, view=None):
-        self.got.pop((i, j, view)).wait_recv()
+    def send(self, i, j, to, di, dj):
+        at = (i + di) % 4, (j + dj) % 4
+        self.got[at] = self.links.push(self.buf.at[i, j], self.buf.at[at], self.side, to)
+
+    def wait(self, i, j):
+        self.got.pop((i, j)).wait_recv()
 
     def along_q(self, j):
+        if self.direct:
+            self.send(0, j, self.q[2], 2, 0)
         self.send(0, j, self.q[0], 1, 0)
         self.send(0, j, self.q[1], 3, 0)
 
     def start(self):
+        self.send(0, 0, self.p[2], 0, 2)
         self.send(0, 0, self.p[0], 0, 1)
         self.send(0, 0, self.p[1], 0, 3)
-        if self.half is None:
-            self.send(0, 0, self.p[2], 0, 2)
         self.along_q(0)
 
     def step1(self):
         self.wait(0, 1)
-        if self.half is not None:
-            self.send(0, 1, self.p[0], 0, 1, 0)
         self.along_q(1)
         self.wait(0, 3)
-        if self.half is not None:
-            self.send(0, 3, self.p[1], 0, 3, 1)
         self.along_q(3)
-        self.wait(1, 0)
-        self.send(1, 0, self.q[0], 1, 0)
+        if not self.direct:
+            self.wait(1, 0)
+            self.send(1, 0, self.q[0], 1, 0)
 
     def step2(self):
-        if self.half is None:
-            self.wait(0, 2)
-        else:
-            self.wait(0, 2, 0)
-            self.wait(0, 2, 1)
+        self.wait(0, 2)
         self.along_q(2)
 
     def step3(self):
@@ -165,38 +157,22 @@
 
 
 class Scatter:
-    def __init__(self, links, side, p, q, m, far, over, near):
-        self.links, self.side, self.p, self.q, self.m = links, side, p, q, m
-        self.far, self.over, self.near = far, over, near
-        self.c_far, self.c_over, self.c_near = {}, {}, {}
-
-    def start_far(self):
+    def __init__(self, links, side, p, q, m, over, near):
+        self.links, self.side, self.p, self.q, self.m, self.over, self.near = links, side, p, q, m, over, near
+        self.c_over, self.c_near = {}, {}
+
+    def along_q(self, i):
         for j in (2, 1, 3, 0):
-            self.far[0, j] = self.m[2, j].astype(BF)
-            self.c_far[j] = self.links.push(self.far.at[0, j], self.far.at[1, j], self.side, self.q[0 if j < 2 else 1])
-
-    def send_over(self, way, j, extra):
-        block = self.m[3 if way == 0 else 1, j]
-        if extra:
-            self.c_far[j].wait_recv()
-            block = block + self.far[1, j].astype(F32)
-        self.over[0, way, j] = block.astype(BF)
-        self.c_over[way, j] = self.links.push(
-            self.over.at[0, way, j], self.over.at[1, way, j], self.side, self.q[way])
-
-    def start_over(self):
-        for j in (2, 1, 3, 0):
-            self.send_over(0 if j >= 2 else 1, j, False)
-
-    def forward(self):
-        for j in (2, 1, 3, 0):
-            self.send_over(0 if j < 2 else 1, j, True)
+            self.over[0, i - 1, j] = self.m[i, j].astype(BF)
+            self.c_over[i, j] = self.links.push(
+                self.over.at[0, i - 1, j], self.over.at[1, i - 1, j], self.side, self.q[(None, 1, 2, 0)[i]])
 
     def turn(self):
         for j in (2, 1, 3, 0):
-            self.c_over[0, j].wait_recv()
-            self.c_over[1, j].wait_recv()
-            block = self.m[0, j] + self.over[1, 0, j].astype(F32) + self.over[1, 1, j].astype(F32)
+            block = self.m[0, j]
+            for i in (2, 1, 3):
+                self.c_over[i, j].wait_recv()
+                block = block + self.over[1, i - 1, j].astype(F32)
             if j == 0:
                 self.own = block
             else:
@@ -258,12 +234,13 @@
 
 
 def kernel(q_ref, k_ref, v_ref, lens_ref, wt_ref, res_ref, gain_ref, ids_ref, route_ref, up_ref, down_ref, out_ref,
-           q_buf, k_buf, v_buf, w_buf, g0, g1, o_st, r_buf, hid, info, n_buf, x_st, x_own, x_far, x_via,
-           w_gu, wd, h_own, h_far, a_own, a_far, d_near, y_st, z_buf, z_via, m_buf, far, over, near,
+           q_buf, k_buf, v_buf, w_buf, g0, g1, o_st, r_buf, hid, info, n_buf, x_st, x_own, x_far,
+           w_gu, wd, h_own, h_far, a_own, a_far, d_near, y_st, z_buf, m_buf, over, near,
            res_buf, gain_buf, ids_buf, route_buf, lens_buf, loc, sends, recvs, os, orv):
     side, g, sa, sb, ca, cb, cx = place()
     other = 1 - side
-    ap, am = moved(g, ca, sa, 1), moved(g, ca, sa, -1)
+    a_way = [moved(g, ca, sa, i) for i in (1, -1, 2)]
+    ap, am = a_way[0], a_way[1]
     b_way = [moved(g, cb, sb, i) for i in (1, -1, 2)]
     x_way = [moved(g, cx, 1, i) for i in (1, -1, 2)]
     links = Links(sends, recvs)
@@ -272,8 +249,8 @@
     def hello(to_side, to):
         pl.semaphore_signal(barrier, inc=1, device_id=(to_side, to), device_id_type=MESH)
 
-    hello(side, ap)
-    hello(side, am)
+    for to in a_way:
+        hello(side, to)
     for i in range(4):
         for j in range(4):
             if i or j:
@@ -312,20 +289,19 @@
     c_route.wait()
     info[0, 0, 0:8, 0:16] = ids_buf[...].astype(F32)
     info[0, 0, 8:16, 0:16] = route_buf[...]
-    pl.semaphore_wait(barrier, 33)
+    pl.semaphore_wait(barrier, 34)
     ring_w = Columns(links, side, ap, am, w_own, lambda source: w_buf.at[lax.rem(ca - source + 4, 4)])
-    tell = Gather(links, side, b_way, x_way, info)
-
-    def cut(size):
-        return lambda ref, h: ref.at[:, h * size:(h + 1) * size]
-
     split = HEADS0 * HD
-    ra = Gather(links, side, b_way, x_way, g0, cut(split // 2))
-    rb = Gather(links, side, x_way, b_way, g1, cut((4096 - split) // 2))
+    ra = Gather(links, side, b_way, x_way, g0, False)
+    rb = Gather(links, side, x_way, b_way, g1, False)
+    ring_w.start()
     ra.start()
     rb.start()
-    tell.start()
-    ring_w.start()
+    told = []
+    for i in range(4):
+        for j in range(4):
+            if i or j:
+                told.append(links.push(info.at[0, 0], info.at[j, i], side, moved(moved(g, cb, sb, i), cx, 1, j)))
     c_res = fetch(res_ref, res_buf, 12)
     c_gain = fetch(gain_ref, gain_buf, 13)
     c_ffn = []
@@ -336,17 +312,11 @@
         c_ffn.append(fetch(down_ref.at[at_side(side if h == 0 else other, 384), at_side(side, 2048)], wd.at[h], 8 + h))
     ra.step1()
     rb.step1()
-    tell.step1()
     ra.step2()
     rb.step2()
-    tell.step2()
     ring_w.forward()
     ra.step3()
     rb.step3()
-    tell.step3()
-    tell.finish()
-    experts = [moved(g, ca, sa, i) for i in range(4)]
-    pick, weigh = routing(info, experts)
     ra.finish()
     rb.finish()
     c_w.wait()
@@ -379,6 +349,10 @@
             src_ref=o_st.at[0], dst_ref=r_buf.at[source_side, n], send_sem=os.at[0, 0], recv_sem=orv.at[source_side, n],
             device_id=(side, ap), device_id_type=MESH).wait_recv()
 
+    for copy in told:
+        copy.wait_recv()
+    experts = [moved(g, ca, sa, i) for i in range(4)]
+    pick, weigh = routing(info, experts)
     for i in range(4):
         for j in range(4):
             if i or j:
@@ -401,44 +375,24 @@
     scaling = lax.rsqrt(jnp.sum(squares, axis=1, keepdims=True) * (1.0 / D) + 1e-06)
 
     half_at = pl.ds(pl.multiple_of(side * 2048, 128), 2048)
-    na = Gather(links, side, x_way, b_way, n_buf, cut(1024))
+    na = Gather(links, side, x_way, b_way, n_buf, True)
     n_buf[0, 0] = (hid[:, half_at] * scaling * gain_buf[:, half_at]).astype(BF)
     na.start()
 
-    def part(r):
-        return slice(r * 1024, (r + 1) * 1024)
-
-    a_way = (ap, am)
-    c_via, c_on, c_one, c_swap = {}, {}, {}, {}
+    c_one, c_swap = {}, {}
 
     def dispatch(b):
         rows = jnp.dot(pick[b], n_buf[b].reshape(64, 2048), preferred_element_type=F32).astype(BF)
         rows = rows.reshape(4, S, 2048)
-        at = SLOT[b]
-        x_st[at] = rows[1:]
-        x_own[at, 0] = rows[0]
-        for r in range(2):
-            c_via[b, r] = links.push(x_st.at[at, 1, :, part(r)], x_via.at[r, at], side, a_way[r])
-        c_one[b] = [links.push(x_st.at[at, 0], x_own.at[at, SLOT[1]], side, ap),
-                    links.push(x_st.at[at, 2], x_own.at[at, SLOT[3]], side, am)]
-
-    def pass_on(b):
-        at = SLOT[b]
-        for r in range(2):
-            c_via[b, r].wait_recv()
-            c_on[b, r] = links.push(x_via.at[r, at], x_own.at[at, SLOT[2], :, part(r)], side, a_way[r])
-
-    def swap_three(b):
-        at = SLOT[b]
+        x_st[b] = rows[1:]
+        x_own[SLOT[b], 0] = rows[0]
+        c_one[b] = [links.push(x_st.at[b, a - 1], x_own.at[SLOT[b], SLOT[a]], side, a_way[(None, 0, 2, 1)[a]])
+                    for a in (2, 1, 3)]
+
+    def swap(b):
         for copy in c_one[b]:
             copy.wait_recv()
-        c_swap[b, 0] = links.push(x_own.at[at, 0:3], x_far.at[at, 0:3], other, g)
-
-    def swap_last(b):
-        at = SLOT[b]
-        for r in range(2):
-            c_on[b, r].wait_recv()
-        c_swap[b, 1] = links.push(x_own.at[at, 3], x_far.at[at, 3], other, g)
+        c_swap[b] = links.push(x_own.at[SLOT[b]], x_far.at[SLOT[b]], other, g)
 
     def front(src, dst, h, low, high):
         rows = src[low:high].reshape((high - low) * 64, 2048)
@@ -447,35 +401,26 @@
     na.step1()
     na.step2()
     dispatch(0)
-    na.step3()
-    na.wait(1, 2)
-    na.wait(1, 3)
+    for j in range(4):
+        na.wait(1, j)
     dispatch(1)
-    na.wait(3, 0)
-    na.wait(3, 1)
+    for j in range(4):
+        na.wait(3, j)
     dispatch(3)
-    pass_on(0)
     na.finish()
     dispatch(2)
-    pass_on(1)
-    pass_on(3)
-    for b in (0, 1, 3):
-        swap_three(b)
-    pass_on(2)
-    for b in (0, 1, 3):
-        swap_last(b)
     for copy in c_ffn:
         copy.wait()
+    swap(0)
+    swap(1)
+    swap(3)
     front(x_own, h_own, 0, 0, 3)
-    swap_three(2)
+    swap(2)
     for b in (0, 1, 3):
-        c_swap[b, 0].wait_recv()
-        c_swap[b, 1].wait_recv()
+        c_swap[b].wait_recv()
     front(x_far, h_far, 1, 0, 3)
-    swap_last(2)
     front(x_own, h_own, 0, 3, 4)
-    c_swap[2, 0].wait_recv()
-    c_swap[2, 1].wait_recv()
+    c_swap[2].wait_recv()
     front(x_far, h_far, 1, 3, 4)
     swaps = []
     for i in range(4):
@@ -486,23 +431,15 @@
     d_near[...] = jnp.dot(a_own[...].reshape(256, 384), wd[0], preferred_element_type=F32).reshape(4, 64, 2048)
     for copy in swaps:
         copy.wait_recv()
-    c_via, c_on, c_back = {}, {}, {}
+    c_back = {}
     for b in (2, 1, 3, 0):
-        at = SLOT[b]
-        rows = d_near[at] + jnp.dot(a_far[at].reshape(64, 384), wd[1], preferred_element_type=F32)
+        rows = d_near[SLOT[b]] + jnp.dot(a_far[SLOT[b]].reshape(64, 384), wd[1], preferred_element_type=F32)
         rows = rows.astype(BF).reshape(4, S, 2048)
+        z_buf[b, 0] = rows[0]
+        c_back[b] = []
         for a in (2, 1, 3):
             y_st[b, a - 1] = rows[SLOT[a]]
-        z_buf[b, 0] = rows[0]
-        for r in range(2):
-            c_via[b, r] = links.push(y_st.at[b, 1, :, part(r)], z_via.at[r, b], side, a_way[r])
-        c_back[b] = [links.push(y_st.at[b, 0], z_buf.at[b, 1], side, am),
-                     links.push(y_st.at[b, 2], z_buf.at[b, 3], side, ap)]
-
-    def back_on(b):
-        for r in range(2):
-            c_via[b, r].wait_recv()
-            c_back[b].append(links.push(z_via.at[r, b], z_buf.at[b, 2, :, part(r)], side, a_way[r]))
+            c_back[b].append(links.push(y_st.at[b, a - 1], z_buf.at[b, a], side, a_way[(None, 1, 2, 0)[a]]))
 
     def mix(b):
         for copy in c_back[b]:
@@ -511,17 +448,13 @@
                                preferred_element_type=F32)
         m_buf[b] = (both[0:64, :] + both[64:128, :]).reshape(4, S, 2048)
 
-    ring = Scatter(links, side, x_way, b_way, m_buf, far, over, near)
-    back_on(2)
-    back_on(1)
-    back_on(3)
+    ring = Scatter(links, side, x_way, b_way, m_buf, over, near)
     mix(2)
-    ring.start_far()
-    back_on(0)
+    ring.along_q(2)
     mix(1)
+    ring.along_q(1)
     mix(3)
-    ring.start_over()
-    ring.forward()
+    ring.along_q(3)
     mix(0)
     ring.turn()
     out_ref[...] = hid[:, half_at] + ring.result()
@@ -550,10 +483,9 @@
             vb(S, 4096), vb(S, CTX, 256), vb(S, CTX, 256), vb(4, 64, 4096),
             vb(4, 4, S, HEADS0 * HD), vb(4, 4, S, 4096 - HEADS0 * HD),
             vb(16, S, 256), vb(2, 16, S, 256), vf(S, D), vf(4, 4, 16, 128), vb(4, 4, S, 2048),
-            vb(4, 3, S, 2048), vb(4, 4, S, 2048), vb(4, 4, S, 2048), vb(2, 4, S, 1024),
+            vb(4, 3, S, 2048), vb(4, 4, S, 2048), vb(4, 4, S, 2048),
             vb(2, 2048, 768), vb(2, 384, 2048), vf(4, 4, S, 768), vf(4, 4, S, 768), vb(4, 4, S, 384), vb(4, 4, S, 384),
-            vf(4, 64, 2048), vb(4, 3, S, 2048), vb(4, 4, S, 2048), vb(2, 4, S, 1024), vf(4, 4, S, 2048),
-            vb(2, 4, S, 2048), vb(2, 2, 4, S, 2048), vb(2, 4, S, 2048),
+            vf(4, 64, 2048), vb(4, 3, S, 2048), vb(4, 4, S, 2048), vf(4, 4, S, 2048), vb(2, 3, 4, S, 2048), vb(2, 4, S, 2048),
             vb(S, D), vf(1, D), pltpu.VMEM((8, S), jnp.int32), vf(8, S), pltpu.SMEM((S,), jnp.int32),
             dma((15,)), dma((160,)), dma((160,)), dma((16, 2)), dma((2, 16)),
         ],

time: 84.5 us -> 79.5 us (0.941); the launches traced: 84.4 us -> 78.4 us
  Pallas kernels: 83.7 us -> 77.7 us
    pallas_call x1, Pallas kernels: 83.7 us -> 77.7 us  [body(): pl.pallas_call(kernel, out_shape=jax.ShapeDtypeStruct((S, D // 2), F32),...]
where the time goes in v5:
time: 79.5 us; the launch traced here: 78.4 us
  Pallas kernels  77.7 us (98%)
    pallas_call x1, Pallas kernels, body(): pl.pallas_call(kernel, out_shape=jax.ShapeDtypeStruct((S, D // 2), F32),...  77.7 us

profile of v5, /device:TPU:0, one launch (start us, length us, event | category | flops | bytes accessed | tf_op | source)
XLA Modules:
  0.0 78.4 jit_solution(7954162990879570930)
XLA Ops:
  0.0 77.7 %decode_layer.1 = f32[16,2048]{1,0:T(8,128)S(1)} custom-call(bf16[16,8192]{1,0:T(8,128)(2,1)} %q_ref.1, bf16[16,128,512]{2,1,0:T(8,128)(2,1)} %k_ref.1, bf16[16,128,512]{2,1,0:T(8,128)(2,1)} %v_ref.1, s32[16]{0:T(128)} %lens_ref.1, bf16[64,8192]{1,0:T(8,128)(2,1)} %bitcast.8, bf16[16,4096]{1,0:T(8,128)(2,1)} %res_ref.1, f32[1,4096]{1,0:T(1,128)} %bitcast.9, ...), custom_call_target="tpu_custom_call" | custom-call | tf_op jit(solution)/shard_map/decode_layer/pallas_call | solution.py:477
  77.7 0.6 convert_element_type.3

commit v6 on v5

--- a/solution.py
+++ b/solution.py
@@ -119,15 +119,15 @@
         self.got.pop((i, j)).wait_recv()
 
     def along_q(self, j):
+        self.send(0, j, self.q[0], 1, 0)
+        self.send(0, j, self.q[1], 3, 0)
         if self.direct:
             self.send(0, j, self.q[2], 2, 0)
-        self.send(0, j, self.q[0], 1, 0)
-        self.send(0, j, self.q[1], 3, 0)
 
     def start(self):
-        self.send(0, 0, self.p[2], 0, 2)
         self.send(0, 0, self.p[0], 0, 1)
         self.send(0, 0, self.p[1], 0, 3)
+        self.send(0, 0, self.p[2], 0, 2)
         self.along_q(0)
 
     def step1(self):
@@ -157,28 +157,27 @@
 
 
 class Scatter:
-    def __init__(self, links, side, p, q, m, over, near):
-        self.links, self.side, self.p, self.q, self.m, self.over, self.near = links, side, p, q, m, over, near
+    def __init__(self, links, side, p, q, block, over, near):
+        self.links, self.side, self.p, self.q, self.block = links, side, p, q, block
+        self.over, self.near = over, near
         self.c_over, self.c_near = {}, {}
 
-    def along_q(self, i):
-        for j in (2, 1, 3, 0):
-            self.over[0, i - 1, j] = self.m[i, j].astype(BF)
-            self.c_over[i, j] = self.links.push(
-                self.over.at[0, i - 1, j], self.over.at[1, i - 1, j], self.side, self.q[(None, 1, 2, 0)[i]])
-
-    def turn(self):
-        for j in (2, 1, 3, 0):
-            block = self.m[0, j]
-            for i in (2, 1, 3):
-                self.c_over[i, j].wait_recv()
-                block = block + self.over[1, i - 1, j].astype(F32)
-            if j == 0:
-                self.own = block
-            else:
-                self.near[0, j] = block.astype(BF)
-                self.c_near[j] = self.links.push(
-                    self.near.at[0, j], self.near.at[1, j], self.side, self.p[(None, 1, 2, 0)[j]])
+    def along_q(self, i, j):
+        self.over[0, i - 1, j] = self.block(i, j).astype(BF)
+        self.c_over[i, j] = self.links.push(
+            self.over.at[0, i - 1, j], self.over.at[1, i - 1, j], self.side, self.q[(None, 1, 2, 0)[i]])
+
+    def turn(self, j):
+        block = self.block(0, j)
+        for i in (2, 1, 3):
+            self.c_over[i, j].wait_recv()
+            block = block + self.over[1, i - 1, j].astype(F32)
+        if j == 0:
+            self.own = block
+        else:
+            self.near[0, j] = block.astype(BF)
+            self.c_near[j] = self.links.push(
+                self.near.at[0, j], self.near.at[1, j], self.side, self.p[(None, 1, 2, 0)[j]])
 
     def result(self):
         block = self.own
@@ -231,11 +230,12 @@
 
 SLOT = (0, 1, 3, 2)
 HEADS0 = 20
+CUT = 1280
 
 
 def kernel(q_ref, k_ref, v_ref, lens_ref, wt_ref, res_ref, gain_ref, ids_ref, route_ref, up_ref, down_ref, out_ref,
-           q_buf, k_buf, v_buf, w_buf, g0, g1, o_st, r_buf, hid, info, n_buf, x_st, x_own, x_far,
-           w_gu, wd, h_own, h_far, a_own, a_far, d_near, y_st, z_buf, m_buf, over, near,
+           q_buf, k_buf, v_buf, w_buf, g0, g1, o_st, r_buf, hid, info, n0, n1, x_st, x_own, x_far,
+           w_gu, wd, h_own, h_far, a_own, a_far, d_near, y_st, z_buf, m_buf, over0, near0, over1, near1,
            res_buf, gain_buf, ids_buf, route_buf, lens_buf, loc, sends, recvs, os, orv):
     side, g, sa, sb, ca, cb, cx = place()
     other = 1 - side
@@ -375,17 +375,21 @@
     scaling = lax.rsqrt(jnp.sum(squares, axis=1, keepdims=True) * (1.0 / D) + 1e-06)
 
     half_at = pl.ds(pl.multiple_of(side * 2048, 128), 2048)
-    na = Gather(links, side, x_way, b_way, n_buf, True)
-    n_buf[0, 0] = (hid[:, half_at] * scaling * gain_buf[:, half_at]).astype(BF)
+    na = Gather(links, side, b_way, x_way, n0, True)
+    nb = Gather(links, side, x_way, b_way, n1, True)
+    normed = (hid[:, half_at] * scaling * gain_buf[:, half_at]).astype(BF)
+    n0[0, 0] = normed[:, 0:CUT]
+    n1[0, 0] = normed[:, CUT:]
+    nb.start()
     na.start()
 
     c_one, c_swap = {}, {}
 
     def dispatch(b):
-        rows = jnp.dot(pick[b], n_buf[b].reshape(64, 2048), preferred_element_type=F32).astype(BF)
-        rows = rows.reshape(4, S, 2048)
-        x_st[b] = rows[1:]
-        x_own[SLOT[b], 0] = rows[0]
+        for at, tokens in ((slice(0, CUT), n0[:, b]), (slice(CUT, 2048), n1[b])):
+            rows = jnp.dot(pick[b], tokens.reshape(64, -1), preferred_element_type=F32).astype(BF).reshape(4, S, -1)
+            x_st[b, :, :, at] = rows[1:]
+            x_own[SLOT[b], 0, :, at] = rows[0]
         c_one[b] = [links.push(x_st.at[b, a - 1], x_own.at[SLOT[b], SLOT[a]], side, a_way[(None, 0, 2, 1)[a]])
                     for a in (2, 1, 3)]
 
@@ -398,30 +402,27 @@
         rows = src[low:high].reshape((high - low) * 64, 2048)
         dst[low:high] = jnp.dot(rows, w_gu[h], preferred_element_type=F32).reshape(high - low, 4, S, 768)
 
+    nb.step1()
     na.step1()
+    nb.step2()
     na.step2()
-    dispatch(0)
-    for j in range(4):
-        na.wait(1, j)
-    dispatch(1)
-    for j in range(4):
-        na.wait(3, j)
-    dispatch(3)
-    na.finish()
-    dispatch(2)
+    for b in (0, 1, 3, 2):
+        for j in range(4):
+            for ring, at in ((nb, (b, j)), (na, (j, b))):
+                if at in ring.got:
+                    ring.wait(*at)
+        dispatch(b)
     for copy in c_ffn:
         copy.wait()
     swap(0)
     swap(1)
+    front(x_own, h_own, 0, 0, 2)
     swap(3)
-    front(x_own, h_own, 0, 0, 3)
     swap(2)
-    for b in (0, 1, 3):
+    front(x_own, h_own, 0, 2, 4)
+    for b in (0, 1, 3, 2):
         c_swap[b].wait_recv()
-    front(x_far, h_far, 1, 0, 3)
-    front(x_own, h_own, 0, 3, 4)
-    c_swap[2].wait_recv()
-    front(x_far, h_far, 1, 3, 4)
+    front(x_far, h_far, 1, 0, 4)
     swaps = []
     for i in range(4):
         both = h_own[i] + h_far[:, i]
@@ -448,16 +449,21 @@
                                preferred_element_type=F32)
         m_buf[b] = (both[0:64, :] + both[64:128, :]).reshape(4, S, 2048)
 
-    ring = Scatter(links, side, x_way, b_way, m_buf, over, near)
-    mix(2)
-    ring.along_q(2)
-    mix(1)
-    ring.along_q(1)
-    mix(3)
-    ring.along_q(3)
-    mix(0)
-    ring.turn()
-    out_ref[...] = hid[:, half_at] + ring.result()
+    r0 = Scatter(links, side, b_way, x_way, lambda i, j: m_buf[j, i, :, 0:CUT], over0, near0)
+    r1 = Scatter(links, side, x_way, b_way, lambda i, j: m_buf[i, j, :, CUT:2048], over1, near1)
+    for b in (2, 1, 3, 0):
+        mix(b)
+        for i in (2, 1, 3):
+            r0.along_q(i, b)
+        if b:
+            for j in (2, 1, 3, 0):
+                r1.along_q(b, j)
+    for j in (2, 1, 3, 0):
+        r0.turn(j)
+        r1.turn(j)
+    at = pl.multiple_of(side * 2048, 128)
+    out_ref[:, 0:CUT] = hid[:, pl.ds(at, CUT)] + r0.result()
+    out_ref[:, CUT:2048] = hid[:, pl.ds(at + CUT, 2048 - CUT)] + r1.result()
     links.drain()
     for copy in sent:
         copy.wait_send()
@@ -482,12 +488,13 @@
         scratch_shapes=[
             vb(S, 4096), vb(S, CTX, 256), vb(S, CTX, 256), vb(4, 64, 4096),
             vb(4, 4, S, HEADS0 * HD), vb(4, 4, S, 4096 - HEADS0 * HD),
-            vb(16, S, 256), vb(2, 16, S, 256), vf(S, D), vf(4, 4, 16, 128), vb(4, 4, S, 2048),
+            vb(16, S, 256), vb(2, 16, S, 256), vf(S, D), vf(4, 4, 16, 128), vb(4, 4, S, CUT), vb(4, 4, S, 2048 - CUT),
             vb(4, 3, S, 2048), vb(4, 4, S, 2048), vb(4, 4, S, 2048),
             vb(2, 2048, 768), vb(2, 384, 2048), vf(4, 4, S, 768), vf(4, 4, S, 768), vb(4, 4, S, 384), vb(4, 4, S, 384),
-            vf(4, 64, 2048), vb(4, 3, S, 2048), vb(4, 4, S, 2048), vf(4, 4, S, 2048), vb(2, 3, 4, S, 2048), vb(2, 4, S, 2048),
+            vf(4, 64, 2048), vb(4, 3, S, 2048), vb(4, 4, S, 2048), vf(4, 4, S, 2048),
+            vb(2, 3, 4, S, CUT), vb(2, 4, S, CUT), vb(2, 3, 4, S, 2048 - CUT), vb(2, 4, S, 2048 - CUT),
             vb(S, D), vf(1, D), pltpu.VMEM((8, S), jnp.int32), vf(8, S), pltpu.SMEM((S,), jnp.int32),
-            dma((15,)), dma((160,)), dma((160,)), dma((16, 2)), dma((2, 16)),
+            dma((15,)), dma((180,)), dma((180,)), dma((16, 2)), dma((2, 16)),
         ],
         compiler_params=pltpu.CompilerParams(collective_id=0, has_side_effects=True, vmem_limit_bytes=46 << 20),
         name="decode_layer",

time: 79.5 us -> 75 us (0.943); the launches traced: 78.4 us -> 74.9 us
  Pallas kernels: 77.7 us -> 74.2 us
    pallas_call x1, Pallas kernels: 77.7 us -> 74.2 us  [body(): pl.pallas_call(kernel, out_shape=jax.ShapeDtypeStruct((S, D // 2), F32),...]
where the time goes in v6:
time: 75 us; the launch traced here: 74.9 us
  Pallas kernels  74.2 us (99%)
    pallas_call x1, Pallas kernels, body(): pl.pallas_call(kernel, out_shape=jax.ShapeDtypeStruct((S, D // 2), F32),...  74.2 us

profile of v6, /device:TPU:0, one launch (start us, length us, event | category | flops | bytes accessed | tf_op | source)
XLA Modules:
  0.0 74.9 jit_solution(17089260664964534494)
XLA Ops:
  0.0 74.2 %decode_layer.1 = f32[16,2048]{1,0:T(8,128)S(1)} custom-call(bf16[16,8192]{1,0:T(8,128)(2,1)} %q_ref.1, bf16[16,128,512]{2,1,0:T(8,128)(2,1)} %k_ref.1, bf16[16,128,512]{2,1,0:T(8,128)(2,1)} %v_ref.1, s32[16]{0:T(128)} %lens_ref.1, bf16[64,8192]{1,0:T(8,128)(2,1)} %bitcast.8, bf16[16,4096]{1,0:T(8,128)(2,1)} %res_ref.1, f32[1,4096]{1,0:T(1,128)} %bitcast.9, ...), custom_call_target="tpu_custom_call" | custom-call | tf_op jit(solution)/shard_map/decode_layer/pallas_call | solution.py:483
  74.2 0.6 convert_element_type.3

commit v7 on v6

--- a/solution.py
+++ b/solution.py
@@ -59,64 +59,92 @@
 
 
 class Links:
-    def __init__(self, sends, recvs):
-        self.sends, self.recvs, self.used, self.open = sends, recvs, 0, []
-
-    def make(self, src, dst, to_side, to):
-        i = self.used
-        self.used += 1
-        copy = pltpu.make_async_remote_copy(
-            src_ref=src, dst_ref=dst, send_sem=self.sends.at[i], recv_sem=self.recvs.at[i],
+    def __init__(self, side, near, sends, recvs):
+        self.side, self.near, self.sends, self.recvs = side, near, sends, recvs
+        self.slots, self.count, self.live = 0, 0, [None] * POOL
+
+    def slot(self):
+        assert self.slots < self.recvs.shape[0]
+        self.slots += 1
+        return self.slots - 1
+
+    def make(self, src, dst, send, recv, to_side, to):
+        return pltpu.make_async_remote_copy(
+            src_ref=src, dst_ref=dst, send_sem=self.sends.at[send], recv_sem=self.recvs.at[recv],
             device_id=(to_side, to), device_id_type=MESH)
-        self.open.append(copy)
-        return copy
-
-    def push(self, src, dst, to_side, to):
-        copy = self.make(src, dst, to_side, to)
+
+    def push(self, src, dst, to_side, to, recv=None, send=None):
+        if recv is None:
+            recv = self.slot()
+        pooled = send is None
+        if pooled:
+            send = self.count % POOL
+            self.count += 1
+            if self.live[send] is not None:
+                self.live[send].wait_send()
+        copy = self.make(src, dst, send, recv, to_side, to)
+        if pooled:
+            self.live[send] = copy
         copy.start()
         return copy
 
+    def wait(self, view, recv):
+        self.make(view, view, 0, recv, self.side, self.near).wait_recv()
+
+    def sent(self, view, send):
+        self.make(view, view, send, 0, self.side, self.near).wait_send()
+
     def drain(self):
-        for copy in self.open:
-            copy.wait_send()
+        for copy in self.live:
+            if copy is not None:
+                copy.wait_send()
 
 
 class Columns:
-    def __init__(self, links, side, plus, minus, own, slot):
+    def __init__(self, links, side, plus, minus, own, slot, whole):
         self.links, self.side, self.plus, self.minus, self.own, self.slot = links, side, plus, minus, own, slot
+        self.whole, self.rest = whole, links.slot()
 
     def start(self):
         low, high = slice(0, 32), slice(32, 64)
         push, own, slot = self.links.push, self.own, self.slot(0)
         self.c0 = push(own.at[low], slot.at[low], self.side, self.plus)
         self.c1 = push(own.at[high], slot.at[high], self.side, self.minus)
-        self.rest = [push(own.at[high], slot.at[high], self.side, self.plus),
-                     push(own.at[low], slot.at[low], self.side, self.minus)]
+        push(own.at[high], slot.at[high], self.side, self.plus, self.rest)
+        push(own.at[low], slot.at[low], self.side, self.minus, self.rest)
 
     def forward(self):
         self.c0.wait_recv()
         at = self.slot(1).at[0:32]
-        self.rest.append(self.links.push(at, at, self.side, self.plus))
+        self.links.push(at, at, self.side, self.plus, self.rest)
         self.c1.wait_recv()
         at = self.slot(3).at[32:64]
-        self.rest.append(self.links.push(at, at, self.side, self.minus))
+        self.links.push(at, at, self.side, self.minus, self.rest)
 
     def finish(self):
-        for copy in self.rest:
-            copy.wait_recv()
+        self.links.wait(self.whole.at[0:2], self.rest)
 
 
 class Gather:
-    def __init__(self, links, side, p, q, buf, direct):
-        self.links, self.side, self.p, self.q, self.buf, self.direct = links, side, p, q, buf, direct
-        self.got = {}
+    def __init__(self, links, side, p, q, buf, direct, group):
+        self.links, self.side, self.p, self.q, self.buf, self.direct, self.group = links, side, p, q, buf, direct, group
+        self.got, self.sems = {}, {}
 
     def send(self, i, j, to, di, dj):
         at = (i + di) % 4, (j + dj) % 4
-        self.got[at] = self.links.push(self.buf.at[i, j], self.buf.at[at], self.side, to)
+        key = self.group(*at)
+        recv = None
+        if key is not None:
+            if key not in self.sems:
+                self.sems[key] = self.links.slot()
+            recv = self.sems[key]
+        self.got[at] = self.links.push(self.buf.at[i, j], self.buf.at[at], self.side, to, recv)
 
     def wait(self, i, j):
-        self.got.pop((i, j)).wait_recv()
+        self.got[i, j].wait_recv()
+
+    def wait_group(self, key, view):
+        self.links.wait(view, self.sems[key])
 
     def along_q(self, j):
         self.send(0, j, self.q[0], 1, 0)
@@ -151,38 +179,37 @@
         self.wait(3, 2)
         self.send(3, 2, self.q[1], 3, 0)
 
-    def finish(self):
-        for key in list(self.got):
-            self.wait(*key)
+
+def relayed(i, j):
+    return None if i == 0 or (i, j) in ((1, 0), (1, 1), (3, 3), (3, 2)) else 0
 
 
 class Scatter:
     def __init__(self, links, side, p, q, block, over, near):
         self.links, self.side, self.p, self.q, self.block = links, side, p, q, block
         self.over, self.near = over, near
-        self.c_over, self.c_near = {}, {}
+        self.s_over, self.s_near = [links.slot() for _ in range(4)], links.slot()
 
     def along_q(self, i, j):
         self.over[0, i - 1, j] = self.block(i, j).astype(BF)
-        self.c_over[i, j] = self.links.push(
-            self.over.at[0, i - 1, j], self.over.at[1, i - 1, j], self.side, self.q[(None, 1, 2, 0)[i]])
+        self.links.push(self.over.at[0, i - 1, j], self.over.at[1, i - 1, j], self.side, self.q[(None, 1, 2, 0)[i]],
+                        self.s_over[j])
 
     def turn(self, j):
+        self.links.wait(self.over.at[1, :, j], self.s_over[j])
         block = self.block(0, j)
         for i in (2, 1, 3):
-            self.c_over[i, j].wait_recv()
             block = block + self.over[1, i - 1, j].astype(F32)
         if j == 0:
             self.own = block
         else:
             self.near[0, j] = block.astype(BF)
-            self.c_near[j] = self.links.push(
-                self.near.at[0, j], self.near.at[1, j], self.side, self.p[(None, 1, 2, 0)[j]])
+            self.links.push(self.near.at[0, j], self.near.at[1, j], self.side, self.p[(None, 1, 2, 0)[j]], self.s_near)
 
     def result(self):
+        self.links.wait(self.near.at[1, 1:4], self.s_near)
         block = self.own
         for j in (1, 3, 2):
-            self.c_near[j].wait_recv()
             block = block + self.near[1, j].astype(F32)
         return block
 
@@ -194,7 +221,7 @@
         tile = jnp.zeros((16, 128), F32)
         for i in range(8):
             b, x = divmod(t * 8 + i, 4)
-            block = info[x, b]
+            block = info[x * 4 + b]
             moved_block = pltpu.roll(block, 16 * i, 1) if i else block
             tile = jnp.where(lane // 16 == i, moved_block, tile)
         tiles.append(tile)
@@ -230,20 +257,21 @@
 
 SLOT = (0, 1, 3, 2)
 HEADS0 = 20
+POOL = 40
 CUT = 1280
 
 
 def kernel(q_ref, k_ref, v_ref, lens_ref, wt_ref, res_ref, gain_ref, ids_ref, route_ref, up_ref, down_ref, out_ref,
            q_buf, k_buf, v_buf, w_buf, g0, g1, o_st, r_buf, hid, info, n0, n1, x_st, x_own, x_far,
            w_gu, wd, h_own, h_far, a_own, a_far, d_near, y_st, z_buf, m_buf, over0, near0, over1, near1,
-           res_buf, gain_buf, ids_buf, route_buf, lens_buf, loc, sends, recvs, os, orv):
+           res_buf, gain_buf, ids_buf, route_buf, lens_buf, loc, sends, recvs):
     side, g, sa, sb, ca, cb, cx = place()
     other = 1 - side
     a_way = [moved(g, ca, sa, i) for i in (1, -1, 2)]
     ap, am = a_way[0], a_way[1]
     b_way = [moved(g, cb, sb, i) for i in (1, -1, 2)]
     x_way = [moved(g, cx, 1, i) for i in (1, -1, 2)]
-    links = Links(sends, recvs)
+    links = Links(side, ap, sends, recvs)
     barrier = pltpu.get_barrier_semaphore()
 
     def hello(to_side, to):
@@ -273,7 +301,7 @@
     c_w = fetch(w_own, w_buf.at[ca], 3)
     c_ids = fetch(ids_ref, ids_buf, 10)
     c_route = fetch(route_ref, route_buf, 11)
-    info[0, 0] = jnp.zeros((16, 128), F32)
+    info[0] = jnp.zeros((16, 128), F32)
     c_lens.wait()
     c_q.wait()
     c_k.wait()
@@ -287,21 +315,21 @@
             out[0, 0, :, n * HD:(n + 1) * HD] = result[j * S:(j + 1) * S, :]
     c_ids.wait()
     c_route.wait()
-    info[0, 0, 0:8, 0:16] = ids_buf[...].astype(F32)
-    info[0, 0, 8:16, 0:16] = route_buf[...]
+    info[0, 0:8, 0:16] = ids_buf[...].astype(F32)
+    info[0, 8:16, 0:16] = route_buf[...]
     pl.semaphore_wait(barrier, 34)
-    ring_w = Columns(links, side, ap, am, w_own, lambda source: w_buf.at[lax.rem(ca - source + 4, 4)])
+    ring_w = Columns(links, side, ap, am, w_own, lambda source: w_buf.at[lax.rem(ca - source + 4, 4)], w_buf)
     split = HEADS0 * HD
-    ra = Gather(links, side, b_way, x_way, g0, False)
-    rb = Gather(links, side, x_way, b_way, g1, False)
+    ra = Gather(links, side, b_way, x_way, g0, False, relayed)
+    rb = Gather(links, side, x_way, b_way, g1, False, relayed)
     ring_w.start()
     ra.start()
     rb.start()
-    told = []
+    told = links.slot()
     for i in range(4):
         for j in range(4):
             if i or j:
-                told.append(links.push(info.at[0, 0], info.at[j, i], side, moved(moved(g, cb, sb, i), cx, 1, j)))
+                links.push(info.at[0], info.at[j * 4 + i], side, moved(moved(g, cb, sb, i), cx, 1, j), told, POOL)
     c_res = fetch(res_ref, res_buf, 12)
     c_gain = fetch(gain_ref, gain_buf, 13)
     c_ffn = []
@@ -317,47 +345,33 @@
     ring_w.forward()
     ra.step3()
     rb.step3()
-    ra.finish()
-    rb.finish()
+    ra.wait_group(0, g0.at[2:4])
+    rb.wait_group(0, g1.at[2:4])
     c_w.wait()
     ring_w.finish()
     p0 = lax.dot_general(g0[...].reshape(256, split), w_buf[:, :, 0:split].reshape(256, split), NT,
                          preferred_element_type=F32)
     p1 = lax.dot_general(g1[...].reshape(256, 4096 - split), w_buf[:, :, split:4096].reshape(256, 4096 - split), NT,
                          preferred_element_type=F32)
-    mine = cb * 4 + cx
-    sent = []
+    mine = side * 16 + cb * 4 + cx
+    columns_in = links.slot()
     for n in sorted(range(16), key=lambda n: -((0, 1, 2, 1)[n // 4] + (0, 1, 2, 1)[n % 4])):
         bi, xi = n // 4, n % 4
         u = (xi * 4 + bi) * S
         block = (p0[u:u + S, :] + p1[n * S:(n + 1) * S, :]).astype(BF)
         o_st[n] = block
         if n == 0:
-            r_buf[side, mine] = block
+            r_buf[mine] = block
         to = moved(moved(g, cb, sb, -bi), cx, 1, -xi)
         for e in range(2):
             if n == 0 and e == 0:
                 continue
-            copy = pltpu.make_async_remote_copy(
-                src_ref=o_st.at[n], dst_ref=r_buf.at[side, mine], send_sem=os.at[n, e], recv_sem=orv.at[side, mine],
-                device_id=(side if e == 0 else other, to), device_id_type=MESH)
-            copy.start()
-            sent.append(copy)
-
-    def arrived(source_side, n):
-        pltpu.make_async_remote_copy(
-            src_ref=o_st.at[0], dst_ref=r_buf.at[source_side, n], send_sem=os.at[0, 0], recv_sem=orv.at[source_side, n],
-            device_id=(side, ap), device_id_type=MESH).wait_recv()
-
-    for copy in told:
-        copy.wait_recv()
+            links.push(o_st.at[n], r_buf.at[mine], side if e == 0 else other, to, columns_in, POOL + 1)
+
+    links.wait(info.at[1:16], told)
     experts = [moved(g, ca, sa, i) for i in range(4)]
     pick, weigh = routing(info, experts)
-    for i in range(4):
-        for j in range(4):
-            if i or j:
-                arrived(side, lax.rem(cb + i, 4) * 4 + lax.rem(cx + j, 4))
-            arrived(other, lax.rem(ca + i, 4) * 4 + lax.rem(cx + j, 4))
+    links.wait(r_buf.at[0:31], columns_in)
     c_res.wait()
     c_gain.wait()
     squares = jnp.zeros((S, 128), F32)
@@ -366,8 +380,8 @@
             for m in range(2):
                 pieces = []
                 for x in (2 * m, 2 * m + 1):
-                    pieces.append(r_buf[0, z * 4 + x, :, y * 64:(y + 1) * 64].astype(F32)
-                                  + r_buf[1, y * 4 + x, :, z * 64:(z + 1) * 64].astype(F32))
+                    pieces.append(r_buf[z * 4 + x, :, y * 64:(y + 1) * 64].astype(F32)
+                                  + r_buf[16 + y * 4 + x, :, z * 64:(z + 1) * 64].astype(F32))
                 at = (y * 8 + z * 2 + m) * 128
                 tile = res_buf[:, at:at + 128].astype(F32) + jnp.concatenate(pieces, axis=1)
                 hid[:, at:at + 128] = tile
@@ -375,28 +389,27 @@
     scaling = lax.rsqrt(jnp.sum(squares, axis=1, keepdims=True) * (1.0 / D) + 1e-06)
 
     half_at = pl.ds(pl.multiple_of(side * 2048, 128), 2048)
-    na = Gather(links, side, b_way, x_way, n0, True)
-    nb = Gather(links, side, x_way, b_way, n1, True)
+    na = Gather(links, side, b_way, x_way, n0, True, lambda i, j: j if i else None)
+    nb = Gather(links, side, x_way, b_way, n1, True, lambda i, j: i if i else None)
     normed = (hid[:, half_at] * scaling * gain_buf[:, half_at]).astype(BF)
     n0[0, 0] = normed[:, 0:CUT]
     n1[0, 0] = normed[:, CUT:]
     nb.start()
     na.start()
 
-    c_one, c_swap = {}, {}
+    s_one, s_swap = [links.slot() for _ in range(4)], links.slot()
 
     def dispatch(b):
         for at, tokens in ((slice(0, CUT), n0[:, b]), (slice(CUT, 2048), n1[b])):
             rows = jnp.dot(pick[b], tokens.reshape(64, -1), preferred_element_type=F32).astype(BF).reshape(4, S, -1)
             x_st[b, :, :, at] = rows[1:]
             x_own[SLOT[b], 0, :, at] = rows[0]
-        c_one[b] = [links.push(x_st.at[b, a - 1], x_own.at[SLOT[b], SLOT[a]], side, a_way[(None, 0, 2, 1)[a]])
-                    for a in (2, 1, 3)]
+        for a in (2, 1, 3):
+            links.push(x_st.at[b, a - 1], x_own.at[SLOT[b], SLOT[a]], side, a_way[(None, 0, 2, 1)[a]], s_one[b])
 
     def swap(b):
-        for copy in c_one[b]:
-            copy.wait_recv()
-        c_swap[b] = links.push(x_own.at[SLOT[b]], x_far.at[SLOT[b]], other, g)
+        links.wait(x_own.at[SLOT[b], 1:4], s_one[b])
+        links.push(x_own.at[SLOT[b]], x_far.at[SLOT[b]], other, g, s_swap)
 
     def front(src, dst, h, low, high):
         rows = src[low:high].reshape((high - low) * 64, 2048)
@@ -407,10 +420,9 @@
     nb.step2()
     na.step2()
     for b in (0, 1, 3, 2):
-        for j in range(4):
-            for ring, at in ((nb, (b, j)), (na, (j, b))):
-                if at in ring.got:
-                    ring.wait(*at)
+        if b:
+            nb.wait_group(b, n1.at[b])
+        na.wait_group(b, n0.at[1:4, b])
         dispatch(b)
     for copy in c_ffn:
         copy.wait()
@@ -420,31 +432,27 @@
     swap(3)
     swap(2)
     front(x_own, h_own, 0, 2, 4)
-    for b in (0, 1, 3, 2):
-        c_swap[b].wait_recv()
+    links.wait(x_far, s_swap)
     front(x_far, h_far, 1, 0, 4)
-    swaps = []
+    s_act = links.slot()
     for i in range(4):
         both = h_own[i] + h_far[:, i]
         gate, up = both[:, :, 0:384], both[:, :, 384:768]
         a_own[i] = (gate / (1.0 + jnp.exp(-gate)) * up).astype(BF)
-        swaps.append(links.push(a_own.at[i], a_far.at[:, i], other, g))
+        links.push(a_own.at[i], a_far.at[:, i], other, g, s_act)
     d_near[...] = jnp.dot(a_own[...].reshape(256, 384), wd[0], preferred_element_type=F32).reshape(4, 64, 2048)
-    for copy in swaps:
-        copy.wait_recv()
-    c_back = {}
+    links.wait(a_far, s_act)
+    s_back = [links.slot() for _ in range(4)]
     for b in (2, 1, 3, 0):
         rows = d_near[SLOT[b]] + jnp.dot(a_far[SLOT[b]].reshape(64, 384), wd[1], preferred_element_type=F32)
         rows = rows.astype(BF).reshape(4, S, 2048)
         z_buf[b, 0] = rows[0]
-        c_back[b] = []
         for a in (2, 1, 3):
             y_st[b, a - 1] = rows[SLOT[a]]
-            c_back[b].append(links.push(y_st.at[b, a - 1], z_buf.at[b, a], side, a_way[(None, 1, 2, 0)[a]]))
+            links.push(y_st.at[b, a - 1], z_buf.at[b, a], side, a_way[(None, 1, 2, 0)[a]], s_back[b])
 
     def mix(b):
-        for copy in c_back[b]:
-            copy.wait_recv()
+        links.wait(z_buf.at[b, 1:4], s_back[b])
         both = lax.dot_general(weigh[b], z_buf[b].reshape(64, 2048), (((0,), (0,)), ((), ())),
                                preferred_element_type=F32)
         m_buf[b] = (both[0:64, :] + both[64:128, :]).reshape(4, S, 2048)
@@ -464,9 +472,9 @@
     at = pl.multiple_of(side * 2048, 128)
     out_ref[:, 0:CUT] = hid[:, pl.ds(at, CUT)] + r0.result()
     out_ref[:, CUT:2048] = hid[:, pl.ds(at + CUT, 2048 - CUT)] + r1.result()
+    links.sent(info.at[1:16], POOL)
+    links.sent(r_buf.at[0:31], POOL + 1)
     links.drain()
-    for copy in sent:
-        copy.wait_send()
 
 
 def body(q, k, v, lens, out_weight, residual, norm_gain, expert_ids, route_weights, gate_up, down_weight):
@@ -488,13 +496,13 @@
         scratch_shapes=[
             vb(S, 4096), vb(S, CTX, 256), vb(S, CTX, 256), vb(4, 64, 4096),
             vb(4, 4, S, HEADS0 * HD), vb(4, 4, S, 4096 - HEADS0 * HD),
-            vb(16, S, 256), vb(2, 16, S, 256), vf(S, D), vf(4, 4, 16, 128), vb(4, 4, S, CUT), vb(4, 4, S, 2048 - CUT),
+            vb(16, S, 256), vb(32, S, 256), vf(S, D), vf(16, 16, 128), vb(4, 4, S, CUT), vb(4, 4, S, 2048 - CUT),
             vb(4, 3, S, 2048), vb(4, 4, S, 2048), vb(4, 4, S, 2048),
             vb(2, 2048, 768), vb(2, 384, 2048), vf(4, 4, S, 768), vf(4, 4, S, 768), vb(4, 4, S, 384), vb(4, 4, S, 384),
             vf(4, 64, 2048), vb(4, 3, S, 2048), vb(4, 4, S, 2048), vf(4, 4, S, 2048),
             vb(2, 3, 4, S, CUT), vb(2, 4, S, CUT), vb(2, 3, 4, S, 2048 - CUT), vb(2, 4, S, 2048 - CUT),
             vb(S, D), vf(1, D), pltpu.VMEM((8, S), jnp.int32), vf(8, S), pltpu.SMEM((S,), jnp.int32),
-            dma((15,)), dma((180,)), dma((180,)), dma((16, 2)), dma((2, 16)),
+            dma((15,)), dma((POOL + 2,)), dma((54,)),
         ],
         compiler_params=pltpu.CompilerParams(collective_id=0, has_side_effects=True, vmem_limit_bytes=46 << 20),
         name="decode_layer",

time: 75 us -> 71.9 us (0.959)
  Pallas kernels: 74.2 us -> 71.2 us
    pallas_call x1, Pallas kernels: 74.2 us -> 71.2 us  [body(): pl.pallas_call(kernel, out_shape=jax.ShapeDtypeStruct((S, D // 2), F32),...]
where the time goes in v7:
time: 71.9 us; the launch traced here: 71.8 us
  Pallas kernels  71.2 us (99%)
    pallas_call x1, Pallas kernels, body(): pl.pallas_call(kernel, out_shape=jax.ShapeDtypeStruct((S, D // 2), F32),...  71.2 us

profile of v7, /device:TPU:0, one launch (start us, length us, event | category | flops | bytes accessed | tf_op | source)
XLA Modules:
  0.0 71.8 jit_solution(5469075724035428490)
XLA Ops:
  0.0 71.2 %decode_layer.1 = f32[16,2048]{1,0:T(8,128)S(1)} custom-call(bf16[16,8192]{1,0:T(8,128)(2,1)} %q_ref.1, bf16[16,128,512]{2,1,0:T(8,128)(2,1)} %k_ref.1, bf16[16,128,512]{2,1,0:T(8,128)(2,1)} %v_ref.1, s32[16]{0:T(128)} %lens_ref.1, bf16[64,8192]{1,0:T(8,128)(2,1)} %bitcast.8, bf16[16,4096]{1,0:T(8,128)(2,1)} %res_ref.1, f32[1,4096]{1,0:T(1,128)} %bitcast.9, ...), custom_call_target="tpu_custom_call" | custom-call | tf_op jit(solution)/shard_map/decode_layer/pallas_call | solution.py:491
  71.2 0.6 convert_element_type.3

commit v8 on v7

--- a/solution.py
+++ b/solution.py
@@ -34,7 +34,7 @@
     return g + (lax.rem(c + by + 4, 4) - c) * stride
 
 
-def attend(q_buf, k_buf, v_buf, lens_ref, kv):
+def attend(q_buf, k_buf, lens_ref, kv):
     lane = lax.broadcasted_iota(jnp.int32, (S, CTX), 1)
     row = lax.broadcasted_iota(jnp.int32, (S, CTX), 0)
     live = jnp.zeros((S, CTX), jnp.int32)
@@ -48,14 +48,12 @@
         [q_buf[:, (kv * group + j) * HD:(kv * group + j + 1) * HD] for j in range(group)], axis=0)
     scores = jnp.zeros((S * group, CTX), F32)
     for s in range(S):
-        part = lax.dot_general(queries, k_buf[s, :, kv * HD:(kv + 1) * HD], NT, preferred_element_type=F32)
+        part = lax.dot_general(queries, k_buf[s], NT, preferred_element_type=F32)
         scores = jnp.where(row == s, part, scores)
     scores = jnp.where(lane < live, scores * HD ** (-0.5), -1e30)
     lifted = jnp.exp(scores - jnp.max(scores, axis=1, keepdims=True))
     weights = (lifted / jnp.sum(lifted, axis=1, keepdims=True))
-    spread = jnp.concatenate([jnp.where(row == s, weights, 0.0).astype(BF) for s in range(S)], axis=1)
-    values = v_buf[:, :, kv * HD:(kv + 1) * HD].reshape(S * CTX, HD)
-    return jnp.dot(spread, values, preferred_element_type=F32).astype(BF)
+    return jnp.concatenate([jnp.where(row == s, weights, 0.0).astype(BF) for s in range(S)], axis=1)
 
 
 class Links:
@@ -106,19 +104,22 @@
         self.whole, self.rest = whole, links.slot()
 
     def start(self):
+        push, own, slot = self.links.push, self.own, self.slot(0)
+        self.up, self.down = [], []
+        for k in range(2):
+            up, down = slice(16 * k, 16 * k + 16), slice(32 + 16 * k, 48 + 16 * k)
+            self.up.append(push(own.at[up], slot.at[up], self.side, self.plus))
+            self.down.append(push(own.at[down], slot.at[down], self.side, self.minus))
         low, high = slice(0, 32), slice(32, 64)
-        push, own, slot = self.links.push, self.own, self.slot(0)
-        self.c0 = push(own.at[low], slot.at[low], self.side, self.plus)
-        self.c1 = push(own.at[high], slot.at[high], self.side, self.minus)
         push(own.at[high], slot.at[high], self.side, self.plus, self.rest)
         push(own.at[low], slot.at[low], self.side, self.minus, self.rest)
 
-    def forward(self):
-        self.c0.wait_recv()
-        at = self.slot(1).at[0:32]
+    def forward(self, k):
+        self.up[k].wait_recv()
+        at = self.slot(1).at[16 * k:16 * k + 16]
         self.links.push(at, at, self.side, self.plus, self.rest)
-        self.c1.wait_recv()
-        at = self.slot(3).at[32:64]
+        self.down[k].wait_recv()
+        at = self.slot(3).at[32 + 16 * k:48 + 16 * k]
         self.links.push(at, at, self.side, self.minus, self.rest)
 
     def finish(self):
@@ -256,9 +257,10 @@
 
 
 SLOT = (0, 1, 3, 2)
-HEADS0 = 20
+HEADS0 = 22
 POOL = 40
 CUT = 1280
+CUTR = 1280
 
 
 def kernel(q_ref, k_ref, v_ref, lens_ref, wt_ref, res_ref, gain_ref, ids_ref, route_ref, up_ref, down_ref, out_ref,
@@ -295,8 +297,8 @@
 
     c_lens = fetch(lens_ref, lens_buf, 14)
     c_q = fetch(q_ref.at[:, at_side(side, 4096)], q_buf, 0)
-    c_k = fetch(k_ref.at[:, :, at_side(side, 256)], k_buf, 1)
-    c_v = fetch(v_ref.at[:, :, at_side(side, 256)], v_buf, 2)
+    c_k = [fetch(k_ref.at[:, :, at_side(2 * side + i, 128)], k_buf.at[i], (1, 15)[i]) for i in range(2)]
+    c_v = [fetch(v_ref.at[:, :, at_side(2 * side + i, 128)], v_buf.at[i], (2, 16)[i]) for i in range(2)]
     w_own = wt_ref.at[:, at_side(side, 4096)]
     c_w = fetch(w_own, w_buf.at[ca], 3)
     c_ids = fetch(ids_ref, ids_buf, 10)
@@ -304,11 +306,14 @@
     info[0] = jnp.zeros((16, 128), F32)
     c_lens.wait()
     c_q.wait()
-    c_k.wait()
-    c_v.wait()
+    spread = []
+    for kv in range(2):
+        c_k[kv].wait()
+        spread.append(attend(q_buf, k_buf.at[kv], lens_buf, kv))
     group = HQ // KVH
     for kv in range(2):
-        result = attend(q_buf, k_buf, v_buf, lens_buf, kv)
+        c_v[kv].wait()
+        result = jnp.dot(spread[kv], v_buf[kv].reshape(S * CTX, HD), preferred_element_type=F32).astype(BF)
         for j in range(group):
             n = kv * group + j
             out, n = (g0, n) if n < HEADS0 else (g1, n - HEADS0)
@@ -342,7 +347,8 @@
     rb.step1()
     ra.step2()
     rb.step2()
-    ring_w.forward()
+    ring_w.forward(0)
+    ring_w.forward(1)
     ra.step3()
     rb.step3()
     ra.wait_group(0, g0.at[2:4])
@@ -397,7 +403,7 @@
     nb.start()
     na.start()
 
-    s_one, s_swap = [links.slot() for _ in range(4)], links.slot()
+    s_one, s_swap = [links.slot() for _ in range(4)], [links.slot(), links.slot()]
 
     def dispatch(b):
         for at, tokens in ((slice(0, CUT), n0[:, b]), (slice(CUT, 2048), n1[b])):
@@ -409,7 +415,7 @@
 
     def swap(b):
         links.wait(x_own.at[SLOT[b], 1:4], s_one[b])
-        links.push(x_own.at[SLOT[b]], x_far.at[SLOT[b]], other, g, s_swap)
+        links.push(x_own.at[SLOT[b]], x_far.at[SLOT[b]], other, g, s_swap[SLOT[b] // 2])
 
     def front(src, dst, h, low, high):
         rows = src[low:high].reshape((high - low) * 64, 2048)
@@ -429,11 +435,13 @@
     swap(0)
     swap(1)
     front(x_own, h_own, 0, 0, 2)
+    links.wait(x_far.at[0:2], s_swap[0])
+    front(x_far, h_far, 1, 0, 2)
     swap(3)
     swap(2)
     front(x_own, h_own, 0, 2, 4)
-    links.wait(x_far, s_swap)
-    front(x_far, h_far, 1, 0, 4)
+    links.wait(x_far.at[2:4], s_swap[1])
+    front(x_far, h_far, 1, 2, 4)
     s_act = links.slot()
     for i in range(4):
         both = h_own[i] + h_far[:, i]
@@ -457,8 +465,8 @@
                                preferred_element_type=F32)
         m_buf[b] = (both[0:64, :] + both[64:128, :]).reshape(4, S, 2048)
 
-    r0 = Scatter(links, side, b_way, x_way, lambda i, j: m_buf[j, i, :, 0:CUT], over0, near0)
-    r1 = Scatter(links, side, x_way, b_way, lambda i, j: m_buf[i, j, :, CUT:2048], over1, near1)
+    r0 = Scatter(links, side, b_way, x_way, lambda i, j: m_buf[j, i, :, 0:CUTR], over0, near0)
+    r1 = Scatter(links, side, x_way, b_way, lambda i, j: m_buf[i, j, :, CUTR:2048], over1, near1)
     for b in (2, 1, 3, 0):
         mix(b)
         for i in (2, 1, 3):
@@ -470,8 +478,8 @@
         r0.turn(j)
         r1.turn(j)
     at = pl.multiple_of(side * 2048, 128)
-    out_ref[:, 0:CUT] = hid[:, pl.ds(at, CUT)] + r0.result()
-    out_ref[:, CUT:2048] = hid[:, pl.ds(at + CUT, 2048 - CUT)] + r1.result()
+    out_ref[:, 0:CUTR] = hid[:, pl.ds(at, CUTR)] + r0.result()
+    out_ref[:, CUTR:2048] = hid[:, pl.ds(at + CUTR, 2048 - CUTR)] + r1.result()
     links.sent(info.at[1:16], POOL)
     links.sent(r_buf.at[0:31], POOL + 1)
     links.drain()
@@ -494,15 +502,15 @@
         in_specs=[hb] * 11,
         out_specs=vm,
         scratch_shapes=[
-            vb(S, 4096), vb(S, CTX, 256), vb(S, CTX, 256), vb(4, 64, 4096),
+            vb(S, 4096), vb(2, S, CTX, HD), vb(2, S, CTX, HD), vb(4, 64, 4096),
             vb(4, 4, S, HEADS0 * HD), vb(4, 4, S, 4096 - HEADS0 * HD),
             vb(16, S, 256), vb(32, S, 256), vf(S, D), vf(16, 16, 128), vb(4, 4, S, CUT), vb(4, 4, S, 2048 - CUT),
             vb(4, 3, S, 2048), vb(4, 4, S, 2048), vb(4, 4, S, 2048),
             vb(2, 2048, 768), vb(2, 384, 2048), vf(4, 4, S, 768), vf(4, 4, S, 768), vb(4, 4, S, 384), vb(4, 4, S, 384),
             vf(4, 64, 2048), vb(4, 3, S, 2048), vb(4, 4, S, 2048), vf(4, 4, S, 2048),
-            vb(2, 3, 4, S, CUT), vb(2, 4, S, CUT), vb(2, 3, 4, S, 2048 - CUT), vb(2, 4, S, 2048 - CUT),
+            vb(2, 3, 4, S, CUTR), vb(2, 4, S, CUTR), vb(2, 3, 4, S, 2048 - CUTR), vb(2, 4, S, 2048 - CUTR),
             vb(S, D), vf(1, D), pltpu.VMEM((8, S), jnp.int32), vf(8, S), pltpu.SMEM((S,), jnp.int32),
-            dma((15,)), dma((POOL + 2,)), dma((54,)),
+            dma((17,)), dma((POOL + 2,)), dma((57,)),
         ],
         compiler_params=pltpu.CompilerParams(collective_id=0, has_side_effects=True, vmem_limit_bytes=46 << 20),
         name="decode_layer",

time: 71.9 us -> 71.2 us (level)
  Pallas kernels: 71.2 us -> 70.4 us
    pallas_call x1, Pallas kernels: 71.2 us -> 70.4 us  [body(): pl.pallas_call(kernel, out_shape=jax.ShapeDtypeStruct((S, D // 2), F32),...]
where the time goes in v8:
time: 71.2 us; the launch traced here: 71.1 us
  Pallas kernels  70.4 us (99%)
    pallas_call x1, Pallas kernels, body(): pl.pallas_call(kernel, out_shape=jax.ShapeDtypeStruct((S, D // 2), F32),...  70.4 us

profile of v8, /device:TPU:0, one launch (start us, length us, event | category | flops | bytes accessed | tf_op | source)
XLA Modules:
  0.0 71.1 jit_solution(10501847863905152422)
XLA Ops:
  0.0 70.4 %decode_layer.1 = f32[16,2048]{1,0:T(8,128)S(1)} custom-call(bf16[16,8192]{1,0:T(8,128)(2,1)} %q_ref.1, bf16[16,128,512]{2,1,0:T(8,128)(2,1)} %k_ref.1, bf16[16,128,512]{2,1,0:T(8,128)(2,1)} %v_ref.1, s32[16]{0:T(128)} %lens_ref.1, bf16[64,8192]{1,0:T(8,128)(2,1)} %bitcast.8, bf16[16,4096]{1,0:T(8,128)(2,1)} %res_ref.1, f32[1,4096]{1,0:T(1,128)} %bitcast.9, ...), custom_call_target="tpu_custom_call" | custom-call | tf_op jit(solution)/shard_map/decode_layer/pallas_call | solution.py:499
  70.4 0.6 convert_element_type.3

commit v9 on v8

--- a/solution.py
+++ b/solution.py
@@ -330,11 +330,6 @@
     ring_w.start()
     ra.start()
     rb.start()
-    told = links.slot()
-    for i in range(4):
-        for j in range(4):
-            if i or j:
-                links.push(info.at[0], info.at[j * 4 + i], side, moved(moved(g, cb, sb, i), cx, 1, j), told, POOL)
     c_res = fetch(res_ref, res_buf, 12)
     c_gain = fetch(gain_ref, gain_buf, 13)
     c_ffn = []
@@ -374,9 +369,11 @@
                 continue
             links.push(o_st.at[n], r_buf.at[mine], side if e == 0 else other, to, columns_in, POOL + 1)
 
-    links.wait(info.at[1:16], told)
-    experts = [moved(g, ca, sa, i) for i in range(4)]
-    pick, weigh = routing(info, experts)
+    told = links.slot()
+    for i in range(4):
+        for j in range(4):
+            if i or j:
+                links.push(info.at[0], info.at[j * 4 + i], side, moved(moved(g, cb, sb, i), cx, 1, j), told, POOL)
     links.wait(r_buf.at[0:31], columns_in)
     c_res.wait()
     c_gain.wait()
@@ -423,6 +420,9 @@
 
     nb.step1()
     na.step1()
+    links.wait(info.at[1:16], told)
+    experts = [moved(g, ca, sa, i) for i in range(4)]
+    pick, weigh = routing(info, experts)
     nb.step2()
     na.step2()
     for b in (0, 1, 3, 2):

time: 71.2 us -> 70.9 us (level)
  no operation moved by 1% of the time
where the time goes in v9:
time: 70.9 us; the launch traced here: 70.7 us
  Pallas kernels  70.1 us (99%)
    pallas_call x1, Pallas kernels, body(): pl.pallas_call(kernel, out_shape=jax.ShapeDtypeStruct((S, D // 2), F32),...  70.1 us

profile of v9, /device:TPU:0, one launch (start us, length us, event | category | flops | bytes accessed | tf_op | source)
XLA Modules:
  0.0 70.7 jit_solution(4717593203870593498)
XLA Ops:
  0.0 70.1 %decode_layer.1 = f32[16,2048]{1,0:T(8,128)S(1)} custom-call(bf16[16,8192]{1,0:T(8,128)(2,1)} %q_ref.1, bf16[16,128,512]{2,1,0:T(8,128)(2,1)} %k_ref.1, bf16[16,128,512]{2,1,0:T(8,128)(2,1)} %v_ref.1, s32[16]{0:T(128)} %lens_ref.1, bf16[64,8192]{1,0:T(8,128)(2,1)} %bitcast.8, bf16[16,4096]{1,0:T(8,128)(2,1)} %res_ref.1, f32[1,4096]{1,0:T(1,128)} %bitcast.9, ...), custom_call_target="tpu_custom_call" | custom-call | tf_op jit(solution)/shard_map/decode_layer/pallas_call | solution.py:499
  70.1 0.6 convert_element_type.3
